TPU v7x, 32 devices: a whole 2x2x4 slice. The times are simulated.
32 devices in a mesh: row: 8 (over y, x, core), col: 4 (over z).
Axes of the slice: x: 2, y: 2, z: 4, core: 2. Of those that a mesh axis runs over, the one named last changes fastest.
Arguments:
- tiles: bfloat16 [8192, 128, 128], P(('row', 'col'))
- tile_src: int32 [8192], P(('row', 'col')), may hold values from 0 to 15
- tile_slot: int32 [8192], P(('row', 'col')), may hold values from 0 to 127
- slot_block: int32 [4096], P(('row', 'col')), may hold values from 0 to 15
- out_degree: int32 [65536], P(('row', 'col')), may hold values from 512 to 2047
- good_seeds: int32 [128, 4096], P(None, ('row', 'col')), may hold values from 0 to 65535, as said below
- spam_cores: int32 [128, 2048], P(None, ('row', 'col')), may hold values from 0 to 65535, as said below
Outputs:
- trust: float32 [65536, 128], P(('row', 'col'))
- distrust: float32 [65536, 128], P(('row', 'col'))
Inputs may be any that keep to these rules, and one draw needn't show every extreme that they name: `tile_slot`: slot s of a device belongs to the peer with index s // 4 along row+col. `slot_block`: entry p * 128 + s is the local index, among the 16 blocks held by peer s // 4, of the target block of slot s of device p. `good_seeds`: entries j * 128 to (j + 1) * 128 - 1 of each column's list are hosts of device j, from j * 2048 to (j + 1) * 2048 - 1. `spam_cores`: entries j * 64 to (j + 1) * 64 - 1 of each column's list are hosts of device j, from j * 2048 to (j + 1) * 2048 - 1.
All inputs are finite; a program needn't handle non-finite values.
Results may differ from a plain program's by a relative error of at most 0.0003.
Values may be sent and summed in bfloat16 or wider, within the bound.
A program may use at most 128 MiB of HBM per device.

v0:
```python
import functools

import jax
import jax.numpy as jnp
from jax import lax
from jax.experimental import pallas as pl
from jax.experimental.pallas import tpu as pltpu
from jax.sharding import PartitionSpec as P

AXES = ("row", "col")
VM = pl.BlockSpec(memory_space=pltpu.VMEM)
SM = pl.BlockSpec(memory_space=pltpu.SMEM)
F32 = jnp.float32
BF16 = jnp.bfloat16
WORD = 15
GROUP = 16
MESH = pl.DeviceIdType.MESH


def count_seeds(columns, source, target):
    blocks, seeds, size = target.shape
    hosts = blocks * size
    base = (lax.axis_index("row") * columns + lax.axis_index("col")) * hosts
    count = source.shape[1]
    factor = F32(hosts / count)
    block_iota = lax.broadcasted_iota(jnp.int32, (blocks, count), 0) * size
    lane_iota = lax.broadcasted_iota(jnp.int32, (size, count), 0)

    def one(s, _):
        local = source[pl.ds(s, 1), :] - base
        shifted = local - block_iota
        inside = jnp.where((shifted >= 0) & (shifted < size), F32(1), F32(0)).astype(BF16)
        start = jnp.max(jnp.where(local >= block_iota, block_iota, 0), axis=0, keepdims=True)
        lane = jnp.where(lane_iota == local - start, F32(1), F32(0)).astype(BF16)
        counts = lax.dot_general(
            inside, lane, (((1,), (1,)), ((), ())), preferred_element_type=F32
        )
        for b in range(blocks):
            target[b, pl.ds(s, 1), :] = counts[b : b + 1, :] * factor
        return 0

    lax.fori_loop(0, seeds, one, 0, unroll=4)


def exponent_of(peak):
    return jnp.floor(jnp.log2(jnp.maximum(peak, F32(2.0**-100)))) + F32(1)


def to_words(value):
    return jnp.clip(jnp.floor(value + F32(0.5)), F32(-32767), F32(32767))


def pack(first, cap, acc, out_ref):
    peers = out_ref.shape[0]
    size = acc.shape[2]
    tail = out_ref.shape[1] - cap * size

    def one(p, _):
        exps, cols = [], []
        for c in range(cap):
            n = p * cap + c
            value = acc[n, :size, :]
            e = exponent_of(jnp.max(jnp.abs(value), axis=0, keepdims=True))
            out_ref[p, c * size : (c + 1) * size, :] = to_words(value * jnp.exp2(WORD - e)).astype(
                jnp.int32
            ).astype(jnp.int16)
            exps.append(e)
            if first:
                col = acc[n, size : size + 8, :][:1, :]
                f = exponent_of(jnp.abs(col))
                scaled = col * jnp.exp2(WORD - f)
                high = to_words(scaled)
                cols += [f, high, to_words((scaled - high) * F32(2.0**WORD))]
        rows = exps + cols
        if tail > len(rows):
            rows.append(jnp.zeros((tail - len(rows), size), F32))
        out_ref[p, cap * size :, :] = jnp.concatenate(rows, axis=0).astype(jnp.int32).astype(jnp.int16)
        return 0

    lax.fori_loop(0, peers, one, 0)


def push_kernel(first, cap, *refs):
    if first:
        src_ref, slot_ref, good_ref, degree_ref, tiles_ref, out_ref, acc, scaled = refs
    else:
        src_ref, slot_ref, inflow, good_ref, degree_ref, tiles_ref, out_ref, acc, scaled = refs
    step = pl.program_id(0)
    blocks, seeds, size = good_ref.shape
    per_step = tiles_ref.shape[0]

    @pl.when(step == 0)
    def _():
        acc[...] = jnp.zeros_like(acc)
        def one(b, _):
            degree = degree_ref[b].astype(F32)
            trust = good_ref[b]
            if not first:
                trust = F32(0.85) * inflow[b] + F32(0.15) * trust
            scaled[b, :seeds, :] = (trust / degree).astype(BF16)
            if first:
                scaled[b, seeds:, :] = jnp.ones((scaled.shape[1] - seeds, size), BF16)
            return 0

        lax.fori_loop(0, blocks, one, 0)

    def some(g, _):
        products = []
        for k in range(GROUP):
            n = step * per_step + g * GROUP + k
            products.append(
                jnp.dot(scaled[src_ref[n]], tiles_ref[g * GROUP + k], preferred_element_type=F32)
            )
        for k in range(GROUP):
            acc[slot_ref[step * per_step + g * GROUP + k]] += products[k]
        return 0

    lax.fori_loop(0, per_step // GROUP, some, 0)

    @pl.when(step == pl.num_programs(0) - 1)
    def _():
        pack(first, cap, acc, out_ref)


def shares(shield_ref, weight_ref, start_of, share_ref):
    def one(b, _):
        share_ref[b] = (shield_ref[b] * start_of(b) / weight_ref[b]).astype(BF16)
        return 0

    lax.fori_loop(0, share_ref.shape[0], one, 0)


def greet(devices):
    barrier = pltpu.get_barrier_semaphore()
    for device, there in devices:
        @pl.when(there)
        def _():
            pl.semaphore_signal(barrier, inc=1, device_id=device, device_id_type=MESH)
    pl.semaphore_wait(barrier, sum(jnp.where(there, 1, 0) for _, there in devices))


def fetch_kernel(rows, columns, cap, want_ref, share_ref, fetched_ref, *scratch):
    line = 2 * (columns - 1)
    held, (picked, line_send, line_recv, send, recv) = scratch[:line], scratch[line:]
    r, z = lax.axis_index("row"), lax.axis_index("col")
    others = [lax.rem(r + d, rows) for d in range(1, rows)]
    sides = (-1, 1)
    inside = {side: (z + side >= 0) & (z + side < columns) for side in sides}
    greet([((t, z), t >= 0) for t in others] + [((r, z + side), inside[side]) for side in sides])

    def place(side, d):
        return 2 * (d - 1) + (0 if side < 0 else 1)

    def pass_on(source, d, side):
        slot = place(-side, d)
        return pltpu.make_async_remote_copy(
            src_ref=source, dst_ref=held[slot],
            send_sem=line_send.at[slot], recv_sem=line_recv.at[slot],
            device_id=(r, z + side), device_id_type=MESH,
        )

    def serve(t, origin):
        return pltpu.make_async_remote_copy(
            src_ref=picked.at[t, pl.ds(origin * cap, cap)],
            dst_ref=fetched_ref.at[pl.ds((r * columns + origin) * cap, cap)],
            send_sem=send.at[t, origin], recv_sem=recv.at[r, origin],
            device_id=(t, z), device_id_type=MESH,
        )

    def spread(source, origin):
        before = None
        for t in others:
            for j in range(cap):
                picked[t, origin * cap + j] = source[want_ref[t, origin * cap + j]]
            if before is not None:
                serve(before, origin).start()
            before = t
        for j in range(cap):
            fetched_ref[(r * columns + origin) * cap + j] = source[want_ref[r, origin * cap + j]]
        serve(before, origin).start()

    for side in sides:
        @pl.when(inside[side])
        def _():
            pass_on(share_ref, 1, side).start()
    spread(share_ref, z)
    for d in range(1, columns):
        for side in sides:
            origin = z + side * d

            @pl.when((origin >= 0) & (origin < columns))
            def _():
                here = held[place(side, d)]
                pass_on(share_ref, d, -side).wait_recv()

                if d < columns - 1:
                    @pl.when(inside[-side])
                    def _():
                        pass_on(here, d + 1, -side).start()

                spread(here, origin)
    for origin in range(columns):
        for t in others:
            serve(t, origin).wait_send()
            pltpu.make_async_remote_copy(
                src_ref=picked.at[t, pl.ds(origin * cap, cap)],
                dst_ref=fetched_ref.at[pl.ds((t * columns + origin) * cap, cap)],
                send_sem=send.at[t, origin], recv_sem=recv.at[t, origin],
                device_id=(t, z), device_id_type=MESH,
            ).wait_recv()
    for d in range(columns - 1):
        for side in sides:
            origin = z - side * d

            @pl.when((origin >= 0) & (origin < columns) & inside[side])
            def _():
                pass_on(share_ref, d + 1, side).wait_send()


def reduce_kernel(first, rows, columns, cap, want_ref, words_ref, *refs):
    if first:
        cores_ref, inflow_ref, weight_ref, spam_ref, *refs = refs
    else:
        inflow_ref, *refs = refs
    (landed, table, partial, exps, scales, packed, final,
     own, send, recv, line_send, line_recv) = refs
    r, z = lax.axis_index("row"), lax.axis_index("col")
    blocks, seeds, size = partial.shape
    others = [lax.rem(r + d, rows) for d in range(1, rows)]
    order = [columns // 2] + [d for d in range(1, columns) if d != columns // 2] + [0]
    block_iota = lax.broadcasted_iota(jnp.int32, (blocks, size), 0)
    data = blocks * seeds
    greet(
        [((t, z), t >= 0) for t in others]
        + [((r, lax.rem(z + d, columns)), z >= 0) for d in range(1, columns)]
    )

    def across(d, t, origin):
        return pltpu.make_async_remote_copy(
            src_ref=words_ref.at[t * columns + lax.rem(z + d, columns)], dst_ref=landed.at[d, origin],
            send_sem=send.at[d, t], recv_sem=recv.at[d, origin], device_id=(t, z), device_id_type=MESH,
        )

    def mine(d):
        return pltpu.make_async_copy(
            words_ref.at[r * columns + lax.rem(z + d, columns)], landed.at[d, r], own.at[d]
        )

    def along(d):
        return pltpu.make_async_remote_copy(
            src_ref=packed.at[d - 1], dst_ref=final.at[d - 1],
            send_sem=line_send.at[d - 1], recv_sem=line_recv.at[d - 1],
            device_id=(r, lax.rem(z + d, columns)), device_id_type=MESH,
        )

    def to_int16(value):
        return value.astype(jnp.int32).astype(jnp.int16)

    def to_float(value):
        return value.astype(jnp.int32).astype(F32)

    for d in order:
        for t in others:
            across(d, t, r).start()
        mine(d).start()
    if first:
        count_seeds(columns, cores_ref, spam_ref)

    cols = jnp.zeros((blocks, size), F32)
    for d in order:
        y = lax.rem(z + d, columns)
        mine(d).wait()
        for t in others:
            across(d, t, t).wait_recv()

        def weigh(q, cols):
            tail = to_float(landed[d, q, cap * seeds :, :])
            for c in range(cap):
                hit = block_iota == want_ref[q, y * cap + c]
                scale = jnp.exp2(tail[c : c + 1, :] - WORD)
                table[q * cap + c] = jnp.where(hit, jnp.broadcast_to(scale, (blocks, size)), F32(0))
                if first:
                    f, high, low = (tail[cap + 3 * c + i : cap + 3 * c + i + 1, :] for i in range(3))
                    col = (high + low * F32(2.0**-WORD)) * jnp.exp2(f - WORD)
                    cols = cols + jnp.where(hit, jnp.broadcast_to(col, (blocks, size)), F32(0))
            return cols

        cols = lax.fori_loop(0, rows, weigh, jnp.zeros((blocks, size), F32))

        def strip(i, _):
            at = pl.multiple_of(i * 16, 16)

            def add(q, sums):
                sums = list(sums)
                for c in range(cap):
                    value = to_float(landed[d, q, pl.ds(pl.multiple_of(c * seeds + at, 16), 16), :])
                    for b in range(blocks):
                        sums[b] = sums[b] + value * table[q * cap + c, b : b + 1, :]
                return tuple(sums)

            sums = lax.fori_loop(0, rows, add, (jnp.zeros((16, size), F32),) * blocks)
            for b in range(blocks):
                partial[b, pl.ds(at, 16), :] = sums[b]
            return 0

        lax.fori_loop(0, seeds // 16, strip, 0)
        if d:
            def squeeze(b, _):
                value = partial[b]
                e = exponent_of(jnp.max(jnp.abs(value), axis=0, keepdims=True))
                exps[pl.ds(b, 1), :] = e
                packed[d - 1, pl.ds(pl.multiple_of(b * seeds, seeds), seeds), :] = to_int16(
                    to_words(value * jnp.exp2(WORD - e))
                )
                return 0

            lax.fori_loop(0, blocks, squeeze, 0)
            packed[d - 1, data : data + blocks, :] = to_int16(exps[...])
            if first:
                f = exponent_of(jnp.abs(cols))
                scaled = cols * jnp.exp2(WORD - f)
                high = to_words(scaled)
                for i, row in enumerate((f, high, to_words((scaled - high) * F32(2.0**WORD)))):
                    packed[d - 1, data + (i + 1) * blocks : data + (i + 2) * blocks, :] = to_int16(row)
            along(d).start()

    for d in order[:-1]:
        along(d).wait_recv()
        scales[d - 1] = jnp.exp2(to_float(final[d - 1, data : data + blocks, :]) - WORD)
        if first:
            f, high, low = (
                to_float(final[d - 1, data + (i + 1) * blocks : data + (i + 2) * blocks, :])
                for i in range(3)
            )
            cols = cols + (high + low * F32(2.0**-WORD)) * jnp.exp2(f - WORD)
    if first:
        for b in range(blocks):
            weight_ref[b] = F32(1) + cols[b : b + 1, :]

    def finish(b, _):
        total = partial[b]
        for d in range(1, columns):
            value = to_float(final[d - 1, pl.ds(pl.multiple_of(b * seeds, seeds), seeds), :])
            total = total + value * scales[d - 1, pl.ds(b, 1), :]
        inflow_ref[b] = total
        return 0

    lax.fori_loop(0, blocks, finish, 0)
    for d in order:
        for t in others:
            across(d, t, r).wait_send()
    for d in order[:-1]:
        along(d).wait_send()


def trust_kernel(inflow, good_ref, spam_ref, weight_ref, trust_ref, shield_ref, share_ref):
    size = inflow.shape[2]

    def one(b, _):
        trust = F32(0.85) * inflow[b] + F32(0.15) * good_ref[b]
        trust_ref[pl.ds(pl.multiple_of(b * size, size), size), :] = jnp.transpose(trust)
        shield_ref[b] = F32(1) / (F32(1) + trust)
        return 0

    lax.fori_loop(0, inflow.shape[0], one, 0)
    shares(shield_ref, weight_ref, lambda b: spam_ref[b], share_ref)


def pull_kernel(last, *refs):
    if last:
        src_ref, slot_ref, fetched_ref, spam_ref, tiles_ref, out_ref, acc = refs
    else:
        (src_ref, slot_ref, fetched_ref, spam_ref, shield_ref, weight_ref, tiles_ref,
         out_ref, acc) = refs
    step = pl.program_id(0)
    per_step = tiles_ref.shape[0]
    size = acc.shape[2]

    @pl.when(step == 0)
    def _():
        acc[...] = jnp.zeros_like(acc)

    def some(g, _):
        products = []
        for k in range(GROUP):
            n = step * per_step + g * GROUP + k
            products.append(
                lax.dot_general(
                    fetched_ref[slot_ref[n]], tiles_ref[g * GROUP + k], (((1,), (1,)), ((), ())),
                    preferred_element_type=F32,
                )
            )
        for k in range(GROUP):
            acc[src_ref[step * per_step + g * GROUP + k]] += products[k]
        return 0

    lax.fori_loop(0, per_step // GROUP, some, 0)

    @pl.when(step == pl.num_programs(0) - 1)
    def _():
        def distrust(b):
            return F32(0.85) * acc[b] + F32(0.15) * spam_ref[b]

        if last:
            def one(b, _):
                out_ref[pl.ds(pl.multiple_of(b * size, size), size), :] = jnp.transpose(distrust(b))
                return 0

            lax.fori_loop(0, acc.shape[0], one, 0)
        else:
            shares(shield_ref, weight_ref, distrust, out_ref)


def body(columns, tiles, tile_src, tile_slot, slot_block, out_degree, good_seeds, spam_cores):
    tile_count, size, _ = tiles.shape
    hosts = out_degree.shape[0]
    blocks = hosts // size
    seeds = good_seeds.shape[0]
    slots = slot_block.shape[0]
    peers = lax.axis_size(AXES)
    cap = slots // peers
    tail = -(-4 * cap // 16) * 16
    steps = 8
    shape = jax.ShapeDtypeStruct
    vector = (blocks, seeds, size)
    degree = out_degree.reshape(blocks, 1, size)

    rows = peers // columns
    want = lax.all_to_all(
        slot_block.reshape(rows, columns * cap), "row", split_axis=0, concat_axis=0, tiled=True
    )
    good = pl.pallas_call(
        functools.partial(count_seeds, columns),
        out_shape=shape(vector, F32),
        in_specs=[VM],
        out_specs=VM,
    )(good_seeds)

    tile_spec = pl.BlockSpec((tile_count // steps, size, size), lambda i: (i, 0, 0))
    words = shape((peers, cap * size + tail, size), jnp.int16)
    outgoing = pl.pallas_call(
        functools.partial(push_kernel, True, cap),
        grid=(steps,),
        out_shape=words,
        in_specs=[SM, SM, VM, VM, tile_spec],
        out_specs=VM,
        scratch_shapes=[
            pltpu.VMEM((slots, seeds + 16, size), F32),
            pltpu.VMEM((blocks, seeds + 16, size), BF16),
        ],
    )(tile_src, tile_slot, good, degree, tiles)
    def reduce(first, words_in, *rest):
        long = blocks * seeds + blocks * (4 if first else 1)
        outs = (shape(vector, F32), shape((blocks, 1, size), F32), shape(vector, F32))
        return pl.pallas_call(
            functools.partial(reduce_kernel, first, rows, columns, cap),
            out_shape=outs if first else outs[:1],
            in_specs=[SM, VM, VM] if first else [SM, VM],
            out_specs=(VM, VM, VM) if first else (VM,),
            scratch_shapes=[
                pltpu.VMEM((columns, rows, cap * size + tail, size), jnp.int16),
                pltpu.VMEM((rows * cap, blocks, size), F32),
                pltpu.VMEM(vector, F32),
                pltpu.VMEM((blocks, size), F32),
                pltpu.VMEM((columns - 1, blocks, size), F32),
                pltpu.VMEM((columns - 1, long, size), jnp.int16),
                pltpu.VMEM((columns - 1, long, size), jnp.int16),
                pltpu.SemaphoreType.DMA((columns,)),
                pltpu.SemaphoreType.DMA((columns, rows)),
                pltpu.SemaphoreType.DMA((columns, rows)),
                pltpu.SemaphoreType.DMA((columns - 1,)),
                pltpu.SemaphoreType.DMA((columns - 1,)),
            ],
            compiler_params=pltpu.CompilerParams(
                collective_id=1 if first else 2, has_side_effects=True
            ),
        )(want, words_in, *rest)

    inflow, weight, spam = reduce(True, outgoing, spam_cores)
    outgoing = pl.pallas_call(
        functools.partial(push_kernel, False, cap),
        grid=(steps,),
        out_shape=words,
        in_specs=[SM, SM, VM, VM, VM, tile_spec],
        out_specs=VM,
        scratch_shapes=[
            pltpu.VMEM((slots, seeds, size), F32),
            pltpu.VMEM(vector, BF16),
        ],
    )(tile_src, tile_slot, inflow, good, degree, tiles)
    (inflow,) = reduce(False, outgoing)
    fetch = pl.pallas_call(
        functools.partial(fetch_kernel, rows, columns, cap),
        out_shape=shape((slots, seeds, size), BF16),
        in_specs=[SM, VM],
        out_specs=VM,
        scratch_shapes=[
            *[pltpu.VMEM(vector, BF16)] * (2 * columns - 2),
            pltpu.VMEM((rows, columns * cap, seeds, size), BF16),
            pltpu.SemaphoreType.DMA((2 * columns - 2,)),
            pltpu.SemaphoreType.DMA((2 * columns - 2,)),
            pltpu.SemaphoreType.DMA((rows, columns)),
            pltpu.SemaphoreType.DMA((rows, columns)),
        ],
        compiler_params=pltpu.CompilerParams(collective_id=0, has_side_effects=True),
    )
    trust, shield, share = pl.pallas_call(
        trust_kernel,
        out_shape=(shape((hosts, seeds), F32), shape(vector, F32), shape(vector, BF16)),
        in_specs=[VM, VM, VM, VM],
        out_specs=(VM, VM, VM),
    )(inflow, good, spam, weight)
    fetched = fetch(want, share)
    share = pl.pallas_call(
        functools.partial(pull_kernel, False),
        grid=(steps,),
        out_shape=shape(vector, BF16),
        in_specs=[SM, SM, VM, VM, VM, VM, tile_spec],
        out_specs=VM,
        scratch_shapes=[pltpu.VMEM(vector, F32)],
    )(tile_src, tile_slot, fetched, spam, shield, weight, tiles)
    fetched = fetch(want, share)
    distrust = pl.pallas_call(
        functools.partial(pull_kernel, True),
        grid=(steps,),
        out_shape=shape((hosts, seeds), F32),
        in_specs=[SM, SM, VM, VM, tile_spec],
        out_specs=VM,
        scratch_shapes=[pltpu.VMEM(vector, F32)],
    )(tile_src, tile_slot, fetched, spam, tiles)
    return trust, distrust


def solution(mesh):
    in_specs = (
        P(AXES, None, None),
        P(AXES),
        P(AXES),
        P(AXES),
        P(AXES),
        P(None, AXES),
        P(None, AXES),
    )
    out_specs = (P(AXES, None), P(AXES, None))
    return jax.shard_map(
        functools.partial(body, mesh.shape["col"]),
        mesh=mesh, in_specs=in_specs, out_specs=out_specs, check_vma=False,
    )
```

profile of v0, /device:TPU:1, one launch (start us, length us, event | category | flops | bytes accessed | tf_op | source)
XLA Modules:
  0.0 336.0 jit_solution(16239207312194530448)
XLA Ops:
  0.6 1.3 all_to_all.7
  2.0 5.2 %all-to-all-start = ((s32[8,1,16]{2,1,0:T(1,128)}), s32[8,1,16]{2,1,0:T(1,128)S(1)}, u32[]{:S(2)}, u32[]{:S(2)}) async-start(s32[8,1,16]{2,1,0:T(1,128)} %bitcast), calls=%async_computation | async-start | bytes 8192 | tf_op jit(solution)/shard_map/all_to_all | solution.py:429
  7.2 1.5 copy.11.refs_0_
  8.7 8.4 %shard_map.86.refs_2_.refs_3_.good_ref = f32[16,128,128]{2,1,0:T(8,128)} custom-call(s32[128,128]{1,0:T(8,128)} %source.1), custom_call_target="tpu_custom_call" | custom-call | tf_op jit(solution)/shard_map/pallas_call | solution.py:432
  17.1 16.5 %shard_map.87.words_ref = s16[32,528,128]{2,1,0:T(8,128)(2,1)} custom-call(s32[256]{0:T(256)} %refs_0_.8, s32[256]{0:T(256)} %refs_1_.7, f32[16,128,128]{2,1,0:T(8,128)} %shard_map.86.refs_2_.refs_3_.good_ref, s32[16,1,128]{2,1,0:T(1,128)} %bitcast.7, bf16[256,128,128]{2,1,0:T(8,128)(2,1)} %refs_4_.3), custom_call_target="tpu_custom_call" | custom-call | tf_op jit(solution)/shard_map/pallas_call | solution.py:441
  33.5 0.0 all-to-all-done
  33.5 0.0 copy-start
  33.6 0.6 copy-done
  34.1 72.8 %shard_map.88 = (f32[16,128,128]{2,1,0:T(8,128)}, f32[16,1,128]{2,1,0:T(1,128)}, f32[16,128,128]{2,1,0:T(8,128)}) custom-call(s32[8,16]{1,0:T(8,128)} %bitcast.3, s16[32,528,128]{2,1,0:T(8,128)(2,1)} %shard_map.87.words_ref, s32[128,64]{1,0:T(8,128)} %copy.11.refs_0_), custom_call_target="tpu_custom_call" | custom-call | tf_op jit(solution)/shard_map/pallas_call | solution.py:455
  107.0 15.1 %shard_map.89.words_ref = s16[32,528,128]{2,1,0:T(8,128)(2,1)} custom-call(s32[256]{0:T(256)} %refs_0_.8, s32[256]{0:T(256)} %refs_1_.7, f32[16,128,128]{2,1,0:T(8,128)} %get-tuple-element.8.refs_2_, f32[16,128,128]{2,1,0:T(8,128)} %shard_map.86.refs_2_.refs_3_.good_ref, s32[16,1,128]{2,1,0:T(1,128)} %bitcast.8, bf16[256,128,128]{2,1,0:T(8,128)(2,1)} %refs_4_.3), custom_call_target="tpu_custom_call" | custom-call | tf_op jit(solution)/shard_map/pallas_call | solution.py:480
  122.1 70.0 %shard_map.90.inflow = f32[16,128,128]{2,1,0:T(8,128)} custom-call(s32[8,16]{1,0:T(8,128)} %bitcast.4, s16[32,528,128]{2,1,0:T(8,128)(2,1)} %shard_map.89.words_ref), custom_call_target="tpu_custom_call" | custom-call | tf_op jit(solution)/shard_map/pallas_call | solution.py:455
  192.1 5.3 %shard_map.91 = (f32[2048,128]{1,0:T(8,128)}, f32[16,128,128]{2,1,0:T(8,128)}, bf16[16,128,128]{2,1,0:T(8,128)(2,1)}) custom-call(f32[16,128,128]{2,1,0:T(8,128)} %shard_map.90.inflow, f32[16,128,128]{2,1,0:T(8,128)} %shard_map.86.refs_2_.refs_3_.good_ref, f32[16,128,128]{2,1,0:T(8,128)} %get-tuple-element.9.spam_ref.refs_3_, ...), custom_call_target="tpu_custom_call" | custom-call | tf_op jit(solution)/shard_map/pallas_call | solution.py:507
  197.3 54.9 %shard_map.92.refs_2_ = bf16[128,128,128]{2,1,0:T(8,128)(2,1)} custom-call(s32[8,16]{1,0:T(8,128)} %bitcast.5, bf16[16,128,128]{2,1,0:T(8,128)(2,1)} %get-tuple-element.12.share_ref), custom_call_target="tpu_custom_call" | custom-call | tf_op jit(solution)/shard_map/pallas_call | solution.py:513
  252.2 13.2 %shard_map.93.share_ref = bf16[16,128,128]{2,1,0:T(8,128)(2,1)} custom-call(s32[256]{0:T(256)} %refs_0_.8, s32[256]{0:T(256)} %refs_1_.7, bf16[128,128,128]{2,1,0:T(8,128)(2,1)} %shard_map.92.refs_2_, f32[16,128,128]{2,1,0:T(8,128)} %get-tuple-element.9.spam_ref.refs_3_, f32[16,128,128]{2,1,0:T(8,128)} %get-tuple-element.13.refs_4_, ...), custom_call_target="tpu_custom_call" | custom-call | tf_op jit(solution)/shard_map/pallas_call | solution.py:514
  265.4 56.3 %shard_map.94.refs_2_ = bf16[128,128,128]{2,1,0:T(8,128)(2,1)} custom-call(s32[8,16]{1,0:T(8,128)} %bitcast.6, bf16[16,128,128]{2,1,0:T(8,128)(2,1)} %shard_map.93.share_ref), custom_call_target="tpu_custom_call" | custom-call | tf_op jit(solution)/shard_map/pallas_call | solution.py:522
  321.6 14.4 %shard_map.95 = f32[2048,128]{1,0:T(8,128)} custom-call(s32[256]{0:T(256)} %refs_0_.8, s32[256]{0:T(256)} %refs_1_.7, bf16[128,128,128]{2,1,0:T(8,128)(2,1)} %shard_map.94.refs_2_, f32[16,128,128]{2,1,0:T(8,128)} %get-tuple-element.9.spam_ref.refs_3_, bf16[256,128,128]{2,1,0:T(8,128)(2,1)} %refs_4_.3), custom_call_target="tpu_custom_call" | custom-call | tf_op jit(solution)/shard_map/pallas_call | solution.py:523
Async XLA Ops:
  2.0 31.6 %all-to-all-start = ((s32[8,1,16]{2,1,0:T(1,128)}), s32[8,1,16]{2,1,0:T(1,128)S(1)}, u32[]{:S(2)}, u32[]{:S(2)}) async-start(s32[8,1,16]{2,1,0:T(1,128)} %bitcast), calls=%async_computation | async-start | bytes 8192 | tf_op jit(solution)/shard_map/all_to_all | solution.py:429
  33.5 0.6 copy-start
where the time goes:
time: 337 us; the launch traced here: 336 us
  Pallas kernels  327 us (97%)
  starting transfers between devices  5.21 us (2%)
  local copies, waits for them, and re-layouts  3.41 us (1%)
    pallas_call x2, Pallas kernels, reduce(): pl.pallas_call(functools.partial(reduce_kernel, first, rows, columns, cap...  143 us
    pallas_call x2, Pallas kernels, body(): fetched = fetch(want, share)  111 us
    pallas_call x1, Pallas kernels, body(): pl.pallas_call(functools.partial(push_kernel, True, cap), grid=(steps,),...  16.5 us
    pallas_call x1, Pallas kernels, body(): pl.pallas_call(functools.partial(push_kernel, False, cap), grid=(steps,),...  15.1 us
    pallas_call x1, Pallas kernels, body(): pl.pallas_call(functools.partial(pull_kernel, True), grid=(steps,), out_s...  14.4 us
    pallas_call x1, Pallas kernels, body(): pl.pallas_call(functools.partial(pull_kernel, False), grid=(steps,), out_...  13.2 us
    pallas_call x1, Pallas kernels, body(): pl.pallas_call(functools.partial(count_seeds, columns), out_shape=shape(v...  8.41 us
  transfers between devices with their start and end apart: 1, of which 0 were waited for; matrix products, arithmetic and copies ran while one was open for 0% of the time, Pallas kernels for 7%

commit v1 on v0

--- a/solution.py
+++ b/solution.py
@@ -10,14 +10,16 @@
 AXES = ("row", "col")
 VM = pl.BlockSpec(memory_space=pltpu.VMEM)
 SM = pl.BlockSpec(memory_space=pltpu.SMEM)
+ANY = pl.BlockSpec(memory_space=pl.ANY)
 F32 = jnp.float32
 BF16 = jnp.bfloat16
 WORD = 15
 GROUP = 16
+HALVES = 2
 MESH = pl.DeviceIdType.MESH
 
 
-def count_seeds(columns, source, target):
+def count_seeds(columns, source, target, step=0, pieces=1):
     blocks, seeds, size = target.shape
     hosts = blocks * size
     base = (lax.axis_index("row") * columns + lax.axis_index("col")) * hosts
@@ -39,7 +41,8 @@
             target[b, pl.ds(s, 1), :] = counts[b : b + 1, :] * factor
         return 0
 
-    lax.fori_loop(0, seeds, one, 0, unroll=4)
+    share = seeds // pieces
+    lax.fori_loop(step * share, (step + 1) * share, one, 0, unroll=4)
 
 
 def exponent_of(peak):
@@ -50,9 +53,10 @@
     return jnp.clip(jnp.floor(value + F32(0.5)), F32(-32767), F32(32767))
 
 
-def pack(first, cap, acc, out_ref):
+def pack(first, cap, part, bits, acc, block_ref, out_ref):
     peers = out_ref.shape[0]
     size = acc.shape[2]
+    halves = size // part
     tail = out_ref.shape[1] - cap * size
 
     def one(p, _):
@@ -61,10 +65,11 @@
             n = p * cap + c
             value = acc[n, :size, :]
             e = exponent_of(jnp.max(jnp.abs(value), axis=0, keepdims=True))
-            out_ref[p, c * size : (c + 1) * size, :] = to_words(value * jnp.exp2(WORD - e)).astype(
-                jnp.int32
-            ).astype(jnp.int16)
-            exps.append(e)
+            words = to_words(value * jnp.exp2(WORD - e)).astype(jnp.int32).astype(jnp.int16)
+            for h in range(halves):
+                at = (h * cap + c) * part + (tail if h else 0)
+                out_ref[p, at : at + part, :] = words[h * part : (h + 1) * part, :]
+            exps.append(e * F32(2**bits) + block_ref[n].astype(F32))
             if first:
                 col = acc[n, size : size + 8, :][:1, :]
                 f = exponent_of(jnp.abs(col))
@@ -74,17 +79,18 @@
         rows = exps + cols
         if tail > len(rows):
             rows.append(jnp.zeros((tail - len(rows), size), F32))
-        out_ref[p, cap * size :, :] = jnp.concatenate(rows, axis=0).astype(jnp.int32).astype(jnp.int16)
+        at = cap * part
+        out_ref[p, at : at + tail, :] = jnp.concatenate(rows, axis=0).astype(jnp.int32).astype(jnp.int16)
         return 0
 
     lax.fori_loop(0, peers, one, 0)
 
 
-def push_kernel(first, cap, *refs):
+def push_kernel(first, cap, part, *refs):
     if first:
-        src_ref, slot_ref, good_ref, degree_ref, tiles_ref, out_ref, acc, scaled = refs
+        src_ref, slot_ref, block_ref, good_ref, degree_ref, tiles_ref, out_ref, acc, scaled = refs
     else:
-        src_ref, slot_ref, inflow, good_ref, degree_ref, tiles_ref, out_ref, acc, scaled = refs
+        src_ref, slot_ref, block_ref, inflow, good_ref, degree_ref, tiles_ref, out_ref, acc, scaled = refs
     step = pl.program_id(0)
     blocks, seeds, size = good_ref.shape
     per_step = tiles_ref.shape[0]
@@ -119,12 +125,13 @@
 
     @pl.when(step == pl.num_programs(0) - 1)
     def _():
-        pack(first, cap, acc, out_ref)
+        pack(first, cap, part, blocks.bit_length() - 1, acc, block_ref, out_ref)
 
 
 def shares(shield_ref, weight_ref, start_of, share_ref):
     def one(b, _):
-        share_ref[b] = (shield_ref[b] * start_of(b) / weight_ref[b]).astype(BF16)
+        weight = weight_ref[pl.ds(b, 1), :]
+        share_ref[b] = (shield_ref[b] * start_of(b) / weight).astype(BF16)
         return 0
 
     lax.fori_loop(0, share_ref.shape[0], one, 0)
@@ -171,12 +178,12 @@
         before = None
         for t in others:
             for j in range(cap):
-                picked[t, origin * cap + j] = source[want_ref[t, origin * cap + j]]
+                picked[t, origin * cap + j] = source[want_ref[t, 0, (r * columns + origin) * cap + j]]
             if before is not None:
                 serve(before, origin).start()
             before = t
         for j in range(cap):
-            fetched_ref[(r * columns + origin) * cap + j] = source[want_ref[r, origin * cap + j]]
+            fetched_ref[(r * columns + origin) * cap + j] = source[want_ref[r, 0, (r * columns + origin) * cap + j]]
         serve(before, origin).start()
 
     for side in sides:
@@ -217,40 +224,70 @@
                 pass_on(share_ref, d + 1, side).wait_send()
 
 
-def reduce_kernel(first, rows, columns, cap, want_ref, words_ref, *refs):
+def order_of(z, columns):
+    table = []
+    for plane in range(columns):
+        line = []
+        for k in range(columns):
+            if columns - 1 - k > plane:
+                line.append(columns - 1 - k)
+            if k < plane:
+                line.append(k)
+        table.append(line + [plane])
+    picks = []
+    for i in range(columns):
+        pick = z * 0
+        for plane in range(columns):
+            pick = pick + jnp.where(z == plane, table[plane][i], 0)
+        picks.append(pick)
+    return picks
+
+
+def reduce_kernel(first, rows, columns, cap, words_ref, *refs):
     if first:
-        cores_ref, inflow_ref, weight_ref, spam_ref, *refs = refs
+        cores_ref, mine_ref, inflow_ref, weight_ref, spam_ref, want_ref, *refs = refs
     else:
         inflow_ref, *refs = refs
-    (landed, table, partial, exps, scales, packed, final,
-     own, send, recv, line_send, line_recv) = refs
+    landed, table, partial, exps, packed, inbox, own, send, recv, chain_send, chain_recv, *refs = refs
     r, z = lax.axis_index("row"), lax.axis_index("col")
-    blocks, seeds, size = partial.shape
+    blocks, part, size = partial.shape
+    seeds = inflow_ref.shape[1]
+    halves = seeds // part
+    bits = blocks.bit_length() - 1
+    tail_at = cap * part
+    spans = []
+    for h in range(halves):
+        start = spans[-1][0] + spans[-1][1] if spans else 0
+        spans.append((start, cap * part + (landed.shape[2] - cap * seeds if h == 0 else 0)))
+    data = blocks * part
+    longs = [data + blocks * (4 if first and h == 0 else 1) for h in range(halves)]
     others = [lax.rem(r + d, rows) for d in range(1, rows)]
-    order = [columns // 2] + [d for d in range(1, columns) if d != columns // 2] + [0]
+    targets = order_of(z, columns)
     block_iota = lax.broadcasted_iota(jnp.int32, (blocks, size), 0)
-    data = blocks * seeds
     greet(
         [((t, z), t >= 0) for t in others]
-        + [((r, lax.rem(z + d, columns)), z >= 0) for d in range(1, columns)]
+        + [((r, z - 1), z > 0), ((r, z + 1), z < columns - 1)]
     )
 
-    def across(d, t, origin):
+    def across(i, h, t, origin):
+        at = pl.ds(*spans[h])
         return pltpu.make_async_remote_copy(
-            src_ref=words_ref.at[t * columns + lax.rem(z + d, columns)], dst_ref=landed.at[d, origin],
-            send_sem=send.at[d, t], recv_sem=recv.at[d, origin], device_id=(t, z), device_id_type=MESH,
+            src_ref=words_ref.at[t * columns + targets[i], at], dst_ref=landed.at[i, origin, at],
+            send_sem=send.at[i, h, t], recv_sem=recv.at[i, h, origin],
+            device_id=(t, z), device_id_type=MESH,
         )
 
-    def mine(d):
+    def mine(i):
         return pltpu.make_async_copy(
-            words_ref.at[r * columns + lax.rem(z + d, columns)], landed.at[d, r], own.at[d]
+            words_ref.at[r * columns + targets[i]], landed.at[i, r], own.at[i]
         )
 
-    def along(d):
+    def chain(i, h, side):
+        at = pl.ds(0, longs[h])
         return pltpu.make_async_remote_copy(
-            src_ref=packed.at[d - 1], dst_ref=final.at[d - 1],
-            send_sem=line_send.at[d - 1], recv_sem=line_recv.at[d - 1],
-            device_id=(r, lax.rem(z + d, columns)), device_id_type=MESH,
+            src_ref=packed.at[min(i, columns - 2), h, at], dst_ref=inbox.at[side, targets[i], h, at],
+            send_sem=chain_send.at[min(i, columns - 2), h], recv_sem=chain_recv.at[side, targets[i], h],
+            device_id=(r, z + 1 - 2 * side), device_id_type=MESH,
         )
 
     def to_int16(value):
@@ -259,98 +296,151 @@
     def to_float(value):
         return value.astype(jnp.int32).astype(F32)
 
-    for d in order:
+    if first:
+        known_send, known_recv = refs
+
+        def know(t, origin):
+            return pltpu.make_async_remote_copy(
+                src_ref=mine_ref, dst_ref=want_ref.at[origin],
+                send_sem=known_send.at[t], recv_sem=known_recv.at[origin],
+                device_id=(t, z), device_id_type=MESH,
+            )
+
         for t in others:
-            across(d, t, r).start()
-        mine(d).start()
+            know(t, r).start()
+        want_ref[r] = mine_ref[...]
+    for i in range(columns):
+        for h in range(halves):
+            for t in others:
+                across(i, h, t, r).start()
+        mine(i).start()
+
+    pieces = min(4, (columns - 1) * halves)
+    for i in range(columns):
+        mine(i).wait()
+        side = jnp.where(targets[i] > z, 0, 1)
+        joined = jnp.where(targets[i] > z, z > 0, z < columns - 1)
+        cols = jnp.zeros((blocks, size), F32)
+        for h in range(halves):
+            for t in others:
+                across(i, h, t, t).wait_recv()
+            if h == 0:
+                def weigh(q, cols):
+                    tail = landed[i, q, tail_at : spans[0][1], :].astype(jnp.int32)
+                    for c in range(cap):
+                        word = tail[c : c + 1, :]
+                        hit = block_iota == (word & (blocks - 1))
+                        scale = jnp.exp2((word >> bits).astype(F32) - WORD)
+                        table[q * cap + c] = jnp.where(
+                            hit, jnp.broadcast_to(scale, (blocks, size)), F32(0)
+                        )
+                        if first:
+                            f, high, low = (
+                                tail[cap + 3 * c + k : cap + 3 * c + k + 1, :].astype(F32) for k in range(3)
+                            )
+                            col = (high + low * F32(2.0**-WORD)) * jnp.exp2(f - WORD)
+                            cols = cols + jnp.where(hit, jnp.broadcast_to(col, (blocks, size)), F32(0))
+                    return cols
+
+                cols = lax.fori_loop(0, rows, weigh, cols)
+
+            begin = spans[h][0]
+
+            def strip(k, _):
+                at = pl.multiple_of(k * 16, 16)
+
+                def add(q, sums):
+                    sums = list(sums)
+                    for c in range(cap):
+                        spot = pl.multiple_of(begin + c * part + at, 16)
+                        value = to_float(landed[i, q, pl.ds(spot, 16), :])
+                        for b in range(blocks):
+                            sums[b] = sums[b] + value * table[q * cap + c, b : b + 1, :]
+                    return tuple(sums)
+
+                sums = lax.fori_loop(0, rows, add, (jnp.zeros((16, size), F32),) * blocks)
+                for b in range(blocks):
+                    partial[b, pl.ds(at, 16), :] = sums[b]
+                return 0
+
+            lax.fori_loop(0, part // 16, strip, 0)
+
+            def join(way):
+                chain(i, h, way).wait_recv()
+                exps[...] = jnp.exp2(to_float(inbox[way, targets[i], h, data : data + blocks, :]) - WORD)
+
+                def one(b, _):
+                    got = to_float(inbox[way, targets[i], h, pl.ds(pl.multiple_of(b * part, part), part), :])
+                    partial[b] += got * exps[pl.ds(b, 1), :]
+                    return 0
+
+                lax.fori_loop(0, blocks, one, 0)
+
+            def join_cols(way):
+                f, high, low = (
+                    to_float(inbox[way, targets[i], h, data + (k + 1) * blocks : data + (k + 2) * blocks, :])
+                    for k in range(3)
+                )
+                colsum[...] += (high + low * F32(2.0**-WORD)) * jnp.exp2(f - WORD)
+
+            if first and h == 0:
+                colsum = weight_ref
+                colsum[...] = cols
+            if i < columns - 1:
+                @pl.when(joined)
+                def _():
+                    join(side)
+                    if first and h == 0:
+                        join_cols(side)
+
+                def squeeze(b, _):
+                    value = partial[b]
+                    e = exponent_of(jnp.max(jnp.abs(value), axis=0, keepdims=True))
+                    exps[pl.ds(b, 1), :] = e
+                    packed[i, h, pl.ds(pl.multiple_of(b * part, part), part), :] = to_int16(
+                        to_words(value * jnp.exp2(WORD - e))
+                    )
+                    return 0
+
+                lax.fori_loop(0, blocks, squeeze, 0)
+                packed[i, h, data : data + blocks, :] = to_int16(exps[...])
+                if first and h == 0:
+                    col = colsum[...]
+                    f = exponent_of(jnp.abs(col))
+                    scaled = col * jnp.exp2(WORD - f)
+                    high = to_words(scaled)
+                    for k, row in enumerate((f, high, to_words((scaled - high) * F32(2.0**WORD)))):
+                        packed[i, h, data + (k + 1) * blocks : data + (k + 2) * blocks, :] = to_int16(row)
+                chain(i, h, side).start()
+            else:
+                for way, there in ((0, z > 0), (1, z < columns - 1)):
+                    @pl.when(there)
+                    def _():
+                        join(way)
+                        if first and h == 0:
+                            join_cols(way)
+
+                def finish(b, _):
+                    inflow_ref[b, h * part : (h + 1) * part, :] = partial[b]
+                    return 0
+
+                lax.fori_loop(0, blocks, finish, 0)
+                if first and h == 0:
+                    colsum[...] += F32(1)
+            step = i * halves + h
+            if first and step < pieces:
+                count_seeds(columns, cores_ref, spam_ref, step, pieces)
+
     if first:
-        count_seeds(columns, cores_ref, spam_ref)
-
-    cols = jnp.zeros((blocks, size), F32)
-    for d in order:
-        y = lax.rem(z + d, columns)
-        mine(d).wait()
         for t in others:
-            across(d, t, t).wait_recv()
-
-        def weigh(q, cols):
-            tail = to_float(landed[d, q, cap * seeds :, :])
-            for c in range(cap):
-                hit = block_iota == want_ref[q, y * cap + c]
-                scale = jnp.exp2(tail[c : c + 1, :] - WORD)
-                table[q * cap + c] = jnp.where(hit, jnp.broadcast_to(scale, (blocks, size)), F32(0))
-                if first:
-                    f, high, low = (tail[cap + 3 * c + i : cap + 3 * c + i + 1, :] for i in range(3))
-                    col = (high + low * F32(2.0**-WORD)) * jnp.exp2(f - WORD)
-                    cols = cols + jnp.where(hit, jnp.broadcast_to(col, (blocks, size)), F32(0))
-            return cols
-
-        cols = lax.fori_loop(0, rows, weigh, jnp.zeros((blocks, size), F32))
-
-        def strip(i, _):
-            at = pl.multiple_of(i * 16, 16)
-
-            def add(q, sums):
-                sums = list(sums)
-                for c in range(cap):
-                    value = to_float(landed[d, q, pl.ds(pl.multiple_of(c * seeds + at, 16), 16), :])
-                    for b in range(blocks):
-                        sums[b] = sums[b] + value * table[q * cap + c, b : b + 1, :]
-                return tuple(sums)
-
-            sums = lax.fori_loop(0, rows, add, (jnp.zeros((16, size), F32),) * blocks)
-            for b in range(blocks):
-                partial[b, pl.ds(at, 16), :] = sums[b]
-            return 0
-
-        lax.fori_loop(0, seeds // 16, strip, 0)
-        if d:
-            def squeeze(b, _):
-                value = partial[b]
-                e = exponent_of(jnp.max(jnp.abs(value), axis=0, keepdims=True))
-                exps[pl.ds(b, 1), :] = e
-                packed[d - 1, pl.ds(pl.multiple_of(b * seeds, seeds), seeds), :] = to_int16(
-                    to_words(value * jnp.exp2(WORD - e))
-                )
-                return 0
-
-            lax.fori_loop(0, blocks, squeeze, 0)
-            packed[d - 1, data : data + blocks, :] = to_int16(exps[...])
-            if first:
-                f = exponent_of(jnp.abs(cols))
-                scaled = cols * jnp.exp2(WORD - f)
-                high = to_words(scaled)
-                for i, row in enumerate((f, high, to_words((scaled - high) * F32(2.0**WORD)))):
-                    packed[d - 1, data + (i + 1) * blocks : data + (i + 2) * blocks, :] = to_int16(row)
-            along(d).start()
-
-    for d in order[:-1]:
-        along(d).wait_recv()
-        scales[d - 1] = jnp.exp2(to_float(final[d - 1, data : data + blocks, :]) - WORD)
-        if first:
-            f, high, low = (
-                to_float(final[d - 1, data + (i + 1) * blocks : data + (i + 2) * blocks, :])
-                for i in range(3)
-            )
-            cols = cols + (high + low * F32(2.0**-WORD)) * jnp.exp2(f - WORD)
-    if first:
-        for b in range(blocks):
-            weight_ref[b] = F32(1) + cols[b : b + 1, :]
-
-    def finish(b, _):
-        total = partial[b]
-        for d in range(1, columns):
-            value = to_float(final[d - 1, pl.ds(pl.multiple_of(b * seeds, seeds), seeds), :])
-            total = total + value * scales[d - 1, pl.ds(b, 1), :]
-        inflow_ref[b] = total
-        return 0
-
-    lax.fori_loop(0, blocks, finish, 0)
-    for d in order:
-        for t in others:
-            across(d, t, r).wait_send()
-    for d in order[:-1]:
-        along(d).wait_send()
+            know(t, r).wait_send()
+            know(t, t).wait_recv()
+    for i in range(columns):
+        for h in range(halves):
+            for t in others:
+                across(i, h, t, r).wait_send()
+            if i < columns - 1:
+                chain(i, h, jnp.where(targets[i] > z, 0, 1)).wait_send()
 
 
 def trust_kernel(inflow, good_ref, spam_ref, weight_ref, trust_ref, shield_ref, share_ref):
@@ -411,6 +501,11 @@
             shares(shield_ref, weight_ref, distrust, out_ref)
 
 
+def start_kernel(columns, good_ref, spam_ref, count_ref, list_ref):
+    list_ref[...] = jnp.transpose(spam_ref[...].astype(F32)).astype(jnp.int32)
+    count_seeds(columns, good_ref, count_ref)
+
+
 def body(columns, tiles, tile_src, tile_slot, slot_block, out_degree, good_seeds, spam_cores):
     tile_count, size, _ = tiles.shape
     hosts = out_degree.shape[0]
@@ -426,68 +521,71 @@
     degree = out_degree.reshape(blocks, 1, size)
 
     rows = peers // columns
-    want = lax.all_to_all(
-        slot_block.reshape(rows, columns * cap), "row", split_axis=0, concat_axis=0, tiled=True
-    )
-    good = pl.pallas_call(
-        functools.partial(count_seeds, columns),
-        out_shape=shape(vector, F32),
-        in_specs=[VM],
-        out_specs=VM,
-    )(good_seeds)
+    part = seeds // HALVES
+    good, spam_list = pl.pallas_call(
+        functools.partial(start_kernel, columns),
+        out_shape=(shape(vector, F32), shape(spam_cores.shape, jnp.int32)),
+        in_specs=[VM, VM],
+        out_specs=(VM, VM),
+    )(good_seeds, spam_cores.T)
 
     tile_spec = pl.BlockSpec((tile_count // steps, size, size), lambda i: (i, 0, 0))
     words = shape((peers, cap * size + tail, size), jnp.int16)
     outgoing = pl.pallas_call(
-        functools.partial(push_kernel, True, cap),
+        functools.partial(push_kernel, True, cap, part),
         grid=(steps,),
         out_shape=words,
-        in_specs=[SM, SM, VM, VM, tile_spec],
+        in_specs=[SM, SM, SM, VM, VM, tile_spec],
         out_specs=VM,
         scratch_shapes=[
             pltpu.VMEM((slots, seeds + 16, size), F32),
             pltpu.VMEM((blocks, seeds + 16, size), BF16),
         ],
-    )(tile_src, tile_slot, good, degree, tiles)
+    )(tile_src, tile_slot, slot_block, good, degree, tiles)
+
     def reduce(first, words_in, *rest):
-        long = blocks * seeds + blocks * (4 if first else 1)
-        outs = (shape(vector, F32), shape((blocks, 1, size), F32), shape(vector, F32))
+        long = blocks * part + blocks * (4 if first else 1)
+        dma = pltpu.SemaphoreType.DMA
+        outs = (
+            shape(vector, F32), shape((blocks, size), F32), shape(vector, F32),
+            shape((rows, 1, slots), jnp.int32),
+        )
         return pl.pallas_call(
             functools.partial(reduce_kernel, first, rows, columns, cap),
             out_shape=outs if first else outs[:1],
-            in_specs=[SM, VM, VM] if first else [SM, VM],
-            out_specs=(VM, VM, VM) if first else (VM,),
+            in_specs=[ANY, VM, VM] if first else [ANY],
+            out_specs=(VM,) * 4 if first else (VM,),
             scratch_shapes=[
                 pltpu.VMEM((columns, rows, cap * size + tail, size), jnp.int16),
                 pltpu.VMEM((rows * cap, blocks, size), F32),
-                pltpu.VMEM(vector, F32),
+                pltpu.VMEM((blocks, part, size), F32),
                 pltpu.VMEM((blocks, size), F32),
-                pltpu.VMEM((columns - 1, blocks, size), F32),
-                pltpu.VMEM((columns - 1, long, size), jnp.int16),
-                pltpu.VMEM((columns - 1, long, size), jnp.int16),
-                pltpu.SemaphoreType.DMA((columns,)),
-                pltpu.SemaphoreType.DMA((columns, rows)),
-                pltpu.SemaphoreType.DMA((columns, rows)),
-                pltpu.SemaphoreType.DMA((columns - 1,)),
-                pltpu.SemaphoreType.DMA((columns - 1,)),
+                pltpu.VMEM((columns - 1, HALVES, long, size), jnp.int16),
+                pltpu.VMEM((2, columns, HALVES, long, size), jnp.int16),
+                dma((columns,)),
+                dma((columns, HALVES, rows)),
+                dma((columns, HALVES, rows)),
+                dma((columns - 1, HALVES)),
+                dma((2, columns, HALVES)),
+                *([dma((rows,)), dma((rows,))] if first else []),
             ],
             compiler_params=pltpu.CompilerParams(
                 collective_id=1 if first else 2, has_side_effects=True
             ),
-        )(want, words_in, *rest)
-
-    inflow, weight, spam = reduce(True, outgoing, spam_cores)
+        )(words_in, *rest)
+
+    inflow, weight, spam, want = reduce(True, outgoing, spam_list, slot_block.reshape(1, slots))
     outgoing = pl.pallas_call(
-        functools.partial(push_kernel, False, cap),
+        functools.partial(push_kernel, False, cap, part),
         grid=(steps,),
         out_shape=words,
-        in_specs=[SM, SM, VM, VM, VM, tile_spec],
+        in_specs=[SM, SM, SM, VM, VM, VM, tile_spec],
         out_specs=VM,
         scratch_shapes=[
             pltpu.VMEM((slots, seeds, size), F32),
             pltpu.VMEM(vector, BF16),
         ],
-    )(tile_src, tile_slot, inflow, good, degree, tiles)
+    )(tile_src, tile_slot, slot_block, inflow, good, degree, tiles)
     (inflow,) = reduce(False, outgoing)
     fetch = pl.pallas_call(
         functools.partial(fetch_kernel, rows, columns, cap),

time: 337 us -> 328 us (0.973)
  starting transfers between devices: 5.21 us -> 0 us
  local copies, waits for them, and re-layouts: 3.41 us -> 0 us
    pallas_call x2, Pallas kernels: 143 us -> 135 us  [reduce(): pl.pallas_call(functools.partial(reduce_kernel, first, rows, columns, cap...]
    pallas_call x2, Pallas kernels: 111 us -> 119 us  [body(): fetched = fetch(want, share)]
    all_to_all x1 -> x0, starting transfers between devices: 5.21 us -> none  [body(): lax.all_to_all(slot_block.reshape(rows, columns * cap), 'row', split_axis...]
  transfers between devices with their start and end apart: 1 -> 0, of which waited for: 0 -> 0; matrix products, arithmetic and copies ran while one was open for 0% -> 0% of each run, Pallas kernels for 7% -> 0%
where the time goes in v1:
time: 328 us; the launch traced here: 327 us
  Pallas kernels  326 us (99%)
    pallas_call x2, Pallas kernels, reduce(): pl.pallas_call(functools.partial(reduce_kernel, first, rows, columns, cap...  135 us
    pallas_call x2, Pallas kernels, body(): fetched = fetch(want, share)  119 us
    pallas_call x1, Pallas kernels, body(): pl.pallas_call(functools.partial(push_kernel, True, cap, part), grid=(ste...  16.5 us
    pallas_call x1, Pallas kernels, body(): pl.pallas_call(functools.partial(push_kernel, False, cap, part), grid=(st...  15.1 us
    pallas_call x1, Pallas kernels, body(): pl.pallas_call(functools.partial(pull_kernel, True), grid=(steps,), out_s...  14.4 us
    pallas_call x1, Pallas kernels, body(): pl.pallas_call(functools.partial(pull_kernel, False), grid=(steps,), out_...  13.1 us
    pallas_call x1, Pallas kernels, body(): pl.pallas_call(functools.partial(start_kernel, columns), out_shape=(shape...  8.52 us

profile of v1, /device:TPU:1, one launch (start us, length us, event | category | flops | bytes accessed | tf_op | source)
XLA Modules:
  0.0 327.1 jit_solution(13875806298455414341)
XLA Ops:
  0.6 8.5 %shard_map.86 = (f32[16,128,128]{2,1,0:T(8,128)}, s32[128,64]{1,0:T(8,128)}) custom-call(s32[128,128]{1,0:T(8,128)} %good_ref.1, s32[64,128]{1,0:T(8,128)} %bitcast.3), custom_call_target="tpu_custom_call" | custom-call | tf_op jit(solution)/shard_map/pallas_call | solution.py:525
  9.1 16.5 %shard_map.87.words_ref = s16[32,528,128]{2,1,0:T(8,128)(2,1)} custom-call(s32[256]{0:T(256)} %refs_0_.7, s32[256]{0:T(256)} %refs_1_.7, s32[128]{0:T(128)} %refs_2_.3, f32[16,128,128]{2,1,0:T(8,128)} %get-tuple-element.11.refs_3_.refs_4_.good_ref, s32[16,1,128]{2,1,0:T(1,128)} %bitcast.4, bf16[256,128,128]{2,1,0:T(8,128)(2,1)} %refs_4_.1), custom_call_target="tpu_custom_call" | custom-call | tf_op jit(solution)/shard_map/pallas_call | solution.py:534
  25.7 66.0 %shard_map.88 = (f32[16,128,128]{2,1,0:T(8,128)}, f32[16,128]{1,0:T(8,128)}, f32[16,128,128]{2,1,0:T(8,128)}, s32[8,1,128]{2,1,0:T(1,128)}) custom-call(s16[32,528,128]{2,1,0:T(8,128)(2,1)} %shard_map.87.words_ref, s32[128,64]{1,0:T(8,128)} %get-tuple-element.12.refs_0_, s32[1,128]{1,0:T(1,128)} %bitcast.6), custom_call_target="tpu_custom_call" | custom-call | tf_op jit(solution)/shard_map/pallas_call | solution.py:553
  91.7 15.1 %shard_map.89.words_ref = s16[32,528,128]{2,1,0:T(8,128)(2,1)} custom-call(s32[256]{0:T(256)} %refs_0_.7, s32[256]{0:T(256)} %refs_1_.7, s32[128]{0:T(128)} %refs_2_.3, f32[16,128,128]{2,1,0:T(8,128)} %get-tuple-element.13.refs_3_, f32[16,128,128]{2,1,0:T(8,128)} %get-tuple-element.11.refs_3_.refs_4_.good_ref, s32[16,1,128]{2,1,0:T(1,128)} %bitcast.5, ...), custom_call_target="tpu_custom_call" | custom-call | tf_op jit(solution)/shard_map/pallas_call | solution.py:578
  106.8 68.6 %shard_map.90.inflow = f32[16,128,128]{2,1,0:T(8,128)} custom-call(s16[32,528,128]{2,1,0:T(8,128)(2,1)} %shard_map.89.words_ref), custom_call_target="tpu_custom_call" | custom-call | tf_op jit(solution)/shard_map/pallas_call | solution.py:553
  175.4 5.3 %shard_map.91 = (f32[2048,128]{1,0:T(8,128)}, f32[16,128,128]{2,1,0:T(8,128)}, bf16[16,128,128]{2,1,0:T(8,128)(2,1)}) custom-call(f32[16,128,128]{2,1,0:T(8,128)} %shard_map.90.inflow, f32[16,128,128]{2,1,0:T(8,128)} %get-tuple-element.11.refs_3_.refs_4_.good_ref, f32[16,128,128]{2,1,0:T(8,128)} %get-tuple-element.14.spam_ref.refs_3_, ...), custom_call_target="tpu_custom_call" | custom-call | tf_op jit(solution)/shard_map/pallas_call | solution.py:605
  180.7 63.6 %shard_map.92.refs_2_ = bf16[128,128,128]{2,1,0:T(8,128)(2,1)} custom-call(s32[8,1,128]{2,1,0:T(1,128)} %get-tuple-element.17.want_ref, bf16[16,128,128]{2,1,0:T(8,128)(2,1)} %get-tuple-element.18.share_ref), custom_call_target="tpu_custom_call" | custom-call | tf_op jit(solution)/shard_map/pallas_call | solution.py:611
  244.3 13.1 %shard_map.93.share_ref = bf16[16,128,128]{2,1,0:T(8,128)(2,1)} custom-call(s32[256]{0:T(256)} %refs_0_.7, s32[256]{0:T(256)} %refs_1_.7, bf16[128,128,128]{2,1,0:T(8,128)(2,1)} %shard_map.92.refs_2_, f32[16,128,128]{2,1,0:T(8,128)} %get-tuple-element.14.spam_ref.refs_3_, f32[16,128,128]{2,1,0:T(8,128)} %get-tuple-element.19.refs_4_, ...), custom_call_target="tpu_custom_call" | custom-call | tf_op jit(solution)/shard_map/pallas_call | solution.py:612
  257.4 55.3 %shard_map.94.refs_2_ = bf16[128,128,128]{2,1,0:T(8,128)(2,1)} custom-call(s32[8,1,128]{2,1,0:T(1,128)} %get-tuple-element.17.want_ref, bf16[16,128,128]{2,1,0:T(8,128)(2,1)} %shard_map.93.share_ref), custom_call_target="tpu_custom_call" | custom-call | tf_op jit(solution)/shard_map/pallas_call | solution.py:620
  312.8 14.4 %shard_map.95 = f32[2048,128]{1,0:T(8,128)} custom-call(s32[256]{0:T(256)} %refs_0_.7, s32[256]{0:T(256)} %refs_1_.7, bf16[128,128,128]{2,1,0:T(8,128)(2,1)} %shard_map.94.refs_2_, f32[16,128,128]{2,1,0:T(8,128)} %get-tuple-element.14.spam_ref.refs_3_, bf16[256,128,128]{2,1,0:T(8,128)(2,1)} %refs_4_.1), custom_call_target="tpu_custom_call" | custom-call | tf_op jit(solution)/shard_map/pallas_call | solution.py:621

commit v2 on v1

--- a/solution.py
+++ b/solution.py
@@ -10,9 +10,11 @@
 AXES = ("row", "col")
 VM = pl.BlockSpec(memory_space=pltpu.VMEM)
 SM = pl.BlockSpec(memory_space=pltpu.SMEM)
+LIMIT = 28 << 20
 ANY = pl.BlockSpec(memory_space=pl.ANY)
 F32 = jnp.float32
 BF16 = jnp.bfloat16
+PLAIN = pltpu.CompilerParams(vmem_limit_bytes=LIMIT)
 WORD = 15
 GROUP = 16
 HALVES = 2
@@ -527,6 +529,7 @@
         out_shape=(shape(vector, F32), shape(spam_cores.shape, jnp.int32)),
         in_specs=[VM, VM],
         out_specs=(VM, VM),
+        compiler_params=PLAIN,
     )(good_seeds, spam_cores.T)
 
     tile_spec = pl.BlockSpec((tile_count // steps, size, size), lambda i: (i, 0, 0))
@@ -541,6 +544,7 @@
             pltpu.VMEM((slots, seeds + 16, size), F32),
             pltpu.VMEM((blocks, seeds + 16, size), BF16),
         ],
+        compiler_params=PLAIN,
     )(tile_src, tile_slot, slot_block, good, degree, tiles)
 
     def reduce(first, words_in, *rest):
@@ -570,7 +574,8 @@
                 *([dma((rows,)), dma((rows,))] if first else []),
             ],
             compiler_params=pltpu.CompilerParams(
-                collective_id=1 if first else 2, has_side_effects=True
+                collective_id=1 if first else 2, has_side_effects=True,
+                vmem_limit_bytes=LIMIT,
             ),
         )(words_in, *rest)
 
@@ -585,6 +590,7 @@
             pltpu.VMEM((slots, seeds, size), F32),
             pltpu.VMEM(vector, BF16),
         ],
+        compiler_params=PLAIN,
     )(tile_src, tile_slot, slot_block, inflow, good, degree, tiles)
     (inflow,) = reduce(False, outgoing)
     fetch = pl.pallas_call(
@@ -600,13 +606,14 @@
             pltpu.SemaphoreType.DMA((rows, columns)),
             pltpu.SemaphoreType.DMA((rows, columns)),
         ],
-        compiler_params=pltpu.CompilerParams(collective_id=0, has_side_effects=True),
+        compiler_params=pltpu.CompilerParams(collective_id=0, has_side_effects=True, vmem_limit_bytes=LIMIT),
     )
     trust, shield, share = pl.pallas_call(
         trust_kernel,
         out_shape=(shape((hosts, seeds), F32), shape(vector, F32), shape(vector, BF16)),
         in_specs=[VM, VM, VM, VM],
         out_specs=(VM, VM, VM),
+        compiler_params=PLAIN,
     )(inflow, good, spam, weight)
     fetched = fetch(want, share)
     share = pl.pallas_call(
@@ -616,6 +623,7 @@
         in_specs=[SM, SM, VM, VM, VM, VM, tile_spec],
         out_specs=VM,
         scratch_shapes=[pltpu.VMEM(vector, F32)],
+        compiler_params=PLAIN,
     )(tile_src, tile_slot, fetched, spam, shield, weight, tiles)
     fetched = fetch(want, share)
     distrust = pl.pallas_call(
@@ -625,6 +633,7 @@
         in_specs=[SM, SM, VM, VM, tile_spec],
         out_specs=VM,
         scratch_shapes=[pltpu.VMEM(vector, F32)],
+        compiler_params=PLAIN,
     )(tile_src, tile_slot, fetched, spam, tiles)
     return trust, distrust
 

time: 328 us -> 306 us (0.933)
  Pallas kernels: 326 us -> 297 us
  local copies, waits for them, and re-layouts: 0 us -> 7.69 us
    unnamed x0 -> x20, local copies, waits for them, and re-layouts: none -> 7.69 us
    pallas_call x1, Pallas kernels: 15.1 us -> 9.58 us  [body(): pl.pallas_call(functools.partial(push_kernel, False, cap, part), grid=(st...]
    pallas_call x2, Pallas kernels: 119 us -> 114 us  [body(): fetched = fetch(want, share)]
    pallas_call x1, Pallas kernels: 13.1 us -> 9.06 us  [body(): pl.pallas_call(functools.partial(pull_kernel, False), grid=(steps,), out_...]
    pallas_call x1, Pallas kernels: 16.5 us -> 12.6 us  [body(): pl.pallas_call(functools.partial(push_kernel, True, cap, part), grid=(ste...]
where the time goes in v2:
time: 306 us
  Pallas kernels  297 us (97%)
  local copies, waits for them, and re-layouts  7.69 us (3%)
    pallas_call x2, Pallas kernels, reduce(): pl.pallas_call(functools.partial(reduce_kernel, first, rows, columns, cap...  131 us
    pallas_call x2, Pallas kernels, body(): fetched = fetch(want, share)  114 us
    pallas_call x1, Pallas kernels, body(): pl.pallas_call(functools.partial(push_kernel, True, cap, part), grid=(ste...  12.6 us
    pallas_call x1, Pallas kernels, body(): pl.pallas_call(functools.partial(pull_kernel, True), grid=(steps,), out_s...  11.4 us
    pallas_call x1, Pallas kernels, body(): pl.pallas_call(functools.partial(push_kernel, False, cap, part), grid=(st...  9.58 us
    pallas_call x1, Pallas kernels, body(): pl.pallas_call(functools.partial(pull_kernel, False), grid=(steps,), out_...  9.06 us
    unnamed x20, local copies, waits for them, and re-layouts  7.69 us
    pallas_call x1, Pallas kernels, body(): pl.pallas_call(functools.partial(start_kernel, columns), out_shape=(shape...  6.7 us

profile of v2, /device:TPU:1, one launch (start us, length us, event | category | flops | bytes accessed | tf_op | source)
XLA Modules:
  0.0 305.9 jit_solution(607317019015582261)
XLA Ops:
  0.6 0.0 copy-start.2
  0.6 0.8 copy-done.2
  1.5 0.0 copy-start.3
  1.5 0.8 copy-done.3
  2.2 6.7 %shard_map.86 = (f32[16,128,128]{2,1,0:T(8,128)S(1)}, s32[128,64]{1,0:T(8,128)S(1)}) custom-call(s32[128,128]{1,0:T(8,128)S(1)} %copy-done.2, s32[64,128]{1,0:T(8,128)S(1)} %bitcast.3), custom_call_target="tpu_custom_call" | custom-call | tf_op jit(solution)/shard_map/pallas_call | solution.py:527
  8.9 0.0 copy-start
  8.9 3.4 %copy-done = bf16[256,128,128]{2,1,0:T(8,128)(2,1)S(1)} copy-done((bf16[256,128,128]{2,1,0:T(8,128)(2,1)S(1)}, bf16[256,128,128]{2,1,0:T(8,128)(2,1)}, u32[]{:S(2)}) %copy-start) | copy-done | bytes 8388632
  12.3 0.0 copy-start.4
  12.3 0.7 copy-done.4
  13.0 0.0 copy-start.5
  13.0 0.7 copy-done.5
  13.7 0.0 copy-start.7
  13.7 0.7 copy-done.7
  14.4 0.0 copy-start.9
  14.4 0.7 copy-done.9
  15.0 0.0 copy-start.1
  15.0 12.6 %shard_map.87.words_ref = s16[32,528,128]{2,1,0:T(8,128)(2,1)S(1)} custom-call(s32[256]{0:T(256)S(1)} %copy-done.5, s32[256]{0:T(256)S(1)} %copy-done.7, s32[128]{0:T(128)S(1)} %copy-done.9, f32[16,128,128]{2,1,0:T(8,128)S(1)} %get-tuple-element.11.refs_3_.refs_4_.good_ref, s32[16,1,128]{2,1,0:T(1,128)S(1)} %bitcast.4, bf16[256,128,128]{2,1,0:T(8,128)(2,1)S(1)} %copy-done), custom_call_target="tpu_custom_call" | custom-call | tf_op jit(solution)/shard_map/pallas_call | solution.py:537
  27.6 63.9 %shard_map.88 = (f32[16,128,128]{2,1,0:T(8,128)S(1)}, f32[16,128]{1,0:T(8,128)S(1)}, f32[16,128,128]{2,1,0:T(8,128)S(1)}, s32[8,1,128]{2,1,0:T(1,128)S(1)}) custom-call(s16[32,528,128]{2,1,0:T(8,128)(2,1)S(1)} %shard_map.87.words_ref, s32[128,64]{1,0:T(8,128)S(1)} %get-tuple-element.12.refs_0_, s32[1,128]{1,0:T(1,128)S(1)} %bitcast.6), custom_call_target="tpu_custom_call" | custom-call | tf_op jit(solution)/shard_map/pallas_call | solution.py:557
  91.5 0.0 copy-done.1
  91.5 9.6 %shard_map.89.words_ref = s16[32,528,128]{2,1,0:T(8,128)(2,1)S(1)} custom-call(s32[256]{0:T(256)S(1)} %copy-done.5, s32[256]{0:T(256)S(1)} %copy-done.7, s32[128]{0:T(128)S(1)} %copy-done.9, f32[16,128,128]{2,1,0:T(8,128)S(1)} %get-tuple-element.13.refs_3_, f32[16,128,128]{2,1,0:T(8,128)S(1)} %get-tuple-element.11.refs_3_.refs_4_.good_ref, ...), custom_call_target="tpu_custom_call" | custom-call | tf_op jit(solution)/shard_map/pallas_call | solution.py:583
  101.1 67.5 %shard_map.90.inflow = f32[16,128,128]{2,1,0:T(8,128)S(1)} custom-call(s16[32,528,128]{2,1,0:T(8,128)(2,1)S(1)} %shard_map.89.words_ref), custom_call_target="tpu_custom_call" | custom-call | tf_op jit(solution)/shard_map/pallas_call | solution.py:557
  168.5 0.0 copy-start.6
  168.5 0.0 copy-start.8
  168.6 2.8 shard_map.91
  171.4 61.2 %shard_map.92.refs_2_ = bf16[128,128,128]{2,1,0:T(8,128)(2,1)S(1)} custom-call(s32[8,1,128]{2,1,0:T(1,128)S(1)} %get-tuple-element.17.want_ref, bf16[16,128,128]{2,1,0:T(8,128)(2,1)S(1)} %get-tuple-element.18.share_ref), custom_call_target="tpu_custom_call" | custom-call | tf_op jit(solution)/shard_map/pallas_call | solution.py:618
  232.5 0.0 copy-done.6
  232.6 0.0 copy-done.8
  232.6 9.1 %shard_map.93.share_ref = bf16[16,128,128]{2,1,0:T(8,128)(2,1)S(1)} custom-call(s32[256]{0:T(256)S(1)} %copy-done.6, s32[256]{0:T(256)S(1)} %copy-done.8, bf16[128,128,128]{2,1,0:T(8,128)(2,1)S(1)} %shard_map.92.refs_2_, f32[16,128,128]{2,1,0:T(8,128)S(1)} %get-tuple-element.14.spam_ref.refs_3_, f32[16,128,128]{2,1,0:T(8,128)S(1)} %get-tuple-element.19.refs_4_, ...), custom_call_target="tpu_custom_call" | custom-call | tf_op jit(solution)/shard_map/pallas_call | solution.py:619
  241.6 52.9 %shard_map.94.refs_2_ = bf16[128,128,128]{2,1,0:T(8,128)(2,1)S(1)} custom-call(s32[8,1,128]{2,1,0:T(1,128)S(1)} %get-tuple-element.17.want_ref, bf16[16,128,128]{2,1,0:T(8,128)(2,1)S(1)} %shard_map.93.share_ref), custom_call_target="tpu_custom_call" | custom-call | tf_op jit(solution)/shard_map/pallas_call | solution.py:628
  294.5 11.4 %shard_map.95 = f32[2048,128]{1,0:T(8,128)} custom-call(s32[256]{0:T(256)S(1)} %copy-done.6, s32[256]{0:T(256)S(1)} %copy-done.8, bf16[128,128,128]{2,1,0:T(8,128)(2,1)S(1)} %shard_map.94.refs_2_, f32[16,128,128]{2,1,0:T(8,128)S(1)} %get-tuple-element.14.spam_ref.refs_3_, bf16[256,128,128]{2,1,0:T(8,128)(2,1)S(1)} %copy-done.1), custom_call_target="tpu_custom_call" | custom-call | tf_op jit(solution)/shard_map/pallas_call | solution.py:629
Async XLA Ops:
  0.6 0.8 copy-start.2
  1.5 0.8 copy-start.3
  8.9 3.4 %copy-start = (bf16[256,128,128]{2,1,0:T(8,128)(2,1)S(1)}, bf16[256,128,128]{2,1,0:T(8,128)(2,1)}, u32[]{:S(2)}) copy-start(bf16[256,128,128]{2,1,0:T(8,128)(2,1)} %refs_4_.1) | copy-start | bytes 25165828
  12.3 0.7 copy-start.4
  13.0 0.7 copy-start.5
  13.7 0.7 copy-start.7
  14.4 0.7 copy-start.9
  15.0 76.4 %copy-start.1 = (bf16[256,128,128]{2,1,0:T(8,128)(2,1)S(1)}, bf16[256,128,128]{2,1,0:T(8,128)(2,1)}, u32[]{:S(2)}) copy-start(bf16[256,128,128]{2,1,0:T(8,128)(2,1)} %refs_4_.1) | copy-start | bytes 25165828
  168.5 64.0 %copy-start.6 = (s32[256]{0:T(256)S(1)}, s32[256]{0:T(256)}, u32[]{:S(2)}) copy-start(s32[256]{0:T(256)} %refs_0_.7) | copy-start | bytes 3076
  168.5 64.0 %copy-start.8 = (s32[256]{0:T(256)S(1)}, s32[256]{0:T(256)}, u32[]{:S(2)}) copy-start(s32[256]{0:T(256)} %refs_1_.7) | copy-start | bytes 3076

commit v3 on v2

--- a/solution.py
+++ b/solution.py
@@ -17,16 +17,15 @@
 PLAIN = pltpu.CompilerParams(vmem_limit_bytes=LIMIT)
 WORD = 15
 GROUP = 16
-HALVES = 2
+HALVES = 4
 MESH = pl.DeviceIdType.MESH
 
 
-def count_seeds(columns, source, target, step=0, pieces=1):
-    blocks, seeds, size = target.shape
+def count_seeds(columns, source, tally, step=0, pieces=1):
+    seeds, blocks, size = tally.shape
     hosts = blocks * size
     base = (lax.axis_index("row") * columns + lax.axis_index("col")) * hosts
     count = source.shape[1]
-    factor = F32(hosts / count)
     block_iota = lax.broadcasted_iota(jnp.int32, (blocks, count), 0) * size
     lane_iota = lax.broadcasted_iota(jnp.int32, (size, count), 0)
 
@@ -36,15 +35,20 @@
         inside = jnp.where((shifted >= 0) & (shifted < size), F32(1), F32(0)).astype(BF16)
         start = jnp.max(jnp.where(local >= block_iota, block_iota, 0), axis=0, keepdims=True)
         lane = jnp.where(lane_iota == local - start, F32(1), F32(0)).astype(BF16)
-        counts = lax.dot_general(
+        tally[s] = lax.dot_general(
             inside, lane, (((1,), (1,)), ((), ())), preferred_element_type=F32
         )
-        for b in range(blocks):
-            target[b, pl.ds(s, 1), :] = counts[b : b + 1, :] * factor
         return 0
 
     share = seeds // pieces
-    lax.fori_loop(step * share, (step + 1) * share, one, 0, unroll=4)
+    lax.fori_loop(step * share, (step + 1) * share, one, 0, unroll=16)
+
+
+def spread_seeds(count, tally, target):
+    blocks, _, size = target.shape
+    factor = F32(blocks * size / count)
+    for b in range(blocks):
+        target[b] = tally[:, b, :] * factor
 
 
 def exponent_of(peak):
@@ -299,7 +303,7 @@
         return value.astype(jnp.int32).astype(F32)
 
     if first:
-        known_send, known_recv = refs
+        known_send, known_recv, tally = refs
 
         def know(t, origin):
             return pltpu.make_async_remote_copy(
@@ -431,7 +435,9 @@
                     colsum[...] += F32(1)
             step = i * halves + h
             if first and step < pieces:
-                count_seeds(columns, cores_ref, spam_ref, step, pieces)
+                count_seeds(columns, cores_ref, tally, step, pieces)
+            if first and step == pieces:
+                spread_seeds(cores_ref.shape[1], tally, spam_ref)
 
     if first:
         for t in others:
@@ -503,13 +509,15 @@
             shares(shield_ref, weight_ref, distrust, out_ref)
 
 
-def start_kernel(columns, good_ref, spam_ref, count_ref, list_ref):
+def start_kernel(columns, good_ref, spam_ref, count_ref, list_ref, tally):
     list_ref[...] = jnp.transpose(spam_ref[...].astype(F32)).astype(jnp.int32)
-    count_seeds(columns, good_ref, count_ref)
+    count_seeds(columns, good_ref, tally)
+    spread_seeds(good_ref.shape[1], tally, count_ref)
 
 
 def body(columns, tiles, tile_src, tile_slot, slot_block, out_degree, good_seeds, spam_cores):
     tile_count, size, _ = tiles.shape
+    here = lambda x: pltpu.with_memory_space_constraint(x, pltpu.HBM)
     hosts = out_degree.shape[0]
     blocks = hosts // size
     seeds = good_seeds.shape[0]
@@ -529,8 +537,13 @@
         out_shape=(shape(vector, F32), shape(spam_cores.shape, jnp.int32)),
         in_specs=[VM, VM],
         out_specs=(VM, VM),
+        scratch_shapes=[pltpu.VMEM((seeds, blocks, size), F32)],
         compiler_params=PLAIN,
-    )(good_seeds, spam_cores.T)
+        cost_estimate=pl.CostEstimate(
+            flops=2 * seeds * good_seeds.size * (blocks + size), transcendentals=0,
+            bytes_accessed=24 << 20,
+        ),
+    )(here(good_seeds), here(spam_cores.T))
 
     tile_spec = pl.BlockSpec((tile_count // steps, size, size), lambda i: (i, 0, 0))
     words = shape((peers, cap * size + tail, size), jnp.int16)
@@ -545,7 +558,7 @@
             pltpu.VMEM((blocks, seeds + 16, size), BF16),
         ],
         compiler_params=PLAIN,
-    )(tile_src, tile_slot, slot_block, good, degree, tiles)
+    )(here(tile_src), here(tile_slot), here(slot_block), good, here(degree), here(tiles))
 
     def reduce(first, words_in, *rest):
         long = blocks * part + blocks * (4 if first else 1)
@@ -571,7 +584,7 @@
                 dma((columns, HALVES, rows)),
                 dma((columns - 1, HALVES)),
                 dma((2, columns, HALVES)),
-                *([dma((rows,)), dma((rows,))] if first else []),
+                *([dma((rows,)), dma((rows,)), pltpu.VMEM((seeds, blocks, size), F32)] if first else []),
             ],
             compiler_params=pltpu.CompilerParams(
                 collective_id=1 if first else 2, has_side_effects=True,

time: 306 us -> 284 us (0.928)
  Pallas kernels: 297 us -> 283 us
  local copies, waits for them, and re-layouts: 7.69 us -> 0.04 us
    pallas_call x2, Pallas kernels: 131 us -> 116 us  [reduce(): pl.pallas_call(functools.partial(reduce_kernel, first, rows, columns, cap...]
    unnamed x20 -> x12, local copies, waits for them, and re-layouts: 7.69 us -> 0.04 us
where the time goes in v3:
time: 284 us; the launch traced here: 283 us
  Pallas kernels  283 us (100%)
    pallas_call x2, Pallas kernels, reduce(): pl.pallas_call(functools.partial(reduce_kernel, first, rows, columns, cap...  116 us
    pallas_call x2, Pallas kernels, body(): fetched = fetch(want, share)  114 us
    pallas_call x1, Pallas kernels, body(): pl.pallas_call(functools.partial(push_kernel, True, cap, part), grid=(ste...  14.3 us
    pallas_call x1, Pallas kernels, body(): pl.pallas_call(functools.partial(pull_kernel, True), grid=(steps,), out_s...  11.4 us
    pallas_call x1, Pallas kernels, body(): pl.pallas_call(functools.partial(push_kernel, False, cap, part), grid=(st...  9.66 us
    pallas_call x1, Pallas kernels, body(): pl.pallas_call(functools.partial(pull_kernel, False), grid=(steps,), out_...  9.05 us

profile of v3, /device:TPU:1, one launch (start us, length us, event | category | flops | bytes accessed | tf_op | source)
XLA Modules:
  0.0 283.4 jit_solution(393652724603329119)
XLA Ops:
  0.6 5.0 %shard_map.86 = (f32[16,128,128]{2,1,0:T(8,128)S(1)}, s32[128,64]{1,0:T(8,128)S(1)}) custom-call(s32[128,128]{1,0:T(8,128)} %good_ref.1, s32[64,128]{1,0:T(8,128)} %bitcast.8), custom_call_target="tpu_custom_call" | custom-call | flops 603979776 | bytes 25165824 | tf_op jit(solution)/shard_map/pallas_call | solution.py:535
  5.6 0.0 slice-start
  5.6 0.0 copy-start.3
  5.6 0.0 slice-start.1
  5.6 14.3 %shard_map.87.words_ref = s16[32,528,128]{2,1,0:T(8,128)(2,1)S(1)} custom-call(s32[256]{0:T(256)} %refs_0_.7, s32[256]{0:T(256)} %refs_1_.7, s32[128]{0:T(128)} %refs_2_.3, f32[16,128,128]{2,1,0:T(8,128)S(1)} %get-tuple-element.11.refs_3_.refs_4_.good_ref, s32[16,1,128]{2,1,0:T(1,128)} %bitcast.5, bf16[256,128,128]{2,1,0:T(8,128)(2,1)} %refs_4_.1), custom_call_target="tpu_custom_call" | custom-call | tf_op jit(solution)/shard_map/pallas_call | solution.py:550
  20.0 0.0 copy-done.3
  20.0 0.0 copy-start
  20.0 0.0 copy-start.1
  20.0 0.0 copy-start.2
  20.0 55.8 %shard_map.88 = (f32[16,128,128]{2,1,0:T(8,128)S(1)}, f32[16,128]{1,0:T(8,128)S(1)}, f32[16,128,128]{2,1,0:T(8,128)S(1)}, s32[8,1,128]{2,1,0:T(1,128)S(1)}) custom-call(s16[32,528,128]{2,1,0:T(8,128)(2,1)S(1)} %shard_map.87.words_ref, s32[128,64]{1,0:T(8,128)S(1)} %get-tuple-element.12.refs_0_, s32[1,128]{1,0:T(1,128)S(1)} %bitcast.7), custom_call_target="tpu_custom_call" | custom-call | tf_op jit(solution)/shard_map/pallas_call | solution.py:570
  75.8 0.0 slice-done
  75.8 0.0 slice-done.1
  75.8 0.0 copy-done
  75.8 0.0 copy-done.1
  75.8 0.0 copy-done.2
  75.9 9.7 %shard_map.89.words_ref = s16[32,528,128]{2,1,0:T(8,128)(2,1)S(1)} custom-call(s32[256]{0:T(256)S(1)} %copy-done.1, s32[256]{0:T(256)S(1)} %copy-done.2, s32[128]{0:T(128)S(1)} %copy-done.3, f32[16,128,128]{2,1,0:T(8,128)S(1)} %get-tuple-element.13.refs_3_, f32[16,128,128]{2,1,0:T(8,128)S(1)} %get-tuple-element.11.refs_3_.refs_4_.good_ref, ...), custom_call_target="tpu_custom_call" | custom-call | tf_op jit(solution)/shard_map/pallas_call | solution.py:596
  85.5 60.7 %shard_map.90.inflow = f32[16,128,128]{2,1,0:T(8,128)S(1)} custom-call(s16[32,528,128]{2,1,0:T(8,128)(2,1)S(1)} %shard_map.89.words_ref), custom_call_target="tpu_custom_call" | custom-call | tf_op jit(solution)/shard_map/pallas_call | solution.py:570
  146.2 2.8 shard_map.91
  149.0 60.9 %shard_map.92.refs_2_ = bf16[128,128,128]{2,1,0:T(8,128)(2,1)S(1)} custom-call(s32[8,1,128]{2,1,0:T(1,128)S(1)} %get-tuple-element.17.want_ref, bf16[16,128,128]{2,1,0:T(8,128)(2,1)S(1)} %get-tuple-element.18.share_ref), custom_call_target="tpu_custom_call" | custom-call | tf_op jit(solution)/shard_map/pallas_call | solution.py:631
  209.9 9.0 %shard_map.93.share_ref = bf16[16,128,128]{2,1,0:T(8,128)(2,1)S(1)} custom-call(s32[256]{0:T(256)S(1)} %copy-done.1, s32[256]{0:T(256)S(1)} %copy-done.2, bf16[128,128,128]{2,1,0:T(8,128)(2,1)S(1)} %shard_map.92.refs_2_, f32[16,128,128]{2,1,0:T(8,128)S(1)} %get-tuple-element.14.spam_ref.refs_3_, f32[16,128,128]{2,1,0:T(8,128)S(1)} %get-tuple-element.19.refs_4_, ...), custom_call_target="tpu_custom_call" | custom-call | tf_op jit(solution)/shard_map/pallas_call | solution.py:632
  218.9 53.1 %shard_map.94.refs_2_ = bf16[128,128,128]{2,1,0:T(8,128)(2,1)S(1)} custom-call(s32[8,1,128]{2,1,0:T(1,128)S(1)} %get-tuple-element.17.want_ref, bf16[16,128,128]{2,1,0:T(8,128)(2,1)S(1)} %shard_map.93.share_ref), custom_call_target="tpu_custom_call" | custom-call | tf_op jit(solution)/shard_map/pallas_call | solution.py:641
  272.0 11.4 %shard_map.95 = f32[2048,128]{1,0:T(8,128)} custom-call(s32[256]{0:T(256)S(1)} %copy-done.1, s32[256]{0:T(256)S(1)} %copy-done.2, bf16[128,128,128]{2,1,0:T(8,128)(2,1)S(1)} %shard_map.94.refs_2_, f32[16,128,128]{2,1,0:T(8,128)S(1)} %get-tuple-element.14.spam_ref.refs_3_, bf16[256,128,128]{2,1,0:T(8,128)(2,1)S(1)} %bitcast.4), custom_call_target="tpu_custom_call" | custom-call | tf_op jit(solution)/shard_map/pallas_call | solution.py:642
  (1 shorter events, 0.0 us)
Async XLA Ops:
  5.6 70.2 %slice-start = ((s8[8388608]{0:T(1024)(128)(4,1)}), s8[4194304]{0:T(1024)(128)(4,1)S(1)}, s32[]{:S(2)}) async-start(s8[8388608]{0:T(1024)(128)(4,1)} %bitcast.3), calls=%async_computation | async-start | bytes 8388608
  5.6 14.4 %copy-start.3 = (s32[128]{0:T(128)S(1)}, s32[128]{0:T(128)}, u32[]{:S(2)}) copy-start(s32[128]{0:T(128)} %refs_2_.3) | copy-start | bytes 1540
  5.6 70.2 %slice-start.1 = ((s8[8388608]{0:T(1024)(128)(4,1)}), s8[4194304]{0:T(1024)(128)(4,1)S(1)}, s32[]{:S(2)}) async-start(s8[8388608]{0:T(1024)(128)(4,1)} %bitcast.3), calls=%async_computation.1 | async-start | bytes 8388608
  20.0 55.8 %copy-start = (s32[2048]{0:T(1024)S(1)}, s32[2048]{0:T(1024)}, u32[]{:S(2)}) copy-start(s32[2048]{0:T(1024)} %param.11) | copy-start | bytes 24580
  20.0 55.8 %copy-start.1 = (s32[256]{0:T(256)S(1)}, s32[256]{0:T(256)}, u32[]{:S(2)}) copy-start(s32[256]{0:T(256)} %refs_0_.7) | copy-start | bytes 3076
  20.0 55.8 %copy-start.2 = (s32[256]{0:T(256)S(1)}, s32[256]{0:T(256)}, u32[]{:S(2)}) copy-start(s32[256]{0:T(256)} %refs_1_.7) | copy-start | bytes 3076

commit v4 on v3

--- a/solution.py
+++ b/solution.py
@@ -18,6 +18,7 @@
 WORD = 15
 GROUP = 16
 HALVES = 4
+LAYERS = 5
 MESH = pl.DeviceIdType.MESH
 
 
@@ -230,6 +231,246 @@
                 pass_on(share_ref, d + 1, side).wait_send()
 
 
+def take(table, index):
+    return jnp.take_along_axis(table, index, axis=1, mode="promise_in_bounds")
+
+
+def bound_of(code):
+    return LAYERS + 4 * code
+
+
+def find_ranks(groups, blocks, keys):
+    lines, size = keys.shape
+    count = size // groups
+    least = lax.broadcasted_iota(jnp.int32, (lines, size), 1) * blocks
+    spots = [jnp.full((lines, size), count * g, jnp.int32) for g in range(groups)]
+    step = count // 2
+    while True:
+        probes = [take(keys, spot + (max(step, 1) - 1)) for spot in spots]
+        spots = [spot + jnp.where(probe < least, max(step, 1), 0) for spot, probe in zip(spots, probes)]
+        if step == 0:
+            return spots
+        step //= 2
+
+
+def ends_of(g, groups, spots):
+    lines, size = spots.shape
+    lane = lax.broadcasted_iota(jnp.int32, (lines, size), 1)
+    after = pltpu.roll(spots, size - 1, 1)
+    return jnp.where(lane == size - 1, (size // groups) * (g + 1), after)
+
+
+def sort_hosts(columns, blocks, raw):
+    count, seeds = raw.shape
+    groups = seeds // count
+    lines = seeds // groups
+    base = (lax.axis_index("row") * columns + lax.axis_index("col")) * (blocks * seeds)
+    local = (raw - base).astype(F32)
+    stacked = jnp.concatenate(
+        [local] + [pltpu.roll(local, seeds - g * lines, 1) for g in range(1, groups)], axis=0
+    )
+    hosts = jnp.transpose(stacked)[:lines, :].astype(jnp.int32)
+    keys = ((hosts & (seeds - 1)) * blocks + hosts // seeds).astype(F32)
+    lane = lax.broadcasted_iota(jnp.int32, keys.shape, 1)
+    k = 2
+    while k <= count:
+        j = k // 2
+        while j:
+            other = take(keys, lane ^ j)
+            rising = ((lane & k) == 0) | (k == count)
+            lower = ((lane & j) == 0) == rising
+            keys = jnp.where(lower, jnp.minimum(keys, other), jnp.maximum(keys, other))
+            j //= 2
+        k *= 2
+    keys = keys.astype(jnp.int32)
+    spots = find_ranks(groups, blocks, keys)
+    most = functools.reduce(
+        jnp.maximum, [ends_of(g, groups, spot) - spot for g, spot in enumerate(spots)]
+    ).astype(F32)
+    most = jnp.max(jnp.max(most, axis=1, keepdims=True), axis=0, keepdims=True).astype(jnp.int32)
+    code = jnp.maximum(most - LAYERS + 3, 0) >> 2
+    return (keys + code * (blocks * seeds)).astype(jnp.int16)
+
+
+class Spread:
+    def __init__(self, rows, columns, own, out, sems):
+        self.rows, self.columns, self.own, self.out = rows, columns, own, out
+        self.line_send, self.line_recv, self.plane_send, self.plane_recv, self.pair_send, self.pair_recv = sems
+        r, z = lax.axis_index("row"), lax.axis_index("col")
+        self.r, self.z = r, z
+        self.twin = r + 1 - 2 * lax.rem(r, 2)
+        self.mates = [lax.rem(r + d, rows) for d in range(2, rows, 2)]
+        self.others = [self.twin] + [lax.rem(self.twin + d, rows) for d in range(2, rows, 2)]
+        self.inside = {side: (z + side >= 0) & (z + side < columns) for side in (-1, 1)}
+
+    def send(self, source, row, origin, sends, recvs, to):
+        return pltpu.make_async_remote_copy(
+            src_ref=source, dst_ref=self.out.at[row * self.columns + origin],
+            send_sem=sends, recv_sem=recvs, device_id=to, device_id_type=MESH,
+        )
+
+    def place(self, row, origin):
+        return self.out.at[row * self.columns + origin]
+
+    def line(self, source, origin, side):
+        way = 0 if side < 0 else 1
+        return self.send(
+            source, self.r, origin, self.line_send.at[way, origin], self.line_recv.at[origin],
+            (self.r, self.z + side),
+        )
+
+    def plane(self, source, t, row, origin):
+        return self.send(
+            source, row, origin, self.plane_send.at[t, origin], self.plane_recv.at[row, origin],
+            (t, self.z),
+        )
+
+    def pair(self, source, row, origin):
+        return self.send(
+            source, row, origin, self.pair_send.at[row, origin], self.pair_recv.at[row, origin],
+            (self.twin, self.z),
+        )
+
+    def across(self, source, origin):
+        for t in self.mates:
+            self.plane(source, t, self.r, origin).start()
+        self.pair(source, self.r, origin).start()
+
+    def begin(self):
+        for side in (-1, 1):
+            @pl.when(self.inside[side])
+            def _():
+                self.line(self.own, self.z, side).start()
+        self.across(self.own, self.z)
+        self.out[self.r * self.columns + self.z] = self.own[...]
+
+    def each(self, d):
+        for side in (-1, 1):
+            origin = self.z + side * d
+            yield side, origin, (origin >= 0) & (origin < self.columns)
+
+    def hop(self, d):
+        for side, origin, there in self.each(d):
+            @pl.when(there)
+            def _():
+                here = self.place(self.r, origin)
+                self.line(here, origin, side).wait_recv()
+
+                @pl.when(self.inside[-side])
+                def _():
+                    self.line(here, origin, -side).start()
+
+                self.across(here, origin)
+
+    def collect(self):
+        for t in self.mates:
+            for origin in range(self.columns):
+                here = self.place(t, origin)
+                self.plane(here, t, t, origin).wait_recv()
+                self.pair(here, t, origin).start()
+
+    def finish(self):
+        for t in self.others:
+            for origin in range(self.columns):
+                self.pair(self.place(t, origin), t, origin).wait_recv()
+        for side in (-1, 1):
+            @pl.when(self.inside[side])
+            def _():
+                self.line(self.own, self.z, side).wait_send()
+        for d in range(1, self.columns):
+            for side, origin, there in self.each(d):
+                @pl.when(there & self.inside[-side])
+                def _():
+                    self.line(self.own, origin, -side).wait_send()
+        for origin in range(self.columns):
+            for t in self.mates:
+                self.plane(self.own, t, self.r, origin).wait_send()
+                self.pair(self.own, t, origin).wait_send()
+            self.pair(self.own, self.r, origin).wait_send()
+
+
+def value_kernel(rows, columns, groups, blocks, own_ref, lists_ref, vals_ref, rank_ref, *sems):
+    spread = Spread(rows, columns, own_ref, vals_ref, sems)
+    peers, lines, size = lists_ref.shape
+    greet(
+        [((t, spread.z), t >= 0) for t in spread.mates + [spread.twin]]
+        + [((spread.r, spread.z + side), spread.inside[side]) for side in (-1, 1)]
+    )
+
+    def find(q, _):
+        keys = lists_ref[q].astype(jnp.int32) & (blocks * size - 1)
+        for g, spots in enumerate(find_ranks(groups, blocks, keys)):
+            rank_ref[q, g * lines : (g + 1) * lines, :] = spots
+        return 0
+
+    share = peers // (columns + 1)
+    spread.begin()
+    for d in range(1, columns):
+        lax.fori_loop((d - 1) * share, d * share, find, 0, unroll=2)
+        spread.hop(d)
+    lax.fori_loop((columns - 1) * share, columns * share, find, 0, unroll=2)
+    spread.collect()
+    lax.fori_loop(columns * share, peers, find, 0, unroll=2)
+    spread.finish()
+
+
+def expand(cap, block_ref, lists_ref, vals_ref, rank_ref, blocks, bounds, fetched):
+    peers, lines, size = lists_ref.shape
+    groups = fetched.shape[1] // lines
+    tall = 16
+
+    def paint(q, low, high):
+        tags = [
+            F32(1) + (block_ref[q * cap + c] + 1).astype(F32) * F32(2.0**-14) for c in range(cap)
+        ]
+
+        def some(i, _):
+            at = pl.multiple_of(i * tall, tall)
+            block = lists_ref[q, pl.ds(at, tall), :].astype(jnp.int32) & (blocks - 1)
+            value = vals_ref[q, pl.ds(at, tall), :].astype(F32)
+            marked = value * (F32(1) + (block + 1).astype(F32) * F32(2.0**-14))
+            for g in range(groups):
+                row = pl.multiple_of(g * lines + at, tall)
+                spots = rank_ref[q, pl.ds(row, tall), :]
+                ends = ends_of(g, groups, spots)
+
+                def layer(j, outs):
+                    spot = spots + j
+                    live = spot < ends
+                    got = jnp.where(live, take(marked, jnp.minimum(spot, size - 1)), F32(0))
+                    plain = got.astype(BF16).astype(F32)
+                    return tuple(
+                        jnp.where(live & (plain * tag == got), plain, out) for tag, out in zip(tags, outs)
+                    )
+
+                if high is None:
+                    outs = (jnp.zeros((tall, size), F32),) * cap
+                    for j in range(low):
+                        outs = layer(j, outs)
+                else:
+                    outs = tuple(
+                        fetched[q * cap + c, pl.ds(row, tall), :].astype(F32) for c in range(cap)
+                    )
+                    outs = lax.fori_loop(low, high, layer, outs)
+                for c in range(cap):
+                    fetched[q * cap + c, pl.ds(row, tall), :] = outs[c].astype(BF16)
+            return 0
+
+        lax.fori_loop(0, lines // tall, some, 0, unroll=2 if high is None else 1)
+
+    def one(q, _):
+        paint(q, LAYERS, None)
+        code = bounds[q, 0]
+
+        @pl.when(code > 0)
+        def _():
+            paint(q, LAYERS, bound_of(code))
+
+        return 0
+
+    lax.fori_loop(0, peers, one, 0)
+
+
 def order_of(z, columns):
     table = []
     for plane in range(columns):
@@ -251,7 +492,7 @@
 
 def reduce_kernel(first, rows, columns, cap, words_ref, *refs):
     if first:
-        cores_ref, mine_ref, inflow_ref, weight_ref, spam_ref, want_ref, *refs = refs
+        cores_ref, mine_ref, keys_ref, inflow_ref, weight_ref, spam_ref, want_ref, lists_ref, *refs = refs
     else:
         inflow_ref, *refs = refs
     landed, table, partial, exps, packed, inbox, own, send, recv, chain_send, chain_recv, *refs = refs
@@ -303,7 +544,8 @@
         return value.astype(jnp.int32).astype(F32)
 
     if first:
-        known_send, known_recv, tally = refs
+        known_send, known_recv, tally, *sems = refs
+        spread = Spread(rows, columns, keys_ref, lists_ref, sems)
 
         def know(t, origin):
             return pltpu.make_async_remote_copy(
@@ -315,6 +557,7 @@
         for t in others:
             know(t, r).start()
         want_ref[r] = mine_ref[...]
+        spread.begin()
     for i in range(columns):
         for h in range(halves):
             for t in others:
@@ -434,6 +677,8 @@
                 if first and h == 0:
                     colsum[...] += F32(1)
             step = i * halves + h
+            if first and 0 < step < columns:
+                spread.hop(step)
             if first and step < pieces:
                 count_seeds(columns, cores_ref, tally, step, pieces)
             if first and step == pieces:
@@ -443,6 +688,8 @@
         for t in others:
             know(t, r).wait_send()
             know(t, t).wait_recv()
+        spread.collect()
+        spread.finish()
     for i in range(columns):
         for h in range(halves):
             for t in others:
@@ -451,25 +698,36 @@
                 chain(i, h, jnp.where(targets[i] > z, 0, 1)).wait_send()
 
 
-def trust_kernel(inflow, good_ref, spam_ref, weight_ref, trust_ref, shield_ref, share_ref):
-    size = inflow.shape[2]
-
-    def one(b, _):
+def trust_kernel(inflow, good_ref, spam_ref, weight_ref, keys_ref, trust_ref, shield_ref, vals_ref):
+    blocks, seeds, size = inflow.shape
+    lines = keys_ref.shape[0]
+    groups = seeds // lines
+    keys = keys_ref[...].astype(jnp.int32) & (blocks * size - 1)
+    lanes = keys // blocks
+    block = keys & (blocks - 1)
+    part = lax.broadcasted_iota(jnp.int32, (lines, size), 1) // (size // groups)
+
+    def one(b, vals):
         trust = F32(0.85) * inflow[b] + F32(0.15) * good_ref[b]
         trust_ref[pl.ds(pl.multiple_of(b * size, size), size), :] = jnp.transpose(trust)
-        shield_ref[b] = F32(1) / (F32(1) + trust)
-        return 0
-
-    lax.fori_loop(0, inflow.shape[0], one, 0)
-    shares(shield_ref, weight_ref, lambda b: spam_ref[b], share_ref)
+        shield = F32(1) / (F32(1) + trust)
+        shield_ref[b] = shield
+        share = (shield * spam_ref[b] / weight_ref[pl.ds(b, 1), :]).astype(BF16).astype(F32)
+        for g in range(groups):
+            got = take(share[g * lines : (g + 1) * lines, :], lanes)
+            vals = jnp.where((block == b) & (part == g), got, vals)
+        return vals
+
+    vals = lax.fori_loop(0, blocks, one, jnp.zeros((lines, size), F32), unroll=2)
+    vals_ref[...] = vals.astype(BF16)
 
 
 def pull_kernel(last, *refs):
     if last:
         src_ref, slot_ref, fetched_ref, spam_ref, tiles_ref, out_ref, acc = refs
     else:
-        (src_ref, slot_ref, fetched_ref, spam_ref, shield_ref, weight_ref, tiles_ref,
-         out_ref, acc) = refs
+        (src_ref, slot_ref, block_ref, lists_ref, vals_ref, rank_ref, spam_ref, shield_ref, weight_ref,
+         tiles_ref, out_ref, acc, fetched_ref, codes, bounds, sem) = refs
     step = pl.program_id(0)
     per_step = tiles_ref.shape[0]
     size = acc.shape[2]
@@ -477,6 +735,16 @@
     @pl.when(step == 0)
     def _():
         acc[...] = jnp.zeros_like(acc)
+        if not last:
+            blocks = acc.shape[0]
+            codes[...] = lists_ref[:, 0, :].astype(jnp.int32) // (blocks * size)
+            copy = pltpu.make_async_copy(codes, bounds, sem)
+            copy.start()
+            copy.wait()
+            expand(
+                block_ref.shape[0] // lists_ref.shape[0], block_ref, lists_ref, vals_ref, rank_ref,
+                blocks, bounds, fetched_ref,
+            )
 
     def some(g, _):
         products = []
@@ -509,8 +777,10 @@
             shares(shield_ref, weight_ref, distrust, out_ref)
 
 
-def start_kernel(columns, good_ref, spam_ref, count_ref, list_ref, tally):
-    list_ref[...] = jnp.transpose(spam_ref[...].astype(F32)).astype(jnp.int32)
+def start_kernel(columns, good_ref, spam_ref, count_ref, list_ref, keys_ref, tally):
+    raw = spam_ref[...]
+    list_ref[...] = jnp.transpose(raw.astype(F32)).astype(jnp.int32)
+    keys_ref[...] = sort_hosts(columns, count_ref.shape[0], raw)
     count_seeds(columns, good_ref, tally)
     spread_seeds(good_ref.shape[1], tally, count_ref)
 
@@ -532,11 +802,16 @@
 
     rows = peers // columns
     part = seeds // HALVES
-    good, spam_list = pl.pallas_call(
+    count = spam_cores.shape[1]
+    groups = seeds // count
+    lines = seeds // groups
+    good, spam_list, keys = pl.pallas_call(
         functools.partial(start_kernel, columns),
-        out_shape=(shape(vector, F32), shape(spam_cores.shape, jnp.int32)),
+        out_shape=(
+            shape(vector, F32), shape(spam_cores.shape, jnp.int32), shape((lines, size), jnp.int16),
+        ),
         in_specs=[VM, VM],
-        out_specs=(VM, VM),
+        out_specs=(VM, VM, VM),
         scratch_shapes=[pltpu.VMEM((seeds, blocks, size), F32)],
         compiler_params=PLAIN,
         cost_estimate=pl.CostEstimate(
@@ -560,18 +835,23 @@
         compiler_params=PLAIN,
     )(here(tile_src), here(tile_slot), here(slot_block), good, here(degree), here(tiles))
 
+    dma = pltpu.SemaphoreType.DMA
+    spread_sems = [
+        dma((2, columns)), dma((columns,)), dma((rows, columns)), dma((rows, columns)),
+        dma((rows, columns)), dma((rows, columns)),
+    ]
+
     def reduce(first, words_in, *rest):
         long = blocks * part + blocks * (4 if first else 1)
-        dma = pltpu.SemaphoreType.DMA
         outs = (
             shape(vector, F32), shape((blocks, size), F32), shape(vector, F32),
-            shape((rows, 1, slots), jnp.int32),
+            shape((rows, 1, slots), jnp.int32), shape((peers, lines, size), jnp.int16),
         )
         return pl.pallas_call(
             functools.partial(reduce_kernel, first, rows, columns, cap),
             out_shape=outs if first else outs[:1],
-            in_specs=[ANY, VM, VM] if first else [ANY],
-            out_specs=(VM,) * 4 if first else (VM,),
+            in_specs=[ANY, VM, VM, VM] if first else [ANY],
+            out_specs=(VM,) * 5 if first else (VM,),
             scratch_shapes=[
                 pltpu.VMEM((columns, rows, cap * size + tail, size), jnp.int16),
                 pltpu.VMEM((rows * cap, blocks, size), F32),
@@ -584,7 +864,7 @@
                 dma((columns, HALVES, rows)),
                 dma((columns - 1, HALVES)),
                 dma((2, columns, HALVES)),
-                *([dma((rows,)), dma((rows,)), pltpu.VMEM((seeds, blocks, size), F32)] if first else []),
+                *([dma((rows,)), dma((rows,)), pltpu.VMEM((seeds, blocks, size), F32), *spread_sems] if first else []),
             ],
             compiler_params=pltpu.CompilerParams(
                 collective_id=1 if first else 2, has_side_effects=True,
@@ -592,7 +872,9 @@
             ),
         )(words_in, *rest)
 
-    inflow, weight, spam, want = reduce(True, outgoing, spam_list, slot_block.reshape(1, slots))
+    inflow, weight, spam, want, lists = reduce(
+        True, outgoing, spam_list, slot_block.reshape(1, slots), keys
+    )
     outgoing = pl.pallas_call(
         functools.partial(push_kernel, False, cap, part),
         grid=(steps,),
@@ -621,23 +903,38 @@
         ],
         compiler_params=pltpu.CompilerParams(collective_id=0, has_side_effects=True, vmem_limit_bytes=LIMIT),
     )
-    trust, shield, share = pl.pallas_call(
+    trust, shield, vals = pl.pallas_call(
         trust_kernel,
-        out_shape=(shape((hosts, seeds), F32), shape(vector, F32), shape(vector, BF16)),
-        in_specs=[VM, VM, VM, VM],
+        out_shape=(shape((hosts, seeds), F32), shape(vector, F32), shape((lines, size), BF16)),
+        in_specs=[VM, VM, VM, VM, VM],
         out_specs=(VM, VM, VM),
         compiler_params=PLAIN,
-    )(inflow, good, spam, weight)
-    fetched = fetch(want, share)
+    )(inflow, good, spam, weight, keys)
+    vals, ranks = pl.pallas_call(
+        functools.partial(value_kernel, rows, columns, groups, blocks),
+        out_shape=(shape((peers, lines, size), BF16), shape((peers, seeds, size), jnp.int32)),
+        in_specs=[VM, VM],
+        out_specs=(VM, VM),
+        scratch_shapes=spread_sems,
+        compiler_params=pltpu.CompilerParams(
+            collective_id=3, has_side_effects=True, vmem_limit_bytes=LIMIT
+        ),
+    )(vals, lists)
     share = pl.pallas_call(
         functools.partial(pull_kernel, False),
         grid=(steps,),
         out_shape=shape(vector, BF16),
-        in_specs=[SM, SM, VM, VM, VM, VM, tile_spec],
+        in_specs=[SM, SM, SM, VM, VM, VM, VM, VM, VM, tile_spec],
         out_specs=VM,
-        scratch_shapes=[pltpu.VMEM(vector, F32)],
+        scratch_shapes=[
+            pltpu.VMEM(vector, F32),
+            pltpu.VMEM((slots, seeds, size), BF16),
+            pltpu.VMEM((peers, size), jnp.int32),
+            pltpu.SMEM((peers, size), jnp.int32),
+            pltpu.SemaphoreType.DMA,
+        ],
         compiler_params=PLAIN,
-    )(tile_src, tile_slot, fetched, spam, shield, weight, tiles)
+    )(tile_src, tile_slot, slot_block, lists, vals, ranks, spam, shield, weight, tiles)
     fetched = fetch(want, share)
     distrust = pl.pallas_call(
         functools.partial(pull_kernel, True),

time: 284 us -> 288 us (1.014)
  Pallas kernels: 283 us -> 287 us
    pallas_call x2 -> x1, Pallas kernels: 114 us -> 54.2 us  [body(): fetched = fetch(want, share)]
    pallas_call x1, Pallas kernels: 9.05 us -> 40.5 us  [body(): pl.pallas_call(functools.partial(pull_kernel, False), grid=(steps,), out_...]
    pallas_call x0 -> x1, Pallas kernels: none -> 23.7 us  [body(): pl.pallas_call(functools.partial(value_kernel, rows, columns, groups, blo...]
    pallas_call x2, Pallas kernels: 116 us -> 124 us  [reduce(): pl.pallas_call(functools.partial(reduce_kernel, first, rows, columns, cap...]
where the time goes in v4:
time: 288 us
  Pallas kernels  287 us (100%)
    pallas_call x2, Pallas kernels, reduce(): pl.pallas_call(functools.partial(reduce_kernel, first, rows, columns, cap...  124 us
    pallas_call x1, Pallas kernels, body(): fetched = fetch(want, share)  54.2 us
    pallas_call x1, Pallas kernels, body(): pl.pallas_call(functools.partial(pull_kernel, False), grid=(steps,), out_...  40.5 us
    pallas_call x1, Pallas kernels, body(): pl.pallas_call(functools.partial(value_kernel, rows, columns, groups, blo...  23.7 us
    pallas_call x1, Pallas kernels, body(): pl.pallas_call(functools.partial(push_kernel, True, cap, part), grid=(ste...  14.3 us
    pallas_call x1, Pallas kernels, body(): pl.pallas_call(functools.partial(pull_kernel, True), grid=(steps,), out_s...  11.3 us
    pallas_call x1, Pallas kernels, body(): pl.pallas_call(functools.partial(push_kernel, False, cap, part), grid=(st...  9.69 us
    pallas_call x1, Pallas kernels, body(): pl.pallas_call(functools.partial(start_kernel, columns), out_shape=(shape...  7.21 us

profile of v4, /device:TPU:1, one launch (start us, length us, event | category | flops | bytes accessed | tf_op | source)
XLA Modules:
  0.0 287.9 jit_solution(18200384878978264081)
XLA Ops:
  0.6 7.2 %shard_map.86 = (f32[16,128,128]{2,1,0:T(8,128)S(1)}, s32[128,64]{1,0:T(8,128)S(1)}, s16[64,128]{1,0:T(8,128)(2,1)S(1)}) custom-call(s32[128,128]{1,0:T(8,128)} %good_ref.1, s32[64,128]{1,0:T(8,128)} %bitcast.8), custom_call_target="tpu_custom_call" | custom-call | flops 603979776 | bytes 25165824 | tf_op jit(solution)/shard_map/pallas_call | solution.py:808
  7.8 0.0 slice-start
  7.9 0.0 copy-start.3
  7.9 0.0 slice-start.1
  7.9 14.3 %shard_map.87.words_ref = s16[32,528,128]{2,1,0:T(8,128)(2,1)S(1)} custom-call(s32[256]{0:T(256)} %refs_0_.7, s32[256]{0:T(256)} %refs_1_.7, s32[128]{0:T(128)} %refs_2_.5, f32[16,128,128]{2,1,0:T(8,128)S(1)} %get-tuple-element.15.refs_3_.refs_4_.good_ref, s32[16,1,128]{2,1,0:T(1,128)} %bitcast.5, bf16[256,128,128]{2,1,0:T(8,128)(2,1)} %refs_4_.1), custom_call_target="tpu_custom_call" | custom-call | tf_op jit(solution)/shard_map/pallas_call | solution.py:825
  22.2 0.0 copy-done.3
  22.2 0.0 copy-start
  22.2 0.0 copy-start.1
  22.3 0.0 copy-start.2
  22.3 64.1 %shard_map.88 = (f32[16,128,128]{2,1,0:T(8,128)S(1)}, f32[16,128]{1,0:T(8,128)S(1)}, f32[16,128,128]{2,1,0:T(8,128)S(1)}, s32[8,1,128]{2,1,0:T(1,128)S(1)}, s16[32,64,128]{2,1,0:T(8,128)(2,1)S(1)}) custom-call(s16[32,528,128]{2,1,0:T(8,128)(2,1)S(1)} %shard_map.87.words_ref, s32[128,64]{1,0:T(8,128)S(1)} %get-tuple-element.16.refs_0_, s32[1,128]{1,0:T(1,128)S(1)} %bitcast.7, ...), custom_call_target="tpu_custom_call" | custom-call | tf_op jit(solution)/shard_map/pallas_call | solution.py:850
  86.4 0.0 slice-done
  86.4 0.0 slice-done.1
  86.4 0.0 copy-done
  86.4 0.0 copy-done.1
  86.4 0.0 copy-done.2
  86.4 9.7 %shard_map.89.words_ref = s16[32,528,128]{2,1,0:T(8,128)(2,1)S(1)} custom-call(s32[256]{0:T(256)S(1)} %copy-done.1, s32[256]{0:T(256)S(1)} %copy-done.2, s32[128]{0:T(128)S(1)} %copy-done.3, f32[16,128,128]{2,1,0:T(8,128)S(1)} %get-tuple-element.18.refs_3_, f32[16,128,128]{2,1,0:T(8,128)S(1)} %get-tuple-element.15.refs_3_.refs_4_.good_ref, ...), custom_call_target="tpu_custom_call" | custom-call | tf_op jit(solution)/shard_map/pallas_call | solution.py:878
  96.1 59.7 %shard_map.90.inflow = f32[16,128,128]{2,1,0:T(8,128)S(1)} custom-call(s16[32,528,128]{2,1,0:T(8,128)(2,1)S(1)} %shard_map.89.words_ref), custom_call_target="tpu_custom_call" | custom-call | tf_op jit(solution)/shard_map/pallas_call | solution.py:850
  155.8 2.3 shard_map.91
  158.1 23.7 %shard_map.92 = (bf16[32,64,128]{2,1,0:T(8,128)(2,1)S(1)}, s32[32,128,128]{2,1,0:T(8,128)S(1)}) custom-call(bf16[64,128]{1,0:T(8,128)(2,1)S(1)} %get-tuple-element.24.own_ref, s16[32,64,128]{2,1,0:T(8,128)(2,1)S(1)} %get-tuple-element.23.lists_ref.refs_3_), custom_call_target="tpu_custom_call" | custom-call | tf_op jit(solution)/shard_map/pallas_call | solution.py:913
  181.8 40.5 %shard_map.93.share_ref = bf16[16,128,128]{2,1,0:T(8,128)(2,1)S(1)} custom-call(s32[256]{0:T(256)S(1)} %copy-done.1, s32[256]{0:T(256)S(1)} %copy-done.2, s32[128]{0:T(128)S(1)} %copy-done.3, s16[32,64,128]{2,1,0:T(8,128)(2,1)S(1)} %get-tuple-element.23.lists_ref.refs_3_, bf16[32,64,128]{2,1,0:T(8,128)(2,1)S(1)} %get-tuple-element.25.refs_4_, ...), custom_call_target="tpu_custom_call" | custom-call | tf_op jit(solution)/shard_map/pallas_call | solution.py:923
  222.4 54.2 %shard_map.94.refs_2_ = bf16[128,128,128]{2,1,0:T(8,128)(2,1)S(1)} custom-call(s32[8,1,128]{2,1,0:T(1,128)S(1)} %get-tuple-element.22.want_ref, bf16[16,128,128]{2,1,0:T(8,128)(2,1)S(1)} %shard_map.93.share_ref), custom_call_target="tpu_custom_call" | custom-call | tf_op jit(solution)/shard_map/pallas_call | solution.py:938
  276.6 11.3 %shard_map.95 = f32[2048,128]{1,0:T(8,128)} custom-call(s32[256]{0:T(256)S(1)} %copy-done.1, s32[256]{0:T(256)S(1)} %copy-done.2, bf16[128,128,128]{2,1,0:T(8,128)(2,1)S(1)} %shard_map.94.refs_2_, f32[16,128,128]{2,1,0:T(8,128)S(1)} %get-tuple-element.19.spam_ref.refs_6_.refs_3_, bf16[256,128,128]{2,1,0:T(8,128)(2,1)S(1)} %bitcast.4), custom_call_target="tpu_custom_call" | custom-call | tf_op jit(solution)/shard_map/pallas_call | solution.py:939
  (1 shorter events, 0.0 us)
Async XLA Ops:
  7.8 78.5 %slice-start = ((s8[8388608]{0:T(1024)(128)(4,1)}), s8[4194304]{0:T(1024)(128)(4,1)S(1)}, s32[]{:S(2)}) async-start(s8[8388608]{0:T(1024)(128)(4,1)} %bitcast.3), calls=%async_computation | async-start | bytes 8388608
  7.9 14.4 %copy-start.3 = (s32[128]{0:T(128)S(1)}, s32[128]{0:T(128)}, u32[]{:S(2)}) copy-start(s32[128]{0:T(128)} %refs_2_.5) | copy-start | bytes 1540
  7.9 78.5 %slice-start.1 = ((s8[8388608]{0:T(1024)(128)(4,1)}), s8[4194304]{0:T(1024)(128)(4,1)S(1)}, s32[]{:S(2)}) async-start(s8[8388608]{0:T(1024)(128)(4,1)} %bitcast.3), calls=%async_computation.1 | async-start | bytes 8388608
  22.2 64.2 %copy-start = (s32[2048]{0:T(1024)S(1)}, s32[2048]{0:T(1024)}, u32[]{:S(2)}) copy-start(s32[2048]{0:T(1024)} %param.11) | copy-start | bytes 24580
  22.2 64.2 %copy-start.1 = (s32[256]{0:T(256)S(1)}, s32[256]{0:T(256)}, u32[]{:S(2)}) copy-start(s32[256]{0:T(256)} %refs_0_.7) | copy-start | bytes 3076
  22.3 64.2 %copy-start.2 = (s32[256]{0:T(256)S(1)}, s32[256]{0:T(256)}, u32[]{:S(2)}) copy-start(s32[256]{0:T(256)} %refs_1_.7) | copy-start | bytes 3076

commit v5 on v4

--- a/solution.py
+++ b/solution.py
@@ -18,7 +18,8 @@
 WORD = 15
 GROUP = 16
 HALVES = 4
-LAYERS = 5
+LAYERS = 6
+MORE = 2
 MESH = pl.DeviceIdType.MESH
 
 
@@ -233,10 +234,6 @@
 
 def take(table, index):
     return jnp.take_along_axis(table, index, axis=1, mode="promise_in_bounds")
-
-
-def bound_of(code):
-    return LAYERS + 4 * code
 
 
 def find_ranks(groups, blocks, keys):
@@ -288,7 +285,7 @@
         jnp.maximum, [ends_of(g, groups, spot) - spot for g, spot in enumerate(spots)]
     ).astype(F32)
     most = jnp.max(jnp.max(most, axis=1, keepdims=True), axis=0, keepdims=True).astype(jnp.int32)
-    code = jnp.maximum(most - LAYERS + 3, 0) >> 2
+    code = jnp.where(most > LAYERS, 1, 0) + jnp.where(most > LAYERS + MORE, 1, 0)
     return (keys + code * (blocks * seeds)).astype(jnp.int16)
 
 
@@ -389,28 +386,16 @@
             self.pair(self.own, self.r, origin).wait_send()
 
 
-def value_kernel(rows, columns, groups, blocks, own_ref, lists_ref, vals_ref, rank_ref, *sems):
+def value_kernel(rows, columns, own_ref, vals_ref, *sems):
     spread = Spread(rows, columns, own_ref, vals_ref, sems)
-    peers, lines, size = lists_ref.shape
     greet(
         [((t, spread.z), t >= 0) for t in spread.mates + [spread.twin]]
         + [((spread.r, spread.z + side), spread.inside[side]) for side in (-1, 1)]
     )
-
-    def find(q, _):
-        keys = lists_ref[q].astype(jnp.int32) & (blocks * size - 1)
-        for g, spots in enumerate(find_ranks(groups, blocks, keys)):
-            rank_ref[q, g * lines : (g + 1) * lines, :] = spots
-        return 0
-
-    share = peers // (columns + 1)
     spread.begin()
     for d in range(1, columns):
-        lax.fori_loop((d - 1) * share, d * share, find, 0, unroll=2)
         spread.hop(d)
-    lax.fori_loop((columns - 1) * share, columns * share, find, 0, unroll=2)
     spread.collect()
-    lax.fori_loop(columns * share, peers, find, 0, unroll=2)
     spread.finish()
 
 
@@ -419,7 +404,7 @@
     groups = fetched.shape[1] // lines
     tall = 16
 
-    def paint(q, low, high):
+    def paint(q, low, high, fresh):
         tags = [
             F32(1) + (block_ref[q * cap + c] + 1).astype(F32) * F32(2.0**-14) for c in range(cap)
         ]
@@ -443,28 +428,34 @@
                         jnp.where(live & (plain * tag == got), plain, out) for tag, out in zip(tags, outs)
                     )
 
-                if high is None:
+                if fresh:
                     outs = (jnp.zeros((tall, size), F32),) * cap
-                    for j in range(low):
-                        outs = layer(j, outs)
                 else:
                     outs = tuple(
                         fetched[q * cap + c, pl.ds(row, tall), :].astype(F32) for c in range(cap)
                     )
+                if high - low > LAYERS:
                     outs = lax.fori_loop(low, high, layer, outs)
+                else:
+                    for j in range(low, high):
+                        outs = layer(j, outs)
                 for c in range(cap):
                     fetched[q * cap + c, pl.ds(row, tall), :] = outs[c].astype(BF16)
             return 0
 
-        lax.fori_loop(0, lines // tall, some, 0, unroll=2 if high is None else 1)
+        lax.fori_loop(0, lines // tall, some, 0, unroll=2 if fresh else 1)
 
     def one(q, _):
-        paint(q, LAYERS, None)
+        paint(q, 0, LAYERS, True)
         code = bounds[q, 0]
 
         @pl.when(code > 0)
         def _():
-            paint(q, LAYERS, bound_of(code))
+            paint(q, LAYERS, LAYERS + MORE, False)
+
+        @pl.when(code > 1)
+        def _():
+            paint(q, LAYERS + MORE, size // groups, False)
 
         return 0
 
@@ -492,9 +483,9 @@
 
 def reduce_kernel(first, rows, columns, cap, words_ref, *refs):
     if first:
-        cores_ref, mine_ref, keys_ref, inflow_ref, weight_ref, spam_ref, want_ref, lists_ref, *refs = refs
+        cores_ref, mine_ref, raw_ref, inflow_ref, weight_ref, spam_ref, want_ref, keys_ref, lists_ref, *refs = refs
     else:
-        inflow_ref, *refs = refs
+        lists_ref, inflow_ref, rank_ref, *refs = refs
     landed, table, partial, exps, packed, inbox, own, send, recv, chain_send, chain_recv, *refs = refs
     r, z = lax.axis_index("row"), lax.axis_index("col")
     blocks, part, size = partial.shape
@@ -557,12 +548,29 @@
         for t in others:
             know(t, r).start()
         want_ref[r] = mine_ref[...]
-        spread.begin()
-    for i in range(columns):
+
+    def launch(i):
         for h in range(halves):
             for t in others:
                 across(i, h, t, r).start()
         mine(i).start()
+
+    launch(0)
+    launch(1)
+    if first:
+        keys_ref[...] = sort_hosts(columns, blocks, raw_ref[...])
+        spread.begin()
+    else:
+        peers, lines, _ = lists_ref.shape
+        groups = seeds // lines
+        turns = min(8, (columns - 1) * halves)
+        load = -(-peers // turns)
+
+        def find(q, _):
+            keys = lists_ref[q].astype(jnp.int32) & (blocks * size - 1)
+            for g, spots in enumerate(find_ranks(groups, blocks, keys)):
+                rank_ref[q, g * lines : (g + 1) * lines, :] = spots
+            return 0
 
     pieces = min(4, (columns - 1) * halves)
     for i in range(columns):
@@ -677,8 +685,14 @@
                 if first and h == 0:
                     colsum[...] += F32(1)
             step = i * halves + h
-            if first and 0 < step < columns:
-                spread.hop(step)
+            if first and step < columns - 1:
+                spread.hop(step + 1)
+            if h == min(columns, halves) - 1 and i + 2 < columns:
+                launch(i + 2)
+            if first and step == (columns - 2) * halves:
+                spread.collect()
+            if not first and step < turns:
+                lax.fori_loop(step * load, min(peers, (step + 1) * load), find, 0, unroll=2)
             if first and step < pieces:
                 count_seeds(columns, cores_ref, tally, step, pieces)
             if first and step == pieces:
@@ -688,7 +702,6 @@
         for t in others:
             know(t, r).wait_send()
             know(t, t).wait_recv()
-        spread.collect()
         spread.finish()
     for i in range(columns):
         for h in range(halves):
@@ -777,10 +790,8 @@
             shares(shield_ref, weight_ref, distrust, out_ref)
 
 
-def start_kernel(columns, good_ref, spam_ref, count_ref, list_ref, keys_ref, tally):
-    raw = spam_ref[...]
-    list_ref[...] = jnp.transpose(raw.astype(F32)).astype(jnp.int32)
-    keys_ref[...] = sort_hosts(columns, count_ref.shape[0], raw)
+def start_kernel(columns, good_ref, spam_ref, count_ref, list_ref, tally):
+    list_ref[...] = jnp.transpose(spam_ref[...].astype(F32)).astype(jnp.int32)
     count_seeds(columns, good_ref, tally)
     spread_seeds(good_ref.shape[1], tally, count_ref)
 
@@ -805,13 +816,11 @@
     count = spam_cores.shape[1]
     groups = seeds // count
     lines = seeds // groups
-    good, spam_list, keys = pl.pallas_call(
+    good, spam_list = pl.pallas_call(
         functools.partial(start_kernel, columns),
-        out_shape=(
-            shape(vector, F32), shape(spam_cores.shape, jnp.int32), shape((lines, size), jnp.int16),
-        ),
+        out_shape=(shape(vector, F32), shape(spam_cores.shape, jnp.int32)),
         in_specs=[VM, VM],
-        out_specs=(VM, VM, VM),
+        out_specs=(VM, VM),
         scratch_shapes=[pltpu.VMEM((seeds, blocks, size), F32)],
         compiler_params=PLAIN,
         cost_estimate=pl.CostEstimate(
@@ -845,13 +854,16 @@
         long = blocks * part + blocks * (4 if first else 1)
         outs = (
             shape(vector, F32), shape((blocks, size), F32), shape(vector, F32),
-            shape((rows, 1, slots), jnp.int32), shape((peers, lines, size), jnp.int16),
-        )
+            shape((rows, 1, slots), jnp.int32), shape((lines, size), jnp.int16),
+            shape((peers, lines, size), jnp.int16),
+        )
+        if not first:
+            outs = (shape(vector, F32), shape((peers, seeds, size), jnp.int32))
         return pl.pallas_call(
             functools.partial(reduce_kernel, first, rows, columns, cap),
-            out_shape=outs if first else outs[:1],
-            in_specs=[ANY, VM, VM, VM] if first else [ANY],
-            out_specs=(VM,) * 5 if first else (VM,),
+            out_shape=outs,
+            in_specs=[ANY, VM, VM, VM] if first else [ANY, VM],
+            out_specs=(VM,) * len(outs),
             scratch_shapes=[
                 pltpu.VMEM((columns, rows, cap * size + tail, size), jnp.int16),
                 pltpu.VMEM((rows * cap, blocks, size), F32),
@@ -872,8 +884,8 @@
             ),
         )(words_in, *rest)
 
-    inflow, weight, spam, want, lists = reduce(
-        True, outgoing, spam_list, slot_block.reshape(1, slots), keys
+    inflow, weight, spam, want, keys, lists = reduce(
+        True, outgoing, spam_list, slot_block.reshape(1, slots), spam_cores.T
     )
     outgoing = pl.pallas_call(
         functools.partial(push_kernel, False, cap, part),
@@ -887,7 +899,7 @@
         ],
         compiler_params=PLAIN,
     )(tile_src, tile_slot, slot_block, inflow, good, degree, tiles)
-    (inflow,) = reduce(False, outgoing)
+    inflow, ranks = reduce(False, outgoing, lists)
     fetch = pl.pallas_call(
         functools.partial(fetch_kernel, rows, columns, cap),
         out_shape=shape((slots, seeds, size), BF16),
@@ -910,16 +922,16 @@
         out_specs=(VM, VM, VM),
         compiler_params=PLAIN,
     )(inflow, good, spam, weight, keys)
-    vals, ranks = pl.pallas_call(
-        functools.partial(value_kernel, rows, columns, groups, blocks),
-        out_shape=(shape((peers, lines, size), BF16), shape((peers, seeds, size), jnp.int32)),
-        in_specs=[VM, VM],
-        out_specs=(VM, VM),
+    vals = pl.pallas_call(
+        functools.partial(value_kernel, rows, columns),
+        out_shape=shape((peers, lines, size), BF16),
+        in_specs=[VM],
+        out_specs=VM,
         scratch_shapes=spread_sems,
         compiler_params=pltpu.CompilerParams(
             collective_id=3, has_side_effects=True, vmem_limit_bytes=LIMIT
         ),
-    )(vals, lists)
+    )(vals)
     share = pl.pallas_call(
         functools.partial(pull_kernel, False),
         grid=(steps,),

time: 288 us -> 277 us (0.962)
  Pallas kernels: 287 us -> 276 us
    pallas_call x1, Pallas kernels: 40.5 us -> 25.5 us  [body(): pl.pallas_call(functools.partial(pull_kernel, False), grid=(steps,), out_...]
    pallas_call x1, Pallas kernels: 23.7 us -> 28.7 us  [body(): pl.pallas_call(functools.partial(value_kernel, rows, columns), out_shape=...]
    pallas_call x2, Pallas kernels: 124 us -> 127 us  [reduce(): pl.pallas_call(functools.partial(reduce_kernel, first, rows, columns, cap...]
where the time goes in v5:
time: 277 us
  Pallas kernels  276 us (100%)
    pallas_call x2, Pallas kernels, reduce(): pl.pallas_call(functools.partial(reduce_kernel, first, rows, columns, cap...  127 us
    pallas_call x1, Pallas kernels, body(): fetched = fetch(want, share)  52.3 us
    pallas_call x1, Pallas kernels, body(): pl.pallas_call(functools.partial(value_kernel, rows, columns), out_shape=...  28.7 us
    pallas_call x1, Pallas kernels, body(): pl.pallas_call(functools.partial(pull_kernel, False), grid=(steps,), out_...  25.5 us
    pallas_call x1, Pallas kernels, body(): pl.pallas_call(functools.partial(push_kernel, True, cap, part), grid=(ste...  14.3 us
    pallas_call x1, Pallas kernels, body(): pl.pallas_call(functools.partial(pull_kernel, True), grid=(steps,), out_s...  11.4 us
    pallas_call x1, Pallas kernels, body(): pl.pallas_call(functools.partial(push_kernel, False, cap, part), grid=(st...  9.7 us

profile of v5, /device:TPU:1, one launch (start us, length us, event | category | flops | bytes accessed | tf_op | source)
XLA Modules:
  0.0 276.8 jit_solution(7842247489057500672)
XLA Ops:
  0.6 5.0 %shard_map.86 = (f32[16,128,128]{2,1,0:T(8,128)S(1)}, s32[128,64]{1,0:T(8,128)S(1)}) custom-call(s32[128,128]{1,0:T(8,128)} %good_ref.1, s32[64,128]{1,0:T(8,128)} %bitcast.5), custom_call_target="tpu_custom_call" | custom-call | flops 603979776 | bytes 25165824 | tf_op jit(solution)/shard_map/pallas_call | solution.py:819
  5.6 0.0 slice-start
  5.6 0.0 copy-start
  5.6 0.0 copy-start.4
  5.6 0.0 slice-start.1
  5.6 14.3 %shard_map.87.words_ref = s16[32,528,128]{2,1,0:T(8,128)(2,1)S(1)} custom-call(s32[256]{0:T(256)} %refs_0_.7, s32[256]{0:T(256)} %refs_1_.7, s32[128]{0:T(128)} %refs_2_.5, f32[16,128,128]{2,1,0:T(8,128)S(1)} %get-tuple-element.15.refs_3_.refs_4_.good_ref, s32[16,1,128]{2,1,0:T(1,128)} %bitcast.7, bf16[256,128,128]{2,1,0:T(8,128)(2,1)} %refs_4_.1), custom_call_target="tpu_custom_call" | custom-call | tf_op jit(solution)/shard_map/pallas_call | solution.py:834
  20.0 0.0 copy-done
  20.0 0.0 copy-done.4
  20.0 0.0 copy-start.1
  20.0 0.0 copy-start.2
  20.0 0.0 copy-start.3
  20.0 63.5 %shard_map.88 = (f32[16,128,128]{2,1,0:T(8,128)S(1)}, f32[16,128]{1,0:T(8,128)S(1)}, f32[16,128,128]{2,1,0:T(8,128)S(1)}, s32[8,1,128]{2,1,0:T(1,128)S(1)}, s16[...) custom-call(s16[32,528,128]{2,1,0:T(8,128)(2,1)S(1)} %shard_map.87.words_ref, ...), custom_call_target="tpu_custom_call" | custom-call | tf_op jit(solution)/shard_map/pallas_call | solution.py:862
  83.6 0.0 slice-done
  83.6 0.0 slice-done.1
  83.6 0.0 copy-done.1
  83.6 0.0 copy-done.2
  83.6 0.0 copy-done.3
  83.6 9.7 %shard_map.89.words_ref = s16[32,528,128]{2,1,0:T(8,128)(2,1)S(1)} custom-call(s32[256]{0:T(256)S(1)} %copy-done.2, s32[256]{0:T(256)S(1)} %copy-done.3, s32[128]{0:T(128)S(1)} %copy-done.4, f32[16,128,128]{2,1,0:T(8,128)S(1)} %get-tuple-element.17.refs_3_, f32[16,128,128]{2,1,0:T(8,128)S(1)} %get-tuple-element.15.refs_3_.refs_4_.good_ref, ...), custom_call_target="tpu_custom_call" | custom-call | tf_op jit(solution)/shard_map/pallas_call | solution.py:890
  93.3 63.3 %shard_map.90 = (f32[16,128,128]{2,1,0:T(8,128)S(1)}, s32[32,128,128]{2,1,0:T(8,128)S(1)}) custom-call(s16[32,528,128]{2,1,0:T(8,128)(2,1)S(1)} %shard_map.89.words_ref, s16[32,64,128]{2,1,0:T(8,128)(2,1)S(1)} %get-tuple-element.18.refs_0_.refs_3_), custom_call_target="tpu_custom_call" | custom-call | tf_op jit(solution)/shard_map/pallas_call | solution.py:862
  156.7 2.3 shard_map.91
  158.9 28.7 %shard_map.92.refs_4_ = bf16[32,64,128]{2,1,0:T(8,128)(2,1)S(1)} custom-call(bf16[64,128]{1,0:T(8,128)(2,1)S(1)} %get-tuple-element.25.own_ref), custom_call_target="tpu_custom_call" | custom-call | tf_op jit(solution)/shard_map/pallas_call | solution.py:925
  187.6 25.5 %shard_map.93.share_ref = bf16[16,128,128]{2,1,0:T(8,128)(2,1)S(1)} custom-call(s32[256]{0:T(256)S(1)} %copy-done.2, s32[256]{0:T(256)S(1)} %copy-done.3, s32[128]{0:T(128)S(1)} %copy-done.4, s16[32,64,128]{2,1,0:T(8,128)(2,1)S(1)} %get-tuple-element.18.refs_0_.refs_3_, bf16[32,64,128]{2,1,0:T(8,128)(2,1)S(1)} %shard_map.92.refs_4_, ...), custom_call_target="tpu_custom_call" | custom-call | tf_op jit(solution)/shard_map/pallas_call | solution.py:935
  213.1 52.3 %shard_map.94.refs_2_ = bf16[128,128,128]{2,1,0:T(8,128)(2,1)S(1)} custom-call(s32[8,1,128]{2,1,0:T(1,128)S(1)} %get-tuple-element.24.want_ref, bf16[16,128,128]{2,1,0:T(8,128)(2,1)S(1)} %shard_map.93.share_ref), custom_call_target="tpu_custom_call" | custom-call | tf_op jit(solution)/shard_map/pallas_call | solution.py:950
  265.4 11.4 %shard_map.95 = f32[2048,128]{1,0:T(8,128)} custom-call(s32[256]{0:T(256)S(1)} %copy-done.2, s32[256]{0:T(256)S(1)} %copy-done.3, bf16[128,128,128]{2,1,0:T(8,128)(2,1)S(1)} %shard_map.94.refs_2_, f32[16,128,128]{2,1,0:T(8,128)S(1)} %get-tuple-element.20.spam_ref.refs_6_.refs_3_, bf16[256,128,128]{2,1,0:T(8,128)(2,1)S(1)} %bitcast.4), custom_call_target="tpu_custom_call" | custom-call | tf_op jit(solution)/shard_map/pallas_call | solution.py:951
  (1 shorter events, 0.0 us)
Async XLA Ops:
  5.6 78.0 %slice-start = ((s8[8388608]{0:T(1024)(128)(4,1)}), s8[4194304]{0:T(1024)(128)(4,1)S(1)}, s32[]{:S(2)}) async-start(s8[8388608]{0:T(1024)(128)(4,1)} %bitcast.3), calls=%async_computation | async-start | bytes 8388608
  5.6 14.4 %copy-start = (s32[128,64]{0,1:T(8,128)S(1)}, s32[128,64]{0,1:T(8,128)}, u32[]{:S(2)}) copy-start(s32[128,64]{0,1:T(8,128)} %param.13) | copy-start | bytes 98308
  5.6 14.4 %copy-start.4 = (s32[128]{0:T(128)S(1)}, s32[128]{0:T(128)}, u32[]{:S(2)}) copy-start(s32[128]{0:T(128)} %refs_2_.5) | copy-start | bytes 1540
  5.6 78.0 %slice-start.1 = ((s8[8388608]{0:T(1024)(128)(4,1)}), s8[4194304]{0:T(1024)(128)(4,1)S(1)}, s32[]{:S(2)}) async-start(s8[8388608]{0:T(1024)(128)(4,1)} %bitcast.3), calls=%async_computation.1 | async-start | bytes 8388608
  20.0 63.6 %copy-start.1 = (s32[2048]{0:T(1024)S(1)}, s32[2048]{0:T(1024)}, u32[]{:S(2)}) copy-start(s32[2048]{0:T(1024)} %param.11) | copy-start | bytes 24580
  20.0 63.6 %copy-start.2 = (s32[256]{0:T(256)S(1)}, s32[256]{0:T(256)}, u32[]{:S(2)}) copy-start(s32[256]{0:T(256)} %refs_0_.7) | copy-start | bytes 3076
  20.0 63.6 %copy-start.3 = (s32[256]{0:T(256)S(1)}, s32[256]{0:T(256)}, u32[]{:S(2)}) copy-start(s32[256]{0:T(256)} %refs_1_.7) | copy-start | bytes 3076

commit v6 on v5

--- a/solution.py
+++ b/solution.py
@@ -298,7 +298,7 @@
         self.twin = r + 1 - 2 * lax.rem(r, 2)
         self.mates = [lax.rem(r + d, rows) for d in range(2, rows, 2)]
         self.others = [self.twin] + [lax.rem(self.twin + d, rows) for d in range(2, rows, 2)]
-        self.inside = {side: (z + side >= 0) & (z + side < columns) for side in (-1, 1)}
+        self.peers = [lax.rem(z + d, columns) for d in range(1, columns)]
 
     def send(self, source, row, origin, sends, recvs, to):
         return pltpu.make_async_remote_copy(
@@ -309,11 +309,10 @@
     def place(self, row, origin):
         return self.out.at[row * self.columns + origin]
 
-    def line(self, source, origin, side):
-        way = 0 if side < 0 else 1
+    def line(self, d, origin):
         return self.send(
-            source, self.r, origin, self.line_send.at[way, origin], self.line_recv.at[origin],
-            (self.r, self.z + side),
+            self.own, self.r, origin, self.line_send.at[d], self.line_recv.at[origin],
+            (self.r, lax.rem(self.z + d, self.columns)),
         )
 
     def plane(self, source, t, row, origin):
@@ -334,30 +333,15 @@
         self.pair(source, self.r, origin).start()
 
     def begin(self):
-        for side in (-1, 1):
-            @pl.when(self.inside[side])
-            def _():
-                self.line(self.own, self.z, side).start()
+        for d in range(1, self.columns):
+            self.line(d, self.z).start()
         self.across(self.own, self.z)
         self.out[self.r * self.columns + self.z] = self.own[...]
 
-    def each(self, d):
-        for side in (-1, 1):
-            origin = self.z + side * d
-            yield side, origin, (origin >= 0) & (origin < self.columns)
-
     def hop(self, d):
-        for side, origin, there in self.each(d):
-            @pl.when(there)
-            def _():
-                here = self.place(self.r, origin)
-                self.line(here, origin, side).wait_recv()
-
-                @pl.when(self.inside[-side])
-                def _():
-                    self.line(here, origin, -side).start()
-
-                self.across(here, origin)
+        origin = lax.rem(self.z + d, self.columns)
+        self.line(d, origin).wait_recv()
+        self.across(self.place(self.r, origin), origin)
 
     def collect(self):
         for t in self.mates:
@@ -370,15 +354,8 @@
         for t in self.others:
             for origin in range(self.columns):
                 self.pair(self.place(t, origin), t, origin).wait_recv()
-        for side in (-1, 1):
-            @pl.when(self.inside[side])
-            def _():
-                self.line(self.own, self.z, side).wait_send()
         for d in range(1, self.columns):
-            for side, origin, there in self.each(d):
-                @pl.when(there & self.inside[-side])
-                def _():
-                    self.line(self.own, origin, -side).wait_send()
+            self.line(d, self.z).wait_send()
         for origin in range(self.columns):
             for t in self.mates:
                 self.plane(self.own, t, self.r, origin).wait_send()
@@ -390,7 +367,7 @@
     spread = Spread(rows, columns, own_ref, vals_ref, sems)
     greet(
         [((t, spread.z), t >= 0) for t in spread.mates + [spread.twin]]
-        + [((spread.r, spread.z + side), spread.inside[side]) for side in (-1, 1)]
+        + [((spread.r, y), y >= 0) for y in spread.peers]
     )
     spread.begin()
     for d in range(1, columns):
@@ -467,10 +444,9 @@
     for plane in range(columns):
         line = []
         for k in range(columns):
-            if columns - 1 - k > plane:
-                line.append(columns - 1 - k)
-            if k < plane:
-                line.append(k)
+            ahead = [t for t in (columns - 1 - k,) if t > plane]
+            back = [t for t in (k,) if t < plane]
+            line += ahead + back if 2 * plane < columns else back + ahead
         table.append(line + [plane])
     picks = []
     for i in range(columns):
@@ -486,7 +462,7 @@
         cores_ref, mine_ref, raw_ref, inflow_ref, weight_ref, spam_ref, want_ref, keys_ref, lists_ref, *refs = refs
     else:
         lists_ref, inflow_ref, rank_ref, *refs = refs
-    landed, table, partial, exps, packed, inbox, own, send, recv, chain_send, chain_recv, *refs = refs
+    landed, table, partial, exps, gains, packed, inbox, own, send, recv, chain_send, chain_recv, *refs = refs
     r, z = lax.axis_index("row"), lax.axis_index("col")
     blocks, part, size = partial.shape
     seeds = inflow_ref.shape[1]
@@ -504,7 +480,10 @@
     block_iota = lax.broadcasted_iota(jnp.int32, (blocks, size), 0)
     greet(
         [((t, z), t >= 0) for t in others]
-        + [((r, z - 1), z > 0), ((r, z + 1), z < columns - 1)]
+        + (
+            [((r, lax.rem(z + d, columns)), z >= 0) for d in range(1, columns)] if first
+            else [((r, z - 1), z > 0), ((r, z + 1), z < columns - 1)]
+        )
     )
 
     def across(i, h, t, origin):
@@ -563,7 +542,7 @@
     else:
         peers, lines, _ = lists_ref.shape
         groups = seeds // lines
-        turns = min(8, (columns - 1) * halves)
+        turns = (columns - 1) * halves - 1
         load = -(-peers // turns)
 
         def find(q, _):
@@ -572,7 +551,7 @@
                 rank_ref[q, g * lines : (g + 1) * lines, :] = spots
             return 0
 
-    pieces = min(4, (columns - 1) * halves)
+    pieces = min(8, (columns - 1) * halves)
     for i in range(columns):
         mine(i).wait()
         side = jnp.where(targets[i] > z, 0, 1)
@@ -599,9 +578,9 @@
                             cols = cols + jnp.where(hit, jnp.broadcast_to(col, (blocks, size)), F32(0))
                     return cols
 
-                cols = lax.fori_loop(0, rows, weigh, cols)
-
-            begin = spans[h][0]
+                cols = lax.fori_loop(0, rows, weigh, cols, unroll=4)
+
+            first_row = spans[h][0]
 
             def strip(k, _):
                 at = pl.multiple_of(k * 16, 16)
@@ -609,7 +588,7 @@
                 def add(q, sums):
                     sums = list(sums)
                     for c in range(cap):
-                        spot = pl.multiple_of(begin + c * part + at, 16)
+                        spot = pl.multiple_of(first_row + c * part + at, 16)
                         value = to_float(landed[i, q, pl.ds(spot, 16), :])
                         for b in range(blocks):
                             sums[b] = sums[b] + value * table[q * cap + c, b : b + 1, :]
@@ -631,7 +610,7 @@
                     partial[b] += got * exps[pl.ds(b, 1), :]
                     return 0
 
-                lax.fori_loop(0, blocks, one, 0)
+                lax.fori_loop(0, blocks, one, 0, unroll=4)
 
             def join_cols(way):
                 f, high, low = (
@@ -650,16 +629,20 @@
                     if first and h == 0:
                         join_cols(side)
 
+                def peak(b, _):
+                    exps[pl.ds(b, 1), :] = jnp.max(jnp.abs(partial[b]), axis=0, keepdims=True)
+                    return 0
+
                 def squeeze(b, _):
-                    value = partial[b]
-                    e = exponent_of(jnp.max(jnp.abs(value), axis=0, keepdims=True))
-                    exps[pl.ds(b, 1), :] = e
                     packed[i, h, pl.ds(pl.multiple_of(b * part, part), part), :] = to_int16(
-                        to_words(value * jnp.exp2(WORD - e))
+                        to_words(partial[b] * gains[pl.ds(b, 1), :])
                     )
                     return 0
 
-                lax.fori_loop(0, blocks, squeeze, 0)
+                lax.fori_loop(0, blocks, peak, 0, unroll=8)
+                exps[...] = exponent_of(exps[...])
+                gains[...] = jnp.exp2(WORD - exps[...])
+                lax.fori_loop(0, blocks, squeeze, 0, unroll=8)
                 packed[i, h, data : data + blocks, :] = to_int16(exps[...])
                 if first and h == 0:
                     col = colsum[...]
@@ -681,7 +664,7 @@
                     inflow_ref[b, h * part : (h + 1) * part, :] = partial[b]
                     return 0
 
-                lax.fori_loop(0, blocks, finish, 0)
+                lax.fori_loop(0, blocks, finish, 0, unroll=4)
                 if first and h == 0:
                     colsum[...] += F32(1)
             step = i * halves + h
@@ -691,11 +674,12 @@
                 launch(i + 2)
             if first and step == (columns - 2) * halves:
                 spread.collect()
-            if not first and step < turns:
-                lax.fori_loop(step * load, min(peers, (step + 1) * load), find, 0, unroll=2)
-            if first and step < pieces:
-                count_seeds(columns, cores_ref, tally, step, pieces)
-            if first and step == pieces:
+            if not first and 0 <= step - halves < turns:
+                begin, end = (min(peers, k * load) for k in (step - halves, step - halves + 1))
+                lax.fori_loop(begin, end, find, 0, unroll=3 if (end - begin) % 3 == 0 else 2)
+            if first and 0 <= step - halves < pieces:
+                count_seeds(columns, cores_ref, tally, step - halves, pieces)
+            if first and step == halves + pieces:
                 spread_seeds(cores_ref.shape[1], tally, spam_ref)
 
     if first:
@@ -846,7 +830,7 @@
 
     dma = pltpu.SemaphoreType.DMA
     spread_sems = [
-        dma((2, columns)), dma((columns,)), dma((rows, columns)), dma((rows, columns)),
+        dma((columns,)), dma((columns,)), dma((rows, columns)), dma((rows, columns)),
         dma((rows, columns)), dma((rows, columns)),
     ]
 
@@ -868,6 +852,7 @@
                 pltpu.VMEM((columns, rows, cap * size + tail, size), jnp.int16),
                 pltpu.VMEM((rows * cap, blocks, size), F32),
                 pltpu.VMEM((blocks, part, size), F32),
+                pltpu.VMEM((blocks, size), F32),
                 pltpu.VMEM((blocks, size), F32),
                 pltpu.VMEM((columns - 1, HALVES, long, size), jnp.int16),
                 pltpu.VMEM((2, columns, HALVES, long, size), jnp.int16),

time: 277 us -> 249 us (0.90)
  Pallas kernels: 276 us -> 248 us
    pallas_call x1, Pallas kernels: 28.7 us -> 11.1 us  [body(): pl.pallas_call(functools.partial(value_kernel, rows, columns), out_shape=...]
    pallas_call x2, Pallas kernels: 127 us -> 115 us  [reduce(): pl.pallas_call(functools.partial(reduce_kernel, first, rows, columns, cap...]
where the time goes in v6:
time: 249 us
  Pallas kernels  248 us (100%)
    pallas_call x2, Pallas kernels, reduce(): pl.pallas_call(functools.partial(reduce_kernel, first, rows, columns, cap...  115 us
    pallas_call x1, Pallas kernels, body(): fetched = fetch(want, share)  53.2 us
    pallas_call x1, Pallas kernels, body(): pl.pallas_call(functools.partial(pull_kernel, False), grid=(steps,), out_...  26 us
    pallas_call x1, Pallas kernels, body(): pl.pallas_call(functools.partial(push_kernel, True, cap, part), grid=(ste...  14.3 us
    pallas_call x1, Pallas kernels, body(): pl.pallas_call(functools.partial(pull_kernel, True), grid=(steps,), out_s...  11.4 us
    pallas_call x1, Pallas kernels, body(): pl.pallas_call(functools.partial(value_kernel, rows, columns), out_shape=...  11.1 us
    pallas_call x1, Pallas kernels, body(): pl.pallas_call(functools.partial(push_kernel, False, cap, part), grid=(st...  9.7 us

profile of v6, /device:TPU:1, one launch (start us, length us, event | category | flops | bytes accessed | tf_op | source)
XLA Modules:
  0.0 249.2 jit_solution(9196316567414074787)
XLA Ops:
  0.6 5.0 %shard_map.86 = (f32[16,128,128]{2,1,0:T(8,128)S(1)}, s32[128,64]{1,0:T(8,128)S(1)}) custom-call(s32[128,128]{1,0:T(8,128)} %good_ref.1, s32[64,128]{1,0:T(8,128)} %bitcast.5), custom_call_target="tpu_custom_call" | custom-call | flops 603979776 | bytes 25165824 | tf_op jit(solution)/shard_map/pallas_call | solution.py:803
  5.6 0.0 slice-start
  5.6 0.0 copy-start
  5.6 0.0 copy-start.4
  5.6 0.0 slice-start.1
  5.6 14.3 %shard_map.87.words_ref = s16[32,528,128]{2,1,0:T(8,128)(2,1)S(1)} custom-call(s32[256]{0:T(256)} %refs_0_.7, s32[256]{0:T(256)} %refs_1_.7, s32[128]{0:T(128)} %refs_2_.5, f32[16,128,128]{2,1,0:T(8,128)S(1)} %get-tuple-element.15.refs_3_.refs_4_.good_ref, s32[16,1,128]{2,1,0:T(1,128)} %bitcast.7, bf16[256,128,128]{2,1,0:T(8,128)(2,1)} %refs_4_.1), custom_call_target="tpu_custom_call" | custom-call | tf_op jit(solution)/shard_map/pallas_call | solution.py:818
  20.0 0.0 copy-done
  20.0 0.0 copy-done.4
  20.0 0.0 copy-start.1
  20.0 0.0 copy-start.2
  20.0 0.0 copy-start.3
  20.1 61.4 %shard_map.88 = (f32[16,128,128]{2,1,0:T(8,128)S(1)}, f32[16,128]{1,0:T(8,128)S(1)}, f32[16,128,128]{2,1,0:T(8,128)S(1)}, s32[8,1,128]{2,1,0:T(1,128)S(1)}, s16[...) custom-call(s16[32,528,128]{2,1,0:T(8,128)(2,1)S(1)} %shard_map.87.words_ref, ...), custom_call_target="tpu_custom_call" | custom-call | tf_op jit(solution)/shard_map/pallas_call | solution.py:846
  81.4 0.0 slice-done
  81.4 0.0 slice-done.1
  81.4 0.0 copy-done.1
  81.5 0.0 copy-done.2
  81.5 0.0 copy-done.3
  81.5 9.7 %shard_map.89.words_ref = s16[32,528,128]{2,1,0:T(8,128)(2,1)S(1)} custom-call(s32[256]{0:T(256)S(1)} %copy-done.2, s32[256]{0:T(256)S(1)} %copy-done.3, s32[128]{0:T(128)S(1)} %copy-done.4, f32[16,128,128]{2,1,0:T(8,128)S(1)} %get-tuple-element.17.refs_3_, f32[16,128,128]{2,1,0:T(8,128)S(1)} %get-tuple-element.15.refs_3_.refs_4_.good_ref, ...), custom_call_target="tpu_custom_call" | custom-call | tf_op jit(solution)/shard_map/pallas_call | solution.py:875
  91.2 53.9 %shard_map.90 = (f32[16,128,128]{2,1,0:T(8,128)S(1)}, s32[32,128,128]{2,1,0:T(8,128)S(1)}) custom-call(s16[32,528,128]{2,1,0:T(8,128)(2,1)S(1)} %shard_map.89.words_ref, s16[32,64,128]{2,1,0:T(8,128)(2,1)S(1)} %get-tuple-element.18.refs_0_.refs_3_), custom_call_target="tpu_custom_call" | custom-call | tf_op jit(solution)/shard_map/pallas_call | solution.py:846
  145.1 2.3 shard_map.91
  147.3 11.1 %shard_map.92.refs_4_ = bf16[32,64,128]{2,1,0:T(8,128)(2,1)S(1)} custom-call(bf16[64,128]{1,0:T(8,128)(2,1)S(1)} %get-tuple-element.25.own_ref), custom_call_target="tpu_custom_call" | custom-call | tf_op jit(solution)/shard_map/pallas_call | solution.py:910
  158.5 26.0 %shard_map.93.share_ref = bf16[16,128,128]{2,1,0:T(8,128)(2,1)S(1)} custom-call(s32[256]{0:T(256)S(1)} %copy-done.2, s32[256]{0:T(256)S(1)} %copy-done.3, s32[128]{0:T(128)S(1)} %copy-done.4, s16[32,64,128]{2,1,0:T(8,128)(2,1)S(1)} %get-tuple-element.18.refs_0_.refs_3_, bf16[32,64,128]{2,1,0:T(8,128)(2,1)S(1)} %shard_map.92.refs_4_, ...), custom_call_target="tpu_custom_call" | custom-call | tf_op jit(solution)/shard_map/pallas_call | solution.py:920
  184.5 53.2 %shard_map.94.refs_2_ = bf16[128,128,128]{2,1,0:T(8,128)(2,1)S(1)} custom-call(s32[8,1,128]{2,1,0:T(1,128)S(1)} %get-tuple-element.24.want_ref, bf16[16,128,128]{2,1,0:T(8,128)(2,1)S(1)} %shard_map.93.share_ref), custom_call_target="tpu_custom_call" | custom-call | tf_op jit(solution)/shard_map/pallas_call | solution.py:935
  237.8 11.4 %shard_map.95 = f32[2048,128]{1,0:T(8,128)} custom-call(s32[256]{0:T(256)S(1)} %copy-done.2, s32[256]{0:T(256)S(1)} %copy-done.3, bf16[128,128,128]{2,1,0:T(8,128)(2,1)S(1)} %shard_map.94.refs_2_, f32[16,128,128]{2,1,0:T(8,128)S(1)} %get-tuple-element.20.spam_ref.refs_6_.refs_3_, bf16[256,128,128]{2,1,0:T(8,128)(2,1)S(1)} %bitcast.4), custom_call_target="tpu_custom_call" | custom-call | tf_op jit(solution)/shard_map/pallas_call | solution.py:936
  (1 shorter events, 0.0 us)
Async XLA Ops:
  5.6 75.8 %slice-start = ((s8[8388608]{0:T(1024)(128)(4,1)}), s8[4194304]{0:T(1024)(128)(4,1)S(1)}, s32[]{:S(2)}) async-start(s8[8388608]{0:T(1024)(128)(4,1)} %bitcast.3), calls=%async_computation | async-start | bytes 8388608
  5.6 14.4 %copy-start = (s32[128,64]{0,1:T(8,128)S(1)}, s32[128,64]{0,1:T(8,128)}, u32[]{:S(2)}) copy-start(s32[128,64]{0,1:T(8,128)} %param.13) | copy-start | bytes 98308
  5.6 14.4 %copy-start.4 = (s32[128]{0:T(128)S(1)}, s32[128]{0:T(128)}, u32[]{:S(2)}) copy-start(s32[128]{0:T(128)} %refs_2_.5) | copy-start | bytes 1540
  5.6 75.8 %slice-start.1 = ((s8[8388608]{0:T(1024)(128)(4,1)}), s8[4194304]{0:T(1024)(128)(4,1)S(1)}, s32[]{:S(2)}) async-start(s8[8388608]{0:T(1024)(128)(4,1)} %bitcast.3), calls=%async_computation.1 | async-start | bytes 8388608
  20.0 61.4 %copy-start.1 = (s32[2048]{0:T(1024)S(1)}, s32[2048]{0:T(1024)}, u32[]{:S(2)}) copy-start(s32[2048]{0:T(1024)} %param.11) | copy-start | bytes 24580
  20.0 61.4 %copy-start.2 = (s32[256]{0:T(256)S(1)}, s32[256]{0:T(256)}, u32[]{:S(2)}) copy-start(s32[256]{0:T(256)} %refs_0_.7) | copy-start | bytes 3076
  20.0 61.4 %copy-start.3 = (s32[256]{0:T(256)S(1)}, s32[256]{0:T(256)}, u32[]{:S(2)}) copy-start(s32[256]{0:T(256)} %refs_1_.7) | copy-start | bytes 3076

commit v7 on v6

--- a/solution.py
+++ b/solution.py
@@ -16,7 +16,7 @@
 BF16 = jnp.bfloat16
 PLAIN = pltpu.CompilerParams(vmem_limit_bytes=LIMIT)
 WORD = 15
-GROUP = 16
+GROUP = 64
 HALVES = 4
 LAYERS = 6
 MORE = 2
@@ -91,7 +91,7 @@
         out_ref[p, at : at + tail, :] = jnp.concatenate(rows, axis=0).astype(jnp.int32).astype(jnp.int16)
         return 0
 
-    lax.fori_loop(0, peers, one, 0)
+    lax.fori_loop(0, peers, one, 0, unroll=2)
 
 
 def push_kernel(first, cap, part, *refs):
@@ -139,10 +139,10 @@
 def shares(shield_ref, weight_ref, start_of, share_ref):
     def one(b, _):
         weight = weight_ref[pl.ds(b, 1), :]
-        share_ref[b] = (shield_ref[b] * start_of(b) / weight).astype(BF16)
+        share_ref[b] = jnp.transpose(shield_ref[b] * start_of(b) / weight).astype(BF16)
         return 0
 
-    lax.fori_loop(0, share_ref.shape[0], one, 0)
+    lax.fori_loop(0, share_ref.shape[0], one, 0, unroll=2)
 
 
 def greet(devices):
@@ -363,15 +363,24 @@
             self.pair(self.own, self.r, origin).wait_send()
 
 
-def value_kernel(rows, columns, own_ref, vals_ref, *sems):
+def value_kernel(rows, columns, own_ref, spam_ref, vals_ref, turned_ref, *sems):
     spread = Spread(rows, columns, own_ref, vals_ref, sems)
     greet(
         [((t, spread.z), t >= 0) for t in spread.mates + [spread.twin]]
         + [((spread.r, y), y >= 0) for y in spread.peers]
     )
     spread.begin()
-    for d in range(1, columns):
-        spread.hop(d)
+
+    def turn(b, _):
+        turned_ref[b] = jnp.transpose(spam_ref[b])
+        return 0
+
+    share = -(-spam_ref.shape[0] // columns)
+    for d in range(columns):
+        if d:
+            spread.hop(d)
+        first, end = (min(spam_ref.shape[0], k * share) for k in (d, d + 1))
+        lax.fori_loop(first, end, turn, 0)
     spread.collect()
     spread.finish()
 
@@ -420,7 +429,7 @@
                     fetched[q * cap + c, pl.ds(row, tall), :] = outs[c].astype(BF16)
             return 0
 
-        lax.fori_loop(0, lines // tall, some, 0, unroll=2 if fresh else 1)
+        lax.fori_loop(0, lines // tall, some, 0, unroll=4 if fresh else 1)
 
     def one(q, _):
         paint(q, 0, LAYERS, True)
@@ -747,12 +756,13 @@
         products = []
         for k in range(GROUP):
             n = step * per_step + g * GROUP + k
-            products.append(
-                lax.dot_general(
-                    fetched_ref[slot_ref[n]], tiles_ref[g * GROUP + k], (((1,), (1,)), ((), ())),
-                    preferred_element_type=F32,
+            tile, got = tiles_ref[g * GROUP + k], fetched_ref[slot_ref[n]]
+            if last:
+                products.append(jnp.dot(tile, got, preferred_element_type=F32))
+            else:
+                products.append(
+                    lax.dot_general(got, tile, (((1,), (1,)), ((), ())), preferred_element_type=F32)
                 )
-            )
         for k in range(GROUP):
             acc[src_ref[step * per_step + g * GROUP + k]] += products[k]
         return 0
@@ -766,18 +776,21 @@
 
         if last:
             def one(b, _):
-                out_ref[pl.ds(pl.multiple_of(b * size, size), size), :] = jnp.transpose(distrust(b))
+                out_ref[pl.ds(pl.multiple_of(b * size, size), size), :] = distrust(b)
                 return 0
 
-            lax.fori_loop(0, acc.shape[0], one, 0)
+            lax.fori_loop(0, acc.shape[0], one, 0, unroll=2)
         else:
             shares(shield_ref, weight_ref, distrust, out_ref)
 
 
-def start_kernel(columns, good_ref, spam_ref, count_ref, list_ref, tally):
+def start_kernel(columns, good_ref, spam_ref, tiles_ref, count_ref, list_ref, near_ref, tally, sem):
+    load = pltpu.make_async_copy(tiles_ref, near_ref, sem)
+    load.start()
     list_ref[...] = jnp.transpose(spam_ref[...].astype(F32)).astype(jnp.int32)
     count_seeds(columns, good_ref, tally)
     spread_seeds(good_ref.shape[1], tally, count_ref)
+    load.wait()
 
 
 def body(columns, tiles, tile_src, tile_slot, slot_block, out_degree, good_seeds, spam_cores):
@@ -790,7 +803,7 @@
     peers = lax.axis_size(AXES)
     cap = slots // peers
     tail = -(-4 * cap // 16) * 16
-    steps = 8
+    steps = 1
     shape = jax.ShapeDtypeStruct
     vector = (blocks, seeds, size)
     degree = out_degree.reshape(blocks, 1, size)
@@ -800,20 +813,22 @@
     count = spam_cores.shape[1]
     groups = seeds // count
     lines = seeds // groups
-    good, spam_list = pl.pallas_call(
+    good, spam_list, tiles = pl.pallas_call(
         functools.partial(start_kernel, columns),
-        out_shape=(shape(vector, F32), shape(spam_cores.shape, jnp.int32)),
-        in_specs=[VM, VM],
-        out_specs=(VM, VM),
-        scratch_shapes=[pltpu.VMEM((seeds, blocks, size), F32)],
+        out_shape=(
+            shape(vector, F32), shape(spam_cores.shape, jnp.int32), shape(tiles.shape, BF16),
+        ),
+        in_specs=[VM, VM, ANY],
+        out_specs=(VM, VM, VM),
+        scratch_shapes=[pltpu.VMEM((seeds, blocks, size), F32), pltpu.SemaphoreType.DMA],
         compiler_params=PLAIN,
         cost_estimate=pl.CostEstimate(
             flops=2 * seeds * good_seeds.size * (blocks + size), transcendentals=0,
             bytes_accessed=24 << 20,
         ),
-    )(here(good_seeds), here(spam_cores.T))
-
-    tile_spec = pl.BlockSpec((tile_count // steps, size, size), lambda i: (i, 0, 0))
+    )(here(good_seeds), here(spam_cores.T), here(tiles))
+
+    tile_spec = VM
     words = shape((peers, cap * size + tail, size), jnp.int16)
     outgoing = pl.pallas_call(
         functools.partial(push_kernel, True, cap, part),
@@ -826,7 +841,7 @@
             pltpu.VMEM((blocks, seeds + 16, size), BF16),
         ],
         compiler_params=PLAIN,
-    )(here(tile_src), here(tile_slot), here(slot_block), good, here(degree), here(tiles))
+    )(here(tile_src), here(tile_slot), here(slot_block), good, here(degree), tiles)
 
     dma = pltpu.SemaphoreType.DMA
     spread_sems = [
@@ -907,16 +922,16 @@
         out_specs=(VM, VM, VM),
         compiler_params=PLAIN,
     )(inflow, good, spam, weight, keys)
-    vals = pl.pallas_call(
+    vals, turned = pl.pallas_call(
         functools.partial(value_kernel, rows, columns),
-        out_shape=shape((peers, lines, size), BF16),
-        in_specs=[VM],
-        out_specs=VM,
+        out_shape=(shape((peers, lines, size), BF16), shape(vector, F32)),
+        in_specs=[VM, VM],
+        out_specs=(VM, VM),
         scratch_shapes=spread_sems,
         compiler_params=pltpu.CompilerParams(
             collective_id=3, has_side_effects=True, vmem_limit_bytes=LIMIT
         ),
-    )(vals)
+    )(vals, spam)
     share = pl.pallas_call(
         functools.partial(pull_kernel, False),
         grid=(steps,),
@@ -941,7 +956,7 @@
         out_specs=VM,
         scratch_shapes=[pltpu.VMEM(vector, F32)],
         compiler_params=PLAIN,
-    )(tile_src, tile_slot, fetched, spam, tiles)
+    )(tile_src, tile_slot, fetched, turned, tiles)
     return trust, distrust
 
 

time: 249 us -> 234 us (0.940)
  Pallas kernels: 248 us -> 233 us
    pallas_call x1, Pallas kernels: 11.4 us -> 5.35 us  [body(): pl.pallas_call(functools.partial(pull_kernel, True), grid=(steps,), out_s...]
    pallas_call x1, Pallas kernels: 14.3 us -> 10.5 us  [body(): pl.pallas_call(functools.partial(push_kernel, True, cap, part), grid=(ste...]
    pallas_call x1, Pallas kernels: 26 us -> 22.2 us  [body(): pl.pallas_call(functools.partial(pull_kernel, False), grid=(steps,), out_...]
where the time goes in v7:
time: 234 us
  Pallas kernels  233 us (100%)
    pallas_call x2, Pallas kernels, reduce(): pl.pallas_call(functools.partial(reduce_kernel, first, rows, columns, cap...  115 us
    pallas_call x1, Pallas kernels, body(): fetched = fetch(want, share)  53.2 us
    pallas_call x1, Pallas kernels, body(): pl.pallas_call(functools.partial(pull_kernel, False), grid=(steps,), out_...  22.2 us
    pallas_call x1, Pallas kernels, body(): pl.pallas_call(functools.partial(value_kernel, rows, columns), out_shape=...  11.3 us
    pallas_call x1, Pallas kernels, body(): pl.pallas_call(functools.partial(push_kernel, True, cap, part), grid=(ste...  10.5 us
    pallas_call x1, Pallas kernels, body(): pl.pallas_call(functools.partial(push_kernel, False, cap, part), grid=(st...  7.76 us
    pallas_call x1, Pallas kernels, body(): pl.pallas_call(functools.partial(pull_kernel, True), grid=(steps,), out_s...  5.35 us
    pallas_call x1, Pallas kernels, body(): pl.pallas_call(functools.partial(start_kernel, columns), out_shape=(shape...  4.97 us

profile of v7, /device:TPU:1, one launch (start us, length us, event | category | flops | bytes accessed | tf_op | source)
XLA Modules:
  0.0 233.6 jit_solution(9224012092046062450)
XLA Ops:
  0.6 5.0 %shard_map.86 = (f32[16,128,128]{2,1,0:T(8,128)S(1)}, s32[128,64]{1,0:T(8,128)S(1)}, bf16[256,128,128]{2,1,0:T(8,128)(2,1)S(1)}) custom-call(s32[128,128]{1,0:T(8,128)} %good_ref.1, s32[64,128]{1,0:T(8,128)} %bitcast.3, bf16[256,128,128]{2,1,0:T(8,128)(2,1)} %tiles_ref.1), custom_call_target="tpu_custom_call" | custom-call | flops 603979776 | bytes 25165824 | tf_op jit(solution)/shard_map/pallas_call | solution.py:816
  5.6 0.0 copy-start
  5.6 0.0 copy-start.4
  5.6 10.5 %shard_map.87.words_ref = s16[32,528,128]{2,1,0:T(8,128)(2,1)S(1)} custom-call(s32[256]{0:T(256)} %refs_0_.7, s32[256]{0:T(256)} %refs_1_.7, s32[128]{0:T(128)} %refs_2_.5, f32[16,128,128]{2,1,0:T(8,128)S(1)} %get-tuple-element.18.refs_3_.refs_4_.good_ref, s32[16,1,128]{2,1,0:T(1,128)} %bitcast.5, ...), custom_call_target="tpu_custom_call" | custom-call | tf_op jit(solution)/shard_map/pallas_call | solution.py:833
  16.1 0.0 copy-done
  16.2 0.0 copy-done.4
  16.2 0.0 copy-start.1
  16.2 0.0 copy-start.2
  16.2 0.0 copy-start.3
  16.2 61.4 %shard_map.88 = (f32[16,128,128]{2,1,0:T(8,128)S(1)}, f32[16,128]{1,0:T(8,128)S(1)}, f32[16,128,128]{2,1,0:T(8,128)S(1)}, s32[8,1,128]{2,1,0:T(1,128)S(1)}, s16[...) custom-call(s16[32,528,128]{2,1,0:T(8,128)(2,1)S(1)} %shard_map.87.words_ref, ...), custom_call_target="tpu_custom_call" | custom-call | tf_op jit(solution)/shard_map/pallas_call | solution.py:861
  77.6 0.0 copy-done.1
  77.6 0.0 copy-done.2
  77.6 0.0 copy-done.3
  77.6 7.8 %shard_map.89.words_ref = s16[32,528,128]{2,1,0:T(8,128)(2,1)S(1)} custom-call(s32[256]{0:T(256)S(1)} %copy-done.2, s32[256]{0:T(256)S(1)} %copy-done.3, s32[128]{0:T(128)S(1)} %copy-done.4, f32[16,128,128]{2,1,0:T(8,128)S(1)} %get-tuple-element.21.refs_3_, f32[16,128,128]{2,1,0:T(8,128)S(1)} %get-tuple-element.18.refs_3_.refs_4_.good_ref, ...), custom_call_target="tpu_custom_call" | custom-call | tf_op jit(solution)/shard_map/pallas_call | solution.py:890
  85.4 53.9 %shard_map.90 = (f32[16,128,128]{2,1,0:T(8,128)S(1)}, s32[32,128,128]{2,1,0:T(8,128)S(1)}) custom-call(s16[32,528,128]{2,1,0:T(8,128)(2,1)S(1)} %shard_map.89.words_ref, s16[32,64,128]{2,1,0:T(8,128)(2,1)S(1)} %get-tuple-element.22.refs_0_.refs_3_), custom_call_target="tpu_custom_call" | custom-call | tf_op jit(solution)/shard_map/pallas_call | solution.py:861
  139.3 2.2 shard_map.91
  141.5 11.3 %shard_map.92 = (bf16[32,64,128]{2,1,0:T(8,128)(2,1)S(1)}, f32[16,128,128]{2,1,0:T(8,128)S(1)}) custom-call(bf16[64,128]{1,0:T(8,128)(2,1)S(1)} %get-tuple-element.29.own_ref, f32[16,128,128]{2,1,0:T(8,128)S(1)} %get-tuple-element.24.spam_ref.refs_6_), custom_call_target="tpu_custom_call" | custom-call | tf_op jit(solution)/shard_map/pallas_call | solution.py:925
  152.8 22.2 %shard_map.93.share_ref = bf16[16,128,128]{2,1,0:T(8,128)(2,1)S(1)} custom-call(s32[256]{0:T(256)S(1)} %copy-done.2, s32[256]{0:T(256)S(1)} %copy-done.3, s32[128]{0:T(128)S(1)} %copy-done.4, s16[32,64,128]{2,1,0:T(8,128)(2,1)S(1)} %get-tuple-element.22.refs_0_.refs_3_, bf16[32,64,128]{2,1,0:T(8,128)(2,1)S(1)} %get-tuple-element.30.refs_4_, ...), custom_call_target="tpu_custom_call" | custom-call | tf_op jit(solution)/shard_map/pallas_call | solution.py:935
  175.0 53.2 %shard_map.94.refs_2_ = bf16[128,128,128]{2,1,0:T(8,128)(2,1)S(1)} custom-call(s32[8,1,128]{2,1,0:T(1,128)S(1)} %get-tuple-element.28.want_ref, bf16[16,128,128]{2,1,0:T(8,128)(2,1)S(1)} %shard_map.93.share_ref), custom_call_target="tpu_custom_call" | custom-call | tf_op jit(solution)/shard_map/pallas_call | solution.py:950
  228.3 5.3 %shard_map.95 = f32[2048,128]{1,0:T(8,128)} custom-call(s32[256]{0:T(256)S(1)} %copy-done.2, s32[256]{0:T(256)S(1)} %copy-done.3, bf16[128,128,128]{2,1,0:T(8,128)(2,1)S(1)} %shard_map.94.refs_2_, f32[16,128,128]{2,1,0:T(8,128)S(1)} %get-tuple-element.33.refs_3_, bf16[256,128,128]{2,1,0:T(8,128)(2,1)S(1)} %get-tuple-element.19.refs_5_.refs_6_.refs_9_.refs_4_), custom_call_target="tpu_custom_call" | custom-call | tf_op jit(solution)/shard_map/pallas_call | solution.py:951
Async XLA Ops:
  5.6 10.5 %copy-start = (s32[128,64]{0,1:T(8,128)S(1)}, s32[128,64]{0,1:T(8,128)}, u32[]{:S(2)}) copy-start(s32[128,64]{0,1:T(8,128)} %param.13) | copy-start | bytes 98308
  5.6 10.5 %copy-start.4 = (s32[128]{0:T(128)S(1)}, s32[128]{0:T(128)}, u32[]{:S(2)}) copy-start(s32[128]{0:T(128)} %refs_2_.5) | copy-start | bytes 1540
  16.2 61.4 %copy-start.1 = (s32[2048]{0:T(1024)S(1)}, s32[2048]{0:T(1024)}, u32[]{:S(2)}) copy-start(s32[2048]{0:T(1024)} %param.11) | copy-start | bytes 24580
  16.2 61.4 %copy-start.2 = (s32[256]{0:T(256)S(1)}, s32[256]{0:T(256)}, u32[]{:S(2)}) copy-start(s32[256]{0:T(256)} %refs_0_.7) | copy-start | bytes 3076
  16.2 61.4 %copy-start.3 = (s32[256]{0:T(256)S(1)}, s32[256]{0:T(256)}, u32[]{:S(2)}) copy-start(s32[256]{0:T(256)} %refs_1_.7) | copy-start | bytes 3076

commit v8 on v7

--- a/solution.py
+++ b/solution.py
@@ -18,6 +18,7 @@
 WORD = 15
 GROUP = 64
 HALVES = 4
+PARTS = 2
 LAYERS = 6
 MORE = 2
 MESH = pl.DeviceIdType.MESH
@@ -156,80 +157,91 @@
 
 def fetch_kernel(rows, columns, cap, want_ref, share_ref, fetched_ref, *scratch):
     line = 2 * (columns - 1)
-    held, (picked, line_send, line_recv, send, recv) = scratch[:line], scratch[line:]
+    held, (picked, line_send, line_recv, send, recv) = scratch[: line * PARTS], scratch[line * PARTS :]
     r, z = lax.axis_index("row"), lax.axis_index("col")
     others = [lax.rem(r + d, rows) for d in range(1, rows)]
     sides = (-1, 1)
     inside = {side: (z + side >= 0) & (z + side < columns) for side in sides}
+    tall = share_ref.shape[1] // PARTS
     greet([((t, z), t >= 0) for t in others] + [((r, z + side), inside[side]) for side in sides])
 
-    def place(side, d):
-        return 2 * (d - 1) + (0 if side < 0 else 1)
-
-    def pass_on(source, d, side):
-        slot = place(-side, d)
+    def place(side, d, k):
+        return (2 * (d - 1) + (0 if side < 0 else 1)) * PARTS + k
+
+    def pass_on(source, d, side, k):
+        slot = place(-side, d, k)
         return pltpu.make_async_remote_copy(
             src_ref=source, dst_ref=held[slot],
             send_sem=line_send.at[slot], recv_sem=line_recv.at[slot],
             device_id=(r, z + side), device_id_type=MESH,
         )
 
-    def serve(t, origin):
+    def own(k):
+        return share_ref.at[:, pl.ds(k * tall, tall)]
+
+    def serve(t, origin, k, source, sender):
+        span = pl.ds(k * tall, tall)
         return pltpu.make_async_remote_copy(
-            src_ref=picked.at[t, pl.ds(origin * cap, cap)],
-            dst_ref=fetched_ref.at[pl.ds((r * columns + origin) * cap, cap)],
-            send_sem=send.at[t, origin], recv_sem=recv.at[r, origin],
+            src_ref=picked.at[t, pl.ds(origin * cap, cap), span],
+            dst_ref=fetched_ref.at[pl.ds((source * columns + origin) * cap, cap), span],
+            send_sem=send.at[t, origin * PARTS + k], recv_sem=recv.at[sender, origin * PARTS + k],
             device_id=(t, z), device_id_type=MESH,
         )
 
-    def spread(source, origin):
+    def spread(source, origin, k):
+        span = slice(k * tall, (k + 1) * tall)
+
+        def pick(t, j):
+            n = want_ref[t, 0, (r * columns + origin) * cap + j]
+            return source[n, span, :] if source.shape[1] > tall else source[n]
+
         before = None
         for t in others:
             for j in range(cap):
-                picked[t, origin * cap + j] = source[want_ref[t, 0, (r * columns + origin) * cap + j]]
+                picked[t, origin * cap + j, span, :] = pick(t, j)
             if before is not None:
-                serve(before, origin).start()
+                serve(before, origin, k, r, r).start()
             before = t
         for j in range(cap):
-            fetched_ref[(r * columns + origin) * cap + j] = source[want_ref[r, 0, (r * columns + origin) * cap + j]]
-        serve(before, origin).start()
-
-    for side in sides:
-        @pl.when(inside[side])
-        def _():
-            pass_on(share_ref, 1, side).start()
-    spread(share_ref, z)
+            fetched_ref[(r * columns + origin) * cap + j, span, :] = pick(r, j)
+        serve(before, origin, k, r, r).start()
+
+    for k in range(PARTS):
+        for side in sides:
+            @pl.when(inside[side])
+            def _():
+                pass_on(own(k), 1, side, k).start()
+    for k in range(PARTS):
+        spread(share_ref, z, k)
     for d in range(1, columns):
-        for side in sides:
-            origin = z + side * d
-
-            @pl.when((origin >= 0) & (origin < columns))
-            def _():
-                here = held[place(side, d)]
-                pass_on(share_ref, d, -side).wait_recv()
-
-                if d < columns - 1:
-                    @pl.when(inside[-side])
-                    def _():
-                        pass_on(here, d + 1, -side).start()
-
-                spread(here, origin)
+        for k in range(PARTS):
+            for side in sides:
+                origin = z + side * d
+
+                @pl.when((origin >= 0) & (origin < columns))
+                def _():
+                    here = held[place(side, d, k)]
+                    pass_on(here, d, -side, k).wait_recv()
+
+                    if d < columns - 1:
+                        @pl.when(inside[-side])
+                        def _():
+                            pass_on(here, d + 1, -side, k).start()
+
+                    spread(here, origin, k)
     for origin in range(columns):
-        for t in others:
-            serve(t, origin).wait_send()
-            pltpu.make_async_remote_copy(
-                src_ref=picked.at[t, pl.ds(origin * cap, cap)],
-                dst_ref=fetched_ref.at[pl.ds((t * columns + origin) * cap, cap)],
-                send_sem=send.at[t, origin], recv_sem=recv.at[t, origin],
-                device_id=(t, z), device_id_type=MESH,
-            ).wait_recv()
+        for k in range(PARTS):
+            for t in others:
+                serve(t, origin, k, r, r).wait_send()
+                serve(t, origin, k, t, t).wait_recv()
     for d in range(columns - 1):
-        for side in sides:
-            origin = z - side * d
-
-            @pl.when((origin >= 0) & (origin < columns) & inside[side])
-            def _():
-                pass_on(share_ref, d + 1, side).wait_send()
+        for k in range(PARTS):
+            for side in sides:
+                origin = z - side * d
+
+                @pl.when((origin >= 0) & (origin < columns) & inside[side])
+                def _():
+                    pass_on(held[0], d + 1, side, k).wait_send()
 
 
 def take(table, index):
@@ -906,12 +918,12 @@
         in_specs=[SM, VM],
         out_specs=VM,
         scratch_shapes=[
-            *[pltpu.VMEM(vector, BF16)] * (2 * columns - 2),
-            pltpu.VMEM((rows, columns * cap, seeds, size), BF16),
-            pltpu.SemaphoreType.DMA((2 * columns - 2,)),
-            pltpu.SemaphoreType.DMA((2 * columns - 2,)),
-            pltpu.SemaphoreType.DMA((rows, columns)),
-            pltpu.SemaphoreType.DMA((rows, columns)),
+            *[pltpu.VMEM((blocks, size // PARTS, seeds), BF16)] * ((2 * columns - 2) * PARTS),
+            pltpu.VMEM((rows, columns * cap, size, seeds), BF16),
+            pltpu.SemaphoreType.DMA(((2 * columns - 2) * PARTS,)),
+            pltpu.SemaphoreType.DMA(((2 * columns - 2) * PARTS,)),
+            pltpu.SemaphoreType.DMA((rows, columns * PARTS)),
+            pltpu.SemaphoreType.DMA((rows, columns * PARTS)),
         ],
         compiler_params=pltpu.CompilerParams(collective_id=0, has_side_effects=True, vmem_limit_bytes=LIMIT),
     )

time: 234 us -> 231 us (0.987)
  Pallas kernels: 233 us -> 230 us
    pallas_call x1, Pallas kernels: 53.2 us -> 50.2 us  [body(): fetched = fetch(want, share)]
where the time goes in v8:
time: 231 us
  Pallas kernels  230 us (100%)
    pallas_call x2, Pallas kernels, reduce(): pl.pallas_call(functools.partial(reduce_kernel, first, rows, columns, cap...  115 us
    pallas_call x1, Pallas kernels, body(): fetched = fetch(want, share)  50.2 us
    pallas_call x1, Pallas kernels, body(): pl.pallas_call(functools.partial(pull_kernel, False), grid=(steps,), out_...  22.6 us
    pallas_call x1, Pallas kernels, body(): pl.pallas_call(functools.partial(value_kernel, rows, columns), out_shape=...  11.3 us
    pallas_call x1, Pallas kernels, body(): pl.pallas_call(functools.partial(push_kernel, True, cap, part), grid=(ste...  10.5 us
    pallas_call x1, Pallas kernels, body(): pl.pallas_call(functools.partial(push_kernel, False, cap, part), grid=(st...  7.76 us
    pallas_call x1, Pallas kernels, body(): pl.pallas_call(functools.partial(pull_kernel, True), grid=(steps,), out_s...  5.34 us
    pallas_call x1, Pallas kernels, body(): pl.pallas_call(functools.partial(start_kernel, columns), out_shape=(shape...  4.97 us

profile of v8, /device:TPU:1, one launch (start us, length us, event | category | flops | bytes accessed | tf_op | source)
XLA Modules:
  0.0 231.0 jit_solution(12740748900170075957)
XLA Ops:
  0.6 5.0 %shard_map.86 = (f32[16,128,128]{2,1,0:T(8,128)S(1)}, s32[128,64]{1,0:T(8,128)S(1)}, bf16[256,128,128]{2,1,0:T(8,128)(2,1)S(1)}) custom-call(s32[128,128]{1,0:T(8,128)} %good_ref.1, s32[64,128]{1,0:T(8,128)} %bitcast.3, bf16[256,128,128]{2,1,0:T(8,128)(2,1)} %tiles_ref.1), custom_call_target="tpu_custom_call" | custom-call | flops 603979776 | bytes 25165824 | tf_op jit(solution)/shard_map/pallas_call | solution.py:828
  5.6 0.0 copy-start
  5.6 0.0 copy-start.4
  5.6 10.5 %shard_map.87.words_ref = s16[32,528,128]{2,1,0:T(8,128)(2,1)S(1)} custom-call(s32[256]{0:T(256)} %refs_0_.7, s32[256]{0:T(256)} %refs_1_.7, s32[128]{0:T(128)} %refs_2_.5, f32[16,128,128]{2,1,0:T(8,128)S(1)} %get-tuple-element.18.refs_3_.refs_4_.good_ref, s32[16,1,128]{2,1,0:T(1,128)} %bitcast.5, ...), custom_call_target="tpu_custom_call" | custom-call | tf_op jit(solution)/shard_map/pallas_call | solution.py:845
  16.2 0.0 copy-done
  16.2 0.0 copy-done.4
  16.2 0.0 copy-start.1
  16.2 0.0 copy-start.2
  16.2 0.0 copy-start.3
  16.2 61.3 %shard_map.88 = (f32[16,128,128]{2,1,0:T(8,128)S(1)}, f32[16,128]{1,0:T(8,128)S(1)}, f32[16,128,128]{2,1,0:T(8,128)S(1)}, s32[8,1,128]{2,1,0:T(1,128)S(1)}, s16[...) custom-call(s16[32,528,128]{2,1,0:T(8,128)(2,1)S(1)} %shard_map.87.words_ref, ...), custom_call_target="tpu_custom_call" | custom-call | tf_op jit(solution)/shard_map/pallas_call | solution.py:873
  77.6 0.0 copy-done.1
  77.6 0.0 copy-done.2
  77.6 0.0 copy-done.3
  77.6 7.8 %shard_map.89.words_ref = s16[32,528,128]{2,1,0:T(8,128)(2,1)S(1)} custom-call(s32[256]{0:T(256)S(1)} %copy-done.2, s32[256]{0:T(256)S(1)} %copy-done.3, s32[128]{0:T(128)S(1)} %copy-done.4, f32[16,128,128]{2,1,0:T(8,128)S(1)} %get-tuple-element.21.refs_3_, f32[16,128,128]{2,1,0:T(8,128)S(1)} %get-tuple-element.18.refs_3_.refs_4_.good_ref, ...), custom_call_target="tpu_custom_call" | custom-call | tf_op jit(solution)/shard_map/pallas_call | solution.py:902
  85.4 53.9 %shard_map.90 = (f32[16,128,128]{2,1,0:T(8,128)S(1)}, s32[32,128,128]{2,1,0:T(8,128)S(1)}) custom-call(s16[32,528,128]{2,1,0:T(8,128)(2,1)S(1)} %shard_map.89.words_ref, s16[32,64,128]{2,1,0:T(8,128)(2,1)S(1)} %get-tuple-element.22.refs_0_.refs_3_), custom_call_target="tpu_custom_call" | custom-call | tf_op jit(solution)/shard_map/pallas_call | solution.py:873
  139.3 2.2 shard_map.91
  141.5 11.3 %shard_map.92 = (bf16[32,64,128]{2,1,0:T(8,128)(2,1)S(1)}, f32[16,128,128]{2,1,0:T(8,128)S(1)}) custom-call(bf16[64,128]{1,0:T(8,128)(2,1)S(1)} %get-tuple-element.29.own_ref, f32[16,128,128]{2,1,0:T(8,128)S(1)} %get-tuple-element.24.spam_ref.refs_6_), custom_call_target="tpu_custom_call" | custom-call | tf_op jit(solution)/shard_map/pallas_call | solution.py:937
  152.8 22.6 %shard_map.93.share_ref = bf16[16,128,128]{2,1,0:T(8,128)(2,1)S(1)} custom-call(s32[256]{0:T(256)S(1)} %copy-done.2, s32[256]{0:T(256)S(1)} %copy-done.3, s32[128]{0:T(128)S(1)} %copy-done.4, s16[32,64,128]{2,1,0:T(8,128)(2,1)S(1)} %get-tuple-element.22.refs_0_.refs_3_, bf16[32,64,128]{2,1,0:T(8,128)(2,1)S(1)} %get-tuple-element.30.refs_4_, ...), custom_call_target="tpu_custom_call" | custom-call | tf_op jit(solution)/shard_map/pallas_call | solution.py:947
  175.4 50.2 %shard_map.94.refs_2_ = bf16[128,128,128]{2,1,0:T(8,128)(2,1)S(1)} custom-call(s32[8,1,128]{2,1,0:T(1,128)S(1)} %get-tuple-element.28.want_ref, bf16[16,128,128]{2,1,0:T(8,128)(2,1)S(1)} %shard_map.93.share_ref), custom_call_target="tpu_custom_call" | custom-call | tf_op jit(solution)/shard_map/pallas_call | solution.py:962
  225.6 5.3 %shard_map.95 = f32[2048,128]{1,0:T(8,128)} custom-call(s32[256]{0:T(256)S(1)} %copy-done.2, s32[256]{0:T(256)S(1)} %copy-done.3, bf16[128,128,128]{2,1,0:T(8,128)(2,1)S(1)} %shard_map.94.refs_2_, f32[16,128,128]{2,1,0:T(8,128)S(1)} %get-tuple-element.33.refs_3_, bf16[256,128,128]{2,1,0:T(8,128)(2,1)S(1)} %get-tuple-element.19.refs_5_.refs_6_.refs_9_.refs_4_), custom_call_target="tpu_custom_call" | custom-call | tf_op jit(solution)/shard_map/pallas_call | solution.py:963
Async XLA Ops:
  5.6 10.6 %copy-start = (s32[128,64]{0,1:T(8,128)S(1)}, s32[128,64]{0,1:T(8,128)}, u32[]{:S(2)}) copy-start(s32[128,64]{0,1:T(8,128)} %param.13) | copy-start | bytes 98308
  5.6 10.5 %copy-start.4 = (s32[128]{0:T(128)S(1)}, s32[128]{0:T(128)}, u32[]{:S(2)}) copy-start(s32[128]{0:T(128)} %refs_2_.5) | copy-start | bytes 1540
  16.2 61.4 %copy-start.1 = (s32[2048]{0:T(1024)S(1)}, s32[2048]{0:T(1024)}, u32[]{:S(2)}) copy-start(s32[2048]{0:T(1024)} %param.11) | copy-start | bytes 24580
  16.2 61.4 %copy-start.2 = (s32[256]{0:T(256)S(1)}, s32[256]{0:T(256)}, u32[]{:S(2)}) copy-start(s32[256]{0:T(256)} %refs_0_.7) | copy-start | bytes 3076
  16.2 61.4 %copy-start.3 = (s32[256]{0:T(256)S(1)}, s32[256]{0:T(256)}, u32[]{:S(2)}) copy-start(s32[256]{0:T(256)} %refs_1_.7) | copy-start | bytes 3076

commit v9 on v8

--- a/solution.py
+++ b/solution.py
@@ -92,7 +92,7 @@
         out_ref[p, at : at + tail, :] = jnp.concatenate(rows, axis=0).astype(jnp.int32).astype(jnp.int16)
         return 0
 
-    lax.fori_loop(0, peers, one, 0, unroll=2)
+    lax.fori_loop(0, peers, one, 0, unroll=4)
 
 
 def push_kernel(first, cap, part, *refs):
@@ -400,7 +400,7 @@
 def expand(cap, block_ref, lists_ref, vals_ref, rank_ref, blocks, bounds, fetched):
     peers, lines, size = lists_ref.shape
     groups = fetched.shape[1] // lines
-    tall = 16
+    tall = 32
 
     def paint(q, low, high, fresh):
         tags = [
@@ -441,7 +441,7 @@
                     fetched[q * cap + c, pl.ds(row, tall), :] = outs[c].astype(BF16)
             return 0
 
-        lax.fori_loop(0, lines // tall, some, 0, unroll=4 if fresh else 1)
+        lax.fori_loop(0, lines // tall, some, 0, unroll=2 if fresh else 1)
 
     def one(q, _):
         paint(q, 0, LAYERS, True)

time: 231 us -> 230 us (level)
  no operation moved by 1% of the time
where the time goes in v9:
time: 230 us
  Pallas kernels  229 us (100%)
    pallas_call x2, Pallas kernels, reduce(): pl.pallas_call(functools.partial(reduce_kernel, first, rows, columns, cap...  115 us
    pallas_call x1, Pallas kernels, body(): fetched = fetch(want, share)  50.3 us
    pallas_call x1, Pallas kernels, body(): pl.pallas_call(functools.partial(pull_kernel, False), grid=(steps,), out_...  21.9 us
    pallas_call x1, Pallas kernels, body(): pl.pallas_call(functools.partial(value_kernel, rows, columns), out_shape=...  11.3 us
    pallas_call x1, Pallas kernels, body(): pl.pallas_call(functools.partial(push_kernel, True, cap, part), grid=(ste...  10.3 us
    pallas_call x1, Pallas kernels, body(): pl.pallas_call(functools.partial(push_kernel, False, cap, part), grid=(st...  7.49 us
    pallas_call x1, Pallas kernels, body(): pl.pallas_call(functools.partial(pull_kernel, True), grid=(steps,), out_s...  5.34 us
    pallas_call x1, Pallas kernels, body(): pl.pallas_call(functools.partial(start_kernel, columns), out_shape=(shape...  4.97 us

profile of v9, /device:TPU:1, one launch (start us, length us, event | category | flops | bytes accessed | tf_op | source)
XLA Modules:
  0.0 229.9 jit_solution(16947285243409354536)
XLA Ops:
  0.6 5.0 %shard_map.86 = (f32[16,128,128]{2,1,0:T(8,128)S(1)}, s32[128,64]{1,0:T(8,128)S(1)}, bf16[256,128,128]{2,1,0:T(8,128)(2,1)S(1)}) custom-call(s32[128,128]{1,0:T(8,128)} %good_ref.1, s32[64,128]{1,0:T(8,128)} %bitcast.3, bf16[256,128,128]{2,1,0:T(8,128)(2,1)} %tiles_ref.1), custom_call_target="tpu_custom_call" | custom-call | flops 603979776 | bytes 25165824 | tf_op jit(solution)/shard_map/pallas_call | solution.py:828
  5.6 0.0 copy-start
  5.6 0.0 copy-start.4
  5.6 10.3 %shard_map.87.words_ref = s16[32,528,128]{2,1,0:T(8,128)(2,1)S(1)} custom-call(s32[256]{0:T(256)} %refs_0_.7, s32[256]{0:T(256)} %refs_1_.7, s32[128]{0:T(128)} %refs_2_.5, f32[16,128,128]{2,1,0:T(8,128)S(1)} %get-tuple-element.18.refs_3_.refs_4_.good_ref, s32[16,1,128]{2,1,0:T(1,128)} %bitcast.5, ...), custom_call_target="tpu_custom_call" | custom-call | tf_op jit(solution)/shard_map/pallas_call | solution.py:845
  15.9 0.0 copy-done
  15.9 0.0 copy-done.4
  15.9 0.0 copy-start.1
  16.0 0.0 copy-start.2
  16.0 0.0 copy-start.3
  16.0 61.4 %shard_map.88 = (f32[16,128,128]{2,1,0:T(8,128)S(1)}, f32[16,128]{1,0:T(8,128)S(1)}, f32[16,128,128]{2,1,0:T(8,128)S(1)}, s32[8,1,128]{2,1,0:T(1,128)S(1)}, s16[...) custom-call(s16[32,528,128]{2,1,0:T(8,128)(2,1)S(1)} %shard_map.87.words_ref, ...), custom_call_target="tpu_custom_call" | custom-call | tf_op jit(solution)/shard_map/pallas_call | solution.py:873
  77.3 0.0 copy-done.1
  77.4 0.0 copy-done.2
  77.4 0.0 copy-done.3
  77.4 7.5 %shard_map.89.words_ref = s16[32,528,128]{2,1,0:T(8,128)(2,1)S(1)} custom-call(s32[256]{0:T(256)S(1)} %copy-done.2, s32[256]{0:T(256)S(1)} %copy-done.3, s32[128]{0:T(128)S(1)} %copy-done.4, f32[16,128,128]{2,1,0:T(8,128)S(1)} %get-tuple-element.21.refs_3_, f32[16,128,128]{2,1,0:T(8,128)S(1)} %get-tuple-element.18.refs_3_.refs_4_.good_ref, ...), custom_call_target="tpu_custom_call" | custom-call | tf_op jit(solution)/shard_map/pallas_call | solution.py:902
  84.9 53.9 %shard_map.90 = (f32[16,128,128]{2,1,0:T(8,128)S(1)}, s32[32,128,128]{2,1,0:T(8,128)S(1)}) custom-call(s16[32,528,128]{2,1,0:T(8,128)(2,1)S(1)} %shard_map.89.words_ref, s16[32,64,128]{2,1,0:T(8,128)(2,1)S(1)} %get-tuple-element.22.refs_0_.refs_3_), custom_call_target="tpu_custom_call" | custom-call | tf_op jit(solution)/shard_map/pallas_call | solution.py:873
  138.8 2.2 shard_map.91
  141.0 11.3 %shard_map.92 = (bf16[32,64,128]{2,1,0:T(8,128)(2,1)S(1)}, f32[16,128,128]{2,1,0:T(8,128)S(1)}) custom-call(bf16[64,128]{1,0:T(8,128)(2,1)S(1)} %get-tuple-element.29.own_ref, f32[16,128,128]{2,1,0:T(8,128)S(1)} %get-tuple-element.24.spam_ref.refs_6_), custom_call_target="tpu_custom_call" | custom-call | tf_op jit(solution)/shard_map/pallas_call | solution.py:937
  152.3 21.9 %shard_map.93.share_ref = bf16[16,128,128]{2,1,0:T(8,128)(2,1)S(1)} custom-call(s32[256]{0:T(256)S(1)} %copy-done.2, s32[256]{0:T(256)S(1)} %copy-done.3, s32[128]{0:T(128)S(1)} %copy-done.4, s16[32,64,128]{2,1,0:T(8,128)(2,1)S(1)} %get-tuple-element.22.refs_0_.refs_3_, bf16[32,64,128]{2,1,0:T(8,128)(2,1)S(1)} %get-tuple-element.30.refs_4_, ...), custom_call_target="tpu_custom_call" | custom-call | tf_op jit(solution)/shard_map/pallas_call | solution.py:947
  174.3 50.3 %shard_map.94.refs_2_ = bf16[128,128,128]{2,1,0:T(8,128)(2,1)S(1)} custom-call(s32[8,1,128]{2,1,0:T(1,128)S(1)} %get-tuple-element.28.want_ref, bf16[16,128,128]{2,1,0:T(8,128)(2,1)S(1)} %shard_map.93.share_ref), custom_call_target="tpu_custom_call" | custom-call | tf_op jit(solution)/shard_map/pallas_call | solution.py:962
  224.5 5.3 %shard_map.95 = f32[2048,128]{1,0:T(8,128)} custom-call(s32[256]{0:T(256)S(1)} %copy-done.2, s32[256]{0:T(256)S(1)} %copy-done.3, bf16[128,128,128]{2,1,0:T(8,128)(2,1)S(1)} %shard_map.94.refs_2_, f32[16,128,128]{2,1,0:T(8,128)S(1)} %get-tuple-element.33.refs_3_, bf16[256,128,128]{2,1,0:T(8,128)(2,1)S(1)} %get-tuple-element.19.refs_5_.refs_6_.refs_9_.refs_4_), custom_call_target="tpu_custom_call" | custom-call | tf_op jit(solution)/shard_map/pallas_call | solution.py:963
Async XLA Ops:
  5.6 10.3 %copy-start = (s32[128,64]{0,1:T(8,128)S(1)}, s32[128,64]{0,1:T(8,128)}, u32[]{:S(2)}) copy-start(s32[128,64]{0,1:T(8,128)} %param.13) | copy-start | bytes 98308
  5.6 10.3 %copy-start.4 = (s32[128]{0:T(128)S(1)}, s32[128]{0:T(128)}, u32[]{:S(2)}) copy-start(s32[128]{0:T(128)} %refs_2_.5) | copy-start | bytes 1540
  15.9 61.4 %copy-start.1 = (s32[2048]{0:T(1024)S(1)}, s32[2048]{0:T(1024)}, u32[]{:S(2)}) copy-start(s32[2048]{0:T(1024)} %param.11) | copy-start | bytes 24580
  16.0 61.4 %copy-start.2 = (s32[256]{0:T(256)S(1)}, s32[256]{0:T(256)}, u32[]{:S(2)}) copy-start(s32[256]{0:T(256)} %refs_0_.7) | copy-start | bytes 3076
  16.0 61.4 %copy-start.3 = (s32[256]{0:T(256)S(1)}, s32[256]{0:T(256)}, u32[]{:S(2)}) copy-start(s32[256]{0:T(256)} %refs_1_.7) | copy-start | bytes 3076
